TPU v7x, 32 devices: a whole 2x2x4 slice. The times are simulated.
32 devices in a mesh: dp: 16 (over z, y, core), tensor: 2 (over x).
Axes of the slice: x: 2, y: 2, z: 4, core: 2. Of those that a mesh axis runs over, the one named last changes fastest.
Arguments:
- residual: float32 [4096, 1024], P(('dp', 'tensor')), may hold values from -6 to 6
- segment_ids: int32 [4096], P('dp'), may hold values from 0 to 3, as said below
- live_counts: int32 [16], P('dp'), may hold values from 128 to 256, as said below
- norm_gain: float32 [1024], replicated, may hold values from 0.5 to 1.5
- z_weight: bfloat16 [1024, 2048], P('dp', 'tensor'), may hold values from -0.1875 to 0.1875
- x_weight: bfloat16 [1024, 2048], P('dp', 'tensor'), may hold values from -0.1875 to 0.1875
- bc_weight: bfloat16 [1024, 256], P('dp'), may hold values from -0.1875 to 0.1875
- dt_weight: bfloat16 [1024, 32], P('dp', 'tensor'), may hold values from -0.1875 to 0.1875
- conv_x: float32 [4, 2048], P(None, 'tensor'), may hold values from -3 to 3
- conv_x_bias: float32 [2048], P('tensor'), may hold values from -3 to 3
- conv_bc: float32 [4, 256], replicated, may hold values from -3 to 3
- conv_bc_bias: float32 [256], replicated, may hold values from -3 to 3
- dt_bias: float32 [32], P('tensor'), may hold values from -6.9 to -2.3
- a_log: float32 [32], P('tensor'), may hold values from 0 to 2.77
- d_skip: float32 [32], P('tensor'), may hold values from 0.5 to 1.5
- gate_gain: float32 [2048], P('tensor'), may hold values from 0.5 to 1.5
- out_weight: bfloat16 [2048, 1024], P('tensor', 'dp'), may hold values from -0.125 to 0.125
- cotangent: float32 [4096, 1024], P(('dp', 'tensor')), may hold values from -6 to 6
Outputs:
- block_out: float32 [4096, 1024], P(('dp', 'tensor'))
- input_grad: float32 [4096, 1024], P(('dp', 'tensor'))
- norm_gain_grad: float32 [1024], replicated
- z_weight_grad: float32 [1024, 2048], P('dp', 'tensor')
- x_weight_grad: float32 [1024, 2048], P('dp', 'tensor')
- bc_weight_grad: float32 [1024, 256], P(('dp', 'tensor'))
- dt_weight_grad: float32 [1024, 32], P('dp', 'tensor')
- conv_x_grad: float32 [4, 2048], P(None, 'tensor')
- conv_x_bias_grad: float32 [2048], P('tensor')
- conv_bc_grad: float32 [4, 256], replicated
- conv_bc_bias_grad: float32 [256], replicated
- dt_bias_grad: float32 [32], P('tensor')
- a_log_grad: float32 [32], P('tensor')
- d_skip_grad: float32 [32], P('tensor')
- gate_gain_grad: float32 [2048], P('tensor')
- out_weight_grad: float32 [2048, 1024], P('tensor', 'dp')
Inputs may be any that keep to these rules, and one draw needn't show every extreme that they name: `segment_ids`: Non-decreasing along each stream of 256 slots, starting at 0, rising by one at exactly three slots of every stream. `live_counts`: one stream is full and one holds exactly half.
All inputs are finite; a program needn't handle non-finite values.
Results may differ from a plain program's by a relative error of at most 0.0082.
Values may be sent and summed in bfloat16 or wider, within the bound.
No kernel may reach another device: no remote copies, remote signals or barrier semaphores. Data moves between devices by JAX's collectives and lax.ppermute only.
A program may use at most 128 MiB of HBM per device.

v0:
```python
from functools import partial

import jax
import jax.numpy as jnp
from jax import lax
from jax.sharding import PartitionSpec as P

D = 1024
SPAN = 128
INNER = 2048


epsilon = 1e-05


def causal_conv(values, kernel, bias_vec, segment):
    width = kernel.shape[0]
    row_total = values.shape[0]
    result = bias_vec + kernel[width - 1] * values
    for lag_steps in range(1, width):
        moved = jnp.concatenate(
            [
                jnp.zeros((lag_steps, values.shape[1]), values.dtype),
                values[: row_total - lag_steps],
            ],
            0,
        )
        seg_moved = jnp.concatenate(
            [jnp.full((lag_steps,), -1, jnp.int32), segment[: row_total - lag_steps]]
        )
        linked = (segment == seg_moved).astype(values.dtype)
        result = result + kernel[width - 1 - lag_steps] * moved * linked[:, None]
    return result


def ssd_core(
    segment,
    block_len,
    z_pre,
    x_pre,
    bc_pre,
    dt_pre,
    conv_x,
    conv_x_bias,
    conv_bc,
    conv_bc_bias,
    dt_bias,
    a_log,
    d_skip,
):
    row_total, head_count = dt_pre.shape
    head_width = x_pre.shape[1] // head_count
    state_size = bc_pre.shape[1] // 2
    highest = lax.Precision.HIGHEST
    x_conv = jax.nn.silu(causal_conv(x_pre, conv_x, conv_x_bias, segment))
    bc_conv = jax.nn.silu(causal_conv(bc_pre, conv_bc, conv_bc_bias, segment))
    b_input = bc_conv[:, :state_size]
    c_output = bc_conv[:, state_size:]
    step_sizes = jax.nn.softplus(dt_pre + dt_bias)
    log_decay = -step_sizes * jnp.exp(a_log)
    x_heads = x_conv.reshape(row_total, head_count, head_width)
    carry_state = jnp.zeros((head_count, head_width, state_size), x_conv.dtype)
    prev_segment = segment[0]
    positions = jnp.arange(block_len)
    lower_tri = positions[:, None] >= positions[None, :]
    pieces = []
    for first_row in range(0, row_total, block_len):
        block_seg = segment[first_row : first_row + block_len]
        block_step = step_sizes[first_row : first_row + block_len]
        block_x = x_heads[first_row : first_row + block_len]
        block_b = b_input[first_row : first_row + block_len]
        block_c = c_output[first_row : first_row + block_len]
        cumulative = jnp.cumsum(log_decay[first_row : first_row + block_len], axis=0)
        within = (block_seg[:, None] == block_seg[None, :]) & lower_tri
        gaps_log = cumulative.T[:, :, None] - cumulative.T[:, None, :]
        within_f = within.astype(x_conv.dtype)[None]
        decay_mat = jnp.exp(jnp.where(within[None], gaps_log, 0.0)) * within_f
        scores = jnp.dot(block_c, block_b.T, precision=highest)
        weighted = decay_mat * scores[None] * block_step.T[:, None, :]
        y_within = jnp.einsum("hts,shp->thp", weighted, block_x, precision=highest)
        keep_prev = (block_seg == prev_segment).astype(x_conv.dtype)
        carried_scale = jnp.exp(cumulative) * keep_prev[:, None]
        y_carried = (
            jnp.einsum("tn,hpn->thp", block_c, carry_state, precision=highest)
            * carried_scale[:, :, None]
        )
        pieces.append(y_within + y_carried)
        last_log = cumulative[-1]
        tail_mask = (block_seg == block_seg[-1]).astype(x_conv.dtype)
        state_coef = jnp.exp(last_log[None, :] - cumulative) * tail_mask[:, None] * block_step
        carry_state = carry_state * (jnp.exp(last_log) * keep_prev[-1])[:, None, None] + jnp.einsum(
            "sh,shp,sn->hpn", state_coef, block_x, block_b, precision=highest
        )
        prev_segment = block_seg[-1]
    y_all = jnp.concatenate(pieces, 0) + d_skip[None, :, None] * x_heads
    return y_all.reshape(row_total, head_count * head_width) * jax.nn.silu(z_pre)


def left_dot(left, right):
    return lax.dot_general(
        left, right, (((0,), (0,)), ((), ())), preferred_element_type=jnp.float32
    )


def right_dot(left, right):
    return lax.dot_general(
        left, right, (((1,), (1,)), ((), ())), preferred_element_type=jnp.float32
    )


def local(
    residual,
    segment_ids,
    live_counts,
    norm_gain,
    z_weight,
    x_weight,
    bc_weight,
    dt_weight,
    conv_x,
    conv_x_bias,
    conv_bc,
    conv_bc_bias,
    dt_bias,
    a_log,
    d_skip,
    gate_gain,
    out_weight,
    cotangent,
):
    inv_rms = lax.rsqrt(jnp.mean(residual * residual, axis=1) + epsilon)
    normed_half = (residual * inv_rms[:, None] * norm_gain).astype(jnp.bfloat16)
    z_full, x_full, dt_full, bc_full, out_full = (
        lax.all_gather(z_weight, "dp", axis=0, tiled=True),
        lax.all_gather(x_weight, "dp", axis=0, tiled=True),
        lax.all_gather(dt_weight, "dp", axis=0, tiled=True),
        lax.all_gather(bc_weight, "dp", axis=0, tiled=True),
        lax.all_gather(out_weight, "dp", axis=1, tiled=True),
    )
    normed = lax.all_gather(normed_half, "tensor", axis=0, tiled=True)
    z_pre = jnp.dot(normed, z_full, preferred_element_type=jnp.float32)
    x_pre = jnp.dot(normed, x_full, preferred_element_type=jnp.float32)
    bc_pre = jnp.dot(normed, bc_full, preferred_element_type=jnp.float32)
    dt_pre = jnp.dot(normed, dt_full, preferred_element_type=jnp.float32)
    core = partial(ssd_core, segment_ids, SPAN)
    gated, core_back = jax.vjp(
        core,
        z_pre,
        x_pre,
        bc_pre,
        dt_pre,
        conv_x,
        conv_x_bias,
        conv_bc,
        conv_bc_bias,
        dt_bias,
        a_log,
        d_skip,
    )
    squares = lax.psum(jnp.sum(gated * gated, axis=1), "tensor")
    gate_inv = lax.rsqrt(squares / INNER + epsilon)
    live_mask = (jnp.arange(gated.shape[0]) < live_counts[0]).astype(jnp.float32)
    mixed = (gated * gate_inv[:, None] * gate_gain * live_mask[:, None]).astype(jnp.bfloat16)
    block_out = residual + lax.psum_scatter(
        jnp.dot(mixed, out_full, preferred_element_type=jnp.float32),
        "tensor",
        scatter_dimension=0,
        tiled=True,
    )
    z_full, x_full, dt_full, bc_full, out_full = (
        lax.all_gather(z_weight, "dp", axis=0, tiled=True),
        lax.all_gather(x_weight, "dp", axis=0, tiled=True),
        lax.all_gather(dt_weight, "dp", axis=0, tiled=True),
        lax.all_gather(bc_weight, "dp", axis=0, tiled=True),
        lax.all_gather(out_weight, "dp", axis=1, tiled=True),
    )
    cot_full = lax.all_gather(cotangent.astype(jnp.bfloat16), "tensor", axis=0, tiled=True)
    out_part = left_dot(mixed, cot_full)
    d_mixed = right_dot(cot_full, out_full)
    d_masked = d_mixed * live_mask[:, None]
    gain_part = jnp.sum(d_masked * gated * gate_inv[:, None], axis=0)
    d_scaled = d_masked * gate_gain
    inner_dot = lax.psum(jnp.sum(d_scaled * gated, axis=1), "tensor")
    d_gated = gate_inv[:, None] * d_scaled - gated * (gate_inv**3 * inner_dot / INNER)[:, None]
    grads = core_back(d_gated)
    dz_b = grads[0].astype(jnp.bfloat16)
    dx_b = grads[1].astype(jnp.bfloat16)
    dbc_b = grads[2].astype(jnp.bfloat16)
    ddt_b = grads[3].astype(jnp.bfloat16)
    z_part = left_dot(normed, dz_b)
    x_part = left_dot(normed, dx_b)
    dt_part = left_dot(normed, ddt_b)
    bc_part = left_dot(normed, dbc_b)
    total = right_dot(dz_b, z_full)
    total = total + right_dot(dx_b, x_full)
    total = total + right_dot(ddt_b, dt_full)
    d_normed = lax.psum_scatter(
        total + right_dot(dbc_b, bc_full), "tensor", scatter_dimension=0, tiled=True
    )
    z_weight_grad, x_weight_grad, dt_weight_grad, out_weight_grad = (
        lax.psum_scatter(z_part, "dp", scatter_dimension=0, tiled=True),
        lax.psum_scatter(x_part, "dp", scatter_dimension=0, tiled=True),
        lax.psum_scatter(dt_part, "dp", scatter_dimension=0, tiled=True),
        lax.psum_scatter(out_part, "dp", scatter_dimension=1, tiled=True),
    )
    bc_weight_grad = lax.psum_scatter(bc_part, ("dp", "tensor"), scatter_dimension=0, tiled=True)
    norm_part = jnp.sum(d_normed * residual * inv_rms[:, None], axis=0)
    d_gain = d_normed * norm_gain
    input_grad = (
        cotangent
        + inv_rms[:, None] * d_gain
        - residual * (inv_rms**3 * jnp.sum(d_gain * residual, axis=1) / D)[:, None]
    )
    conv_x_grad, conv_x_bias_grad, dt_bias_grad, a_log_grad, d_skip_grad, gate_gain_grad = lax.psum(
        (grads[4], grads[5], grads[8], grads[9], grads[10], gain_part), "dp"
    )
    conv_bc_grad, conv_bc_bias_grad, norm_gain_grad = lax.psum(
        (grads[6], grads[7], norm_part), ("dp", "tensor")
    )
    return (
        block_out,
        input_grad,
        norm_gain_grad,
        z_weight_grad,
        x_weight_grad,
        bc_weight_grad,
        dt_weight_grad,
        conv_x_grad,
        conv_x_bias_grad,
        conv_bc_grad,
        conv_bc_bias_grad,
        dt_bias_grad,
        a_log_grad,
        d_skip_grad,
        gate_gain_grad,
        out_weight_grad,
    )


def solution(mesh):
    placed = (
        P(("dp", "tensor"), None),
        P("dp"),
        P("dp"),
        P(),
        P("dp", "tensor"),
        P("dp", "tensor"),
        P("dp", None),
        P("dp", "tensor"),
        P(None, "tensor"),
        P("tensor"),
        P(),
        P(),
        P("tensor"),
        P("tensor"),
        P("tensor"),
        P("tensor"),
        P("tensor", "dp"),
        P(("dp", "tensor"), None),
    )
    return jax.shard_map(
        local,
        mesh=mesh,
        in_specs=placed,
        out_specs=(
            P(("dp", "tensor"), None),
            P(("dp", "tensor"), None),
            P(),
            P("dp", "tensor"),
            P("dp", "tensor"),
            P(("dp", "tensor"), None),
            P("dp", "tensor"),
            P(None, "tensor"),
            P("tensor"),
            P(),
            P(),
            P("tensor"),
            P("tensor"),
            P("tensor"),
            P("tensor"),
            P("tensor", "dp"),
        ),
        check_vma=False,
    )
```

profile of v0, /device:TPU:0, one launch (start us, length us, event | category | flops | bytes accessed | tf_op | source)
XLA Modules:
  0.0 691.3 jit_solution(10442533371596515218)
XLA Ops:
  9.5 1.3 fusion.131
  12.9 1.2 multiply_reduce_fusion.18
  14.1 2.1 compare_convert_fusion.1
  18.5 23.7 %all-gather = bf16[16,64,16]{1,2,0:T(8,128)(2,1)S(1)} all-gather(bf16[1,64,16]{1,2,0:T(8,128)(2,1)} %bitcast.220), channel_id=1, replica_groups=mesh['dp'=16,'tensor'=2] {'dp'}, dimensions={0}, use_global_device_ids=true | all-gather | bytes 34816 | tf_op jit(solution)/shard_map/all_gather | solution.py:136
  42.4 1.2 multiply_convert_fusion.1
  43.6 9.2 %all_gather.26 = bf16[256,1024]{1,0:T(8,128)(2,1)S(1)} all-gather(bf16[128,1024]{1,0:T(8,128)(2,1)S(1)} %multiply_convert_fusion.1), channel_id=1, replica_groups=mesh['dp'=16,'tensor'=2] {'tensor'}, dimensions={0}, use_global_device_ids=true | all-gather | bytes 786432 | tf_op jit(solution)/shard_map/all_gather | solution.py:140
  52.9 8.5 %all_gather.32 = bf16[256,1024]{1,0:T(8,128)(2,1)} all-gather(bf16[128,1024]{1,0:T(8,128)(2,1)S(1)} %convert_element_type.74), channel_id=1, replica_groups=mesh['dp'=16,'tensor'=2] {'tensor'}, dimensions={0}, use_global_device_ids=true | all-gather | bytes 786432 | tf_op jit(solution)/shard_map/all_gather | solution.py:177
  62.8 1.2 multiply_multiply_fusion.4
  64.0 19.0 %all_gather.29 = bf16[1024,256]{1,0:T(8,128)(2,1)S(1)} all-gather(bf16[64,256]{1,0:T(8,128)(2,1)S(1)} %copy-done.62), channel_id=1, replica_groups=mesh['dp'=16,'tensor'=2] {'dp'}, dimensions={0}, use_global_device_ids=true | all-gather | bytes 557056 | tf_op jit(solution)/shard_map/all_gather | solution.py:137
  90.2 2.5 fusion.132
  92.7 1.8 fusion.19
  95.6 1.2 copy.168
  96.9 3.0 fusion.2
  99.9 2.1 copy.181
  102.0 2.0 copy.175
  106.0 3.0 fusion.1
  109.0 2.0 copy.182
  111.1 4.3 multiply_reduce_fusion.11
  115.3 4.9 psum.77
  120.3 19.8 %all-gather.9.cloned.1.call-done = bf16[1024,1024]{0,1:T(8,128)(2,1)} async-done(((bf16[1024,64]{0,1:T(8,128)(2,1)}), bf16[1024,1024]{0,1:T(8,128)(2,1)}) %all-gather.9.cloned.1.call-update) | async-done | bytes 2097168 | tf_op jit(solution)/shard_map/all_gather | solution.py:138
  140.0 4.2 multiply_reduce_fusion
  144.2 5.1 psum.78
  149.3 4.9 multiply_reduce_fusion.1
  154.2 2.6 copy.183
  156.8 2.3 fusion.125
  159.1 2.1 copy.184
  161.2 1.9 multiply_reduce_fusion.17
  163.0 4.4 fusion.21
  167.4 2.2 convolution_bitcast_fusion.1
  170.6 1.2 multiply_reduce_fusion.16
  171.8 1.6 convolution_bitcast_fusion.4
  173.4 2.0 multiply_reduce_fusion.12
  178.7 2.0 copy.185
  180.7 1.9 multiply_reduce_fusion.15
  182.6 4.4 fusion.23
  187.0 1.5 fusion
  188.6 1.3 pad_add_fusion
  189.9 2.6 copy.186
  192.5 2.0 convolution_bitcast_fusion.5
  196.4 4.2 multiply_reduce_fusion.5
  201.3 1.7 reduce_window_sum.36
  203.8 1.4 copy.192
  205.3 1.4 copy.194
  207.5 1.4 bitcast_add_fusion.2
  208.9 1.3 bitcast_add_fusion.5
  211.2 1.7 reduce_window_sum.37
  213.9 1.4 multiply_reduce_fusion.22
  215.3 1.4 slice_multiply_fusion.5
  216.7 1.5 fusion.120
  226.9 1.3 convolution_add_fusion
  228.3 3.4 fusion.116
  231.8 1.3 fusion.137
  233.4 2.8 fusion.115
  237.3 2.7 fusion.135
  240.1 2.8 fusion.136
  243.8 58.3 %all-reduce.36 = (f32[4,1024]{1,0:T(4,128)}, f32[1024]{0:T(1024)}, f32[16]{0:T(128)}, f32[16]{0:T(128)}, f32[16]{0:T(128)}, /*index=5*/f32[1024]{0:T(1024)}) all-reduce(f32[4,1024]{1,0:T(4,128)S(1)} %pad_add_fusion.4, f32[1024]{0:T(1024)S(1)} %get-tuple-element.26, ...), channel_id=1, replica_groups=mesh['dp'=16,'tensor'=2] {'dp'}, use_global_device_ids=true, to_apply=%region_34.35 | all-reduce | flops 6192 | bytes 49536 | tf_op jit(solution)/shard_map/psum | solution.py:214
  302.1 1.4 copy.202
  303.6 1.3 multiply_reduce_fusion.13
  304.9 37.4 %all-reduce.35 = (f32[1024]{0:T(1024)}, f32[4,256]{1,0:T(4,128)}, f32[256]{0:T(256)}) all-reduce(f32[1024]{0:T(1024)S(1)} %get-tuple-element.28, f32[4,256]{1,0:T(4,128)S(1)} %pad_add_fusion.5, f32[256]{0:T(256)S(1)} %get-tuple-element.30), channel_id=1, replica_groups=mesh['dp'=16,'tensor'=2] {'dp','tensor'}, use_global_device_ids=true, to_apply=%region_25.26 | all-reduce | flops 2304 | bytes 18432 | tf_op jit(solution)/shard_map/psum | solution.py:217
  342.3 2.4 multiply_subtract_fusion.1
  344.7 113.8 %reduce-scatter.18.cloned.1.call-done = f32[32,256]{1,0:T(8,128)} async-done(((f32[1024,256]{1,0:T(8,128)}), f32[32,256]{1,0:T(8,128)}) %reduce-scatter.18.cloned.1.call-update) | async-done | bytes 32784 | tf_op jit(solution)/shard_map/reduce_scatter | solution.py:206
  458.5 73.1 %reduce-scatter.20.cloned.1.call-done = f32[1024,64]{0,1:T(8,128)} async-done(((f32[1024,1024]{0,1:T(8,128)}), f32[1024,64]{0,1:T(8,128)}) %reduce-scatter.20.cloned.1.call-update) | async-done | bytes 262160 | tf_op jit(solution)/shard_map/reduce_scatter | solution.py:204
  531.6 76.3 %reduce-scatter.14.cloned.1.call-done = f32[64,1024]{1,0:T(8,128)} async-done(((f32[1024,1024]{1,0:T(8,128)}), f32[64,1024]{1,0:T(8,128)}) %reduce-scatter.14.cloned.1.call-update) | async-done | bytes 262160 | tf_op jit(solution)/shard_map/reduce_scatter | solution.py:201
  607.9 76.2 %reduce-scatter.16.cloned.1.call-done = f32[64,1024]{1,0:T(8,128)} async-done(((f32[1024,1024]{1,0:T(8,128)}), f32[64,1024]{1,0:T(8,128)}) %reduce-scatter.16.cloned.1.call-update) | async-done | bytes 262160 | tf_op jit(solution)/shard_map/reduce_scatter | solution.py:202
  (328 shorter events, 39.0 us)
Async XLA Ops:
  7.2 45.7 %copy-start.22 = (f32[128,1024]{1,0:T(8,128)S(1)}, f32[128,1024]{1,0:T(8,128)}, u32[]{:S(2)}) copy-start(f32[128,1024]{1,0:T(8,128)} %param.35) | copy-start | bytes 1572868
  7.2 83.0 %all-gather.5.cloned.1.call-start = ((), (), s32[]{:S(2)}) async-start(), calls=%async_computation.7 | async-start | bytes 2228224 | tf_op jit(solution)/shard_map/all_gather | solution.py:135
  7.9 103.1 %all-gather.7.cloned.1.call-start = ((), (), s32[]{:S(2)}) async-start(), calls=%async_computation.8 | async-start | bytes 2228224 | tf_op jit(solution)/shard_map/all_gather | solution.py:134
  8.7 52.7 %copy-start.114 = (f32[16]{0:T(128)S(1)}, f32[16]{0:T(128)}, u32[]{:S(2)}) copy-start(f32[16]{0:T(128)} %param.30) | copy-start | bytes 196
  8.7 131.3 %all-gather.9.cloned.1.call-start = ((), (), s32[]{:S(2)}) async-start(), calls=%async_computation.9 | async-start | bytes 2228224 | tf_op jit(solution)/shard_map/all_gather | solution.py:138
  9.4 292.7 %reduce-scatter.22.cloned.1.call-start = ((), (), s32[]{:S(2)}) async-start(), calls=%async_computation.16 | async-start | bytes 557056
  12.9 49.5 %copy-start.112 = (f32[16]{0:T(128)}, f32[16]{0:T(128)S(1)}, u32[]{:S(2)}) copy-start(f32[16]{0:T(128)S(1)} %exp.57) | copy-start | bytes 196
  14.0 28.4 %copy-start.109 = (f32[128]{0:T(128)}, f32[128]{0:T(128)S(1)}, u32[]{:S(2)}) copy-start(f32[128]{0:T(128)S(1)} %multiply_reduce_fusion.18) | copy-start | bytes 1540
  14.1 48.3 %copy-start.95 = (f32[128]{0:T(128)}, f32[128]{0:T(128)S(1)}, u32[]{:S(2)}) copy-start(f32[128]{0:T(128)S(1)} %add_rsqrt_fusion.1) | copy-start | bytes 1540
  16.1 68.0 %copy-start.97 = (f32[128]{0:T(128)}, f32[128]{0:T(128)S(1)}, u32[]{:S(2)}) copy-start(f32[128]{0:T(128)S(1)} %get-tuple-element.99) | copy-start | bytes 1540
  16.1 68.0 %copy-start.94 = (f32[128]{0:T(128)}, f32[128]{0:T(128)S(1)}, u32[]{:S(2)}) copy-start(f32[128]{0:T(128)S(1)} %get-tuple-element.101) | copy-start | bytes 1540
  16.1 68.0 %copy-start.99 = (f32[128]{0:T(128)}, f32[128]{0:T(128)S(1)}, u32[]{:S(2)}) copy-start(f32[128]{0:T(128)S(1)} %get-tuple-element.100) | copy-start | bytes 1540
  17.6 70.5 %copy-start.79 = (f32[1,256]{1,0:T(1,128)}, f32[1,256]{1,0:T(1,128)S(1)}, u32[]{:S(2)}) copy-start(f32[1,256]{1,0:T(1,128)S(1)} %get-tuple-element.93) | copy-start | bytes 3076
  17.6 70.5 %copy-start.81 = (f32[1,256]{1,0:T(1,128)}, f32[1,256]{1,0:T(1,128)S(1)}, u32[]{:S(2)}) copy-start(f32[1,256]{1,0:T(1,128)S(1)} %get-tuple-element.94) | copy-start | bytes 3076
  17.6 70.5 %copy-start.83 = (f32[1,256]{1,0:T(1,128)}, f32[1,256]{1,0:T(1,128)S(1)}, u32[]{:S(2)}) copy-start(f32[1,256]{1,0:T(1,128)S(1)} %get-tuple-element.96) | copy-start | bytes 3076
  17.6 70.5 %copy-start.85 = (f32[1,256]{1,0:T(1,128)}, f32[1,256]{1,0:T(1,128)S(1)}, u32[]{:S(2)}) copy-start(f32[1,256]{1,0:T(1,128)S(1)} %get-tuple-element.95) | copy-start | bytes 3076
  18.5 74.2 %copy-start.52 = (f32[1,1024]{1,0:T(1,128)}, f32[1,1024]{1,0:T(1,128)S(1)}, u32[]{:S(2)}) copy-start(f32[1,1024]{1,0:T(1,128)S(1)} %get-tuple-element.90) | copy-start | bytes 12292
  18.5 74.2 %copy-start.54 = (f32[1,1024]{1,0:T(1,128)}, f32[1,1024]{1,0:T(1,128)S(1)}, u32[]{:S(2)}) copy-start(f32[1,1024]{1,0:T(1,128)S(1)} %get-tuple-element.92) | copy-start | bytes 12292
  18.5 74.2 %copy-start.56 = (f32[1,1024]{1,0:T(1,128)}, f32[1,1024]{1,0:T(1,128)S(1)}, u32[]{:S(2)}) copy-start(f32[1,1024]{1,0:T(1,128)S(1)} %get-tuple-element.91) | copy-start | bytes 12292
  42.3 20.1 %copy-start.37 = (bf16[1024,16]{0,1:T(8,128)(2,1)}, bf16[1024,16]{0,1:T(8,128)(2,1)S(1)}, u32[]{:S(2)}) copy-start(bf16[1024,16]{0,1:T(8,128)(2,1)S(1)} %reshape.385) | copy-start | bytes 98308
  42.4 54.4 %copy-start.46 = (f32[128,128]{1,0:T(8,128)}, f32[128,128]{1,0:T(8,128)S(1)}, u32[]{:S(2)}) copy-start(f32[128,128]{1,0:T(8,128)S(1)} %get-tuple-element.108) | copy-start | bytes 196612
  42.4 54.4 %copy-start.73 = (pred[128,128]{1,0:T(8,128)(4,1)}, pred[128,128]{1,0:T(8,128)(4,1)S(1)}, u32[]{:S(2)}) copy-start(pred[128,128]{1,0:T(8,128)(4,1)S(1)} %get-tuple-element.107) | copy-start | bytes 49156
  43.6 20.4 %copy-start.62 = (bf16[64,256]{1,0:T(8,128)(2,1)S(1)}, bf16[64,256]{1,0:T(8,128)(2,1)}, u32[]{:S(2)}) copy-start(bf16[64,256]{1,0:T(8,128)(2,1)} %param.24) | copy-start | bytes 98308
  61.4 22.9 %copy-start.50 = (s32[256]{0:T(256)S(1)}, s32[256]{0:T(256)}, u32[]{:S(2)}) copy-start(s32[256]{0:T(256)} %param.19) | copy-start | bytes 3076
  61.4 23.0 %copy-start.106 = (f32[16]{0:T(128)S(1)}, f32[16]{0:T(128)}, u32[]{:S(2)}) copy-start(f32[16]{0:T(128)} %param.32) | copy-start | bytes 196
  61.4 26.7 %copy-start.108 = (f32[256]{0:T(256)S(1)}, f32[256]{0:T(256)}, u32[]{:S(2)}) copy-start(f32[256]{0:T(256)} %param.29) | copy-start | bytes 3076
  62.4 25.7 %copy-start.28 = (f32[256,16]{1,0:T(8,128)}, f32[256,16]{1,0:T(8,128)S(1)}, u32[]{:S(2)}) copy-start(f32[256,16]{1,0:T(8,128)S(1)} %get-tuple-element.87) | copy-start | bytes 49156
  62.6 21.5 %copy-start.40 = (f32[128,16]{0,1:T(8,128)}, f32[128,16]{0,1:T(8,128)S(1)}, u32[]{:S(2)}) copy-start(f32[128,16]{0,1:T(8,128)S(1)} %copy.180) | copy-start | bytes 24580
  62.8 23.7 %copy-start.101 = (f32[16]{0:T(128)}, f32[16]{0:T(128)S(1)}, u32[]{:S(2)}) copy-start(f32[16]{0:T(128)S(1)} %slice_bitcast_fusion.2) | copy-start | bytes 196
  84.4 8.3 %copy-start.65 = (f32[256]{0:T(256)}, f32[256]{0:T(256)S(1)}, u32[]{:S(2)}) copy-start(f32[256]{0:T(256)S(1)} %get-tuple-element.104) | copy-start | bytes 3076
  84.4 8.4 %copy-start.68 = (f32[256]{0:T(256)}, f32[256]{0:T(256)S(1)}, u32[]{:S(2)}) copy-start(f32[256]{0:T(256)S(1)} %get-tuple-element.106) | copy-start | bytes 3076
  84.4 8.4 %copy-start.70 = (f32[256]{0:T(256)}, f32[256]{0:T(256)S(1)}, u32[]{:S(2)}) copy-start(f32[256]{0:T(256)S(1)} %get-tuple-element.105) | copy-start | bytes 3076
  84.4 55.6 %copy-start.77 = (f32[256]{0:T(256)}, f32[256]{0:T(256)S(1)}, u32[]{:S(2)}) copy-start(f32[256]{0:T(256)S(1)} %compare_convert_fusion) | copy-start | bytes 3076
  87.3 9.5 %copy-start.58 = (f32[128,16]{0,1:T(8,128)}, f32[128,16]{0,1:T(8,128)S(1)}, u32[]{:S(2)}) copy-start(f32[128,16]{0,1:T(8,128)S(1)} %copy.174) | copy-start | bytes 24580
  88.1 17.2 %copy-start.48 = (f32[128,128]{1,0:T(8,128)}, f32[128,128]{1,0:T(8,128)S(1)}, u32[]{:S(2)}) copy-start(f32[128,128]{1,0:T(8,128)S(1)} %get-tuple-element.110) | copy-start | bytes 196612
  89.0 15.6 %copy-start.4 = (f32[256,256]{1,0:T(8,128)}, f32[256,256]{1,0:T(8,128)S(1)}, u32[]{:S(2)}) copy-start(f32[256,256]{1,0:T(8,128)S(1)} %get-tuple-element.61) | copy-start | bytes 786436
  89.3 15.9 %copy-start.44 = (f32[128,128]{1,0:T(8,128)}, f32[128,128]{1,0:T(8,128)S(1)}, u32[]{:S(2)}) copy-start(f32[128,128]{1,0:T(8,128)S(1)} %fusion.84) | copy-start | bytes 196612
  89.5 7.3 %copy-start.42 = (f32[128,128]{1,0:T(8,128)}, f32[128,128]{1,0:T(8,128)S(1)}, u32[]{:S(2)}) copy-start(f32[128,128]{1,0:T(8,128)S(1)} %fusion.88) | copy-start | bytes 196612
  90.2 6.7 copy-start.20
  99.9 6.1 copy-start.75
  99.9 6.1 copy-start.90
  99.9 6.1 copy-start.91
  104.6 6.5 copy-start.7
  111.1 29.0 %copy-start.36 = (f32[1024]{0:T(1024)S(1)}, f32[1024]{0:T(1024)}, u32[]{:S(2)}) copy-start(f32[1024]{0:T(1024)} %param.33) | copy-start | bytes 12292
  120.3 29.1 %copy-start.63 = (f32[256]{0:T(256)}, f32[256]{0:T(256)S(1)}, u32[]{:S(2)}) copy-start(f32[256]{0:T(256)S(1)} %add_rsqrt_fusion) | copy-start | bytes 3076
  189.9 6.4 copy-start.71
  196.4 11.1 %copy-start.29 = (f32[256,16]{1,0:T(8,128)S(1)}, f32[256,16]{1,0:T(8,128)}, u32[]{:S(2)}) copy-start(f32[256,16]{1,0:T(8,128)} %copy-done.28) | copy-start | bytes 49156
  200.5 13.4 %copy-start.25 = (f32[256,256]{1,0:T(8,128)S(1)}, f32[256,256]{1,0:T(8,128)}, u32[]{:S(2)}) copy-start(f32[256,256]{1,0:T(8,128)} %get-tuple-element.62) | copy-start | bytes 786436
  211.1 5.5 copy-start.31
  213.9 5.6 copy-start.66
  215.3 5.2 copy-start.16
  215.3 5.2 copy-start.84
  219.4 84.1 %reduce-scatter.12.cloned.1.call-start = ((), (), s32[]{:S(2)}) async-start(), calls=%async_computation.11 | async-start | bytes 1572864 | tf_op jit(solution)/shard_map/reduce_scatter | solution.py:197
  228.3 114.0 %reduce-scatter.10.cloned.1.call-start = ((), (), s32[]{:S(2)}) async-start(), calls=%async_computation.10 | async-start | bytes 1572864 | tf_op jit(solution)/shard_map/reduce_scatter | solution.py:164
  231.7 226.7 %reduce-scatter.18.cloned.1.call-start = ((), (), s32[]{:S(2)}) async-start(), calls=%async_computation.14 | async-start | bytes 1081344 | tf_op jit(solution)/shard_map/reduce_scatter | solution.py:206
  233.1 298.4 %reduce-scatter.20.cloned.1.call-start = ((), (), s32[]{:S(2)}) async-start(), calls=%async_computation.15 | async-start | bytes 4456448 | tf_op jit(solution)/shard_map/reduce_scatter | solution.py:204
  236.3 371.6 %reduce-scatter.14.cloned.1.call-start = ((), (), s32[]{:S(2)}) async-start(), calls=%async_computation.12 | async-start | bytes 4456448 | tf_op jit(solution)/shard_map/reduce_scatter | solution.py:201
  240.1 444.0 %reduce-scatter.16.cloned.1.call-start = ((), (), s32[]{:S(2)}) async-start(), calls=%async_computation.13 | async-start | bytes 4456448 | tf_op jit(solution)/shard_map/reduce_scatter | solution.py:202
  242.9 59.2 %copy-start.102 = (f32[256]{0:T(256)S(1)}, f32[256]{0:T(256)}, u32[]{:S(2)}) copy-start(f32[256]{0:T(256)} %get-tuple-element.52) | copy-start | bytes 3076
  242.9 60.6 %copy-start.2 = (f32[128,1024]{1,0:T(8,128)S(1)}, f32[128,1024]{1,0:T(8,128)}, u32[]{:S(2)}) copy-start(f32[128,1024]{1,0:T(8,128)} %param.18) | copy-start | bytes 1572868
  242.9 60.6 %copy-start.51 = (f32[1024]{0:T(1024)S(1)}, f32[1024]{0:T(1024)}, u32[]{:S(2)}) copy-start(f32[1024]{0:T(1024)} %param.21) | copy-start | bytes 12292
  243.0 60.6 %copy-start.96 = (f32[128]{0:T(128)S(1)}, f32[128]{0:T(128)}, u32[]{:S(2)}) copy-start(f32[128]{0:T(128)} %copy-done.95) | copy-start | bytes 1540
  243.0 99.3 %copy-start.110 = (f32[128]{0:T(128)S(1)}, f32[128]{0:T(128)}, u32[]{:S(2)}) copy-start(f32[128]{0:T(128)} %copy-done.109) | copy-start | bytes 1540
  243.0 99.3 %copy-start.23 = (f32[128,1024]{1,0:T(8,128)S(1)}, f32[128,1024]{1,0:T(8,128)}, u32[]{:S(2)}) copy-start(f32[128,1024]{1,0:T(8,128)} %param.35) | copy-start | bytes 1572868
  (62 other events, 162.9 us)
Sparse Core Ops, SparseCore 0:
  10.2 44.2 all-gather.4
  56.6 40.9 all-gather.6
  99.8 40.1 all-gather.8
  219.5 54.8 reduce-scatter.21
  276.5 19.4 reduce-scatter.11
  298.1 21.0 reduce-scatter.9
  321.9 136.4 reduce-scatter.17
  462.9 68.6 reduce-scatter.19
  536.0 71.8 reduce-scatter.13
  612.2 71.8 reduce-scatter.15
where the time goes:
time: 702 us; the launch traced here: 691 us
  waiting for transfers between devices  361 us (51%)
  blocking collectives  166 us (24%)
  matrix products  61.5 us (9%)
  other arithmetic  43.2 us (6%)
  local copies, waits for them, and re-layouts  42 us (6%)
  between operations  16.6 us (2%)
    reduce_scatter x1, waiting for transfers between devices, local(): lax.psum_scatter(bc_part, ('dp', 'tensor'), scatter_dimension=0, tiled=True)  114 us
    reduce_scatter x1, waiting for transfers between devices, local(): lax.psum_scatter(z_part, 'dp', scatter_dimension=0, tiled=True)  76.3 us
    reduce_scatter x1, waiting for transfers between devices, local(): lax.psum_scatter(x_part, 'dp', scatter_dimension=0, tiled=True)  76.2 us
    reduce_scatter x1, waiting for transfers between devices, local(): lax.psum_scatter(out_part, 'dp', scatter_dimension=1, tiled=True)  73.1 us
    psum x1, blocking collectives, local(): lax.psum((grads[4], grads[5], grads[8], grads[9], grads[10], gain_part),...  58.3 us
    psum x1, blocking collectives, local(): lax.psum((grads[6], grads[7], norm_part), ('dp', 'tensor'))  37.4 us
    all_gather x1, blocking collectives, local(): lax.all_gather(dt_weight, 'dp', axis=0, tiled=True)  23.7 us
    all_gather x1, waiting for transfers between devices, local(): lax.all_gather(out_weight, 'dp', axis=1, tiled=True)  19.8 us
  transfers between devices with their start and end apart: 10, of which 5 were waited for; matrix products, arithmetic and copies ran while one was open for 10% of the time, Pallas kernels for 0%

commit v1 on v0

v1 whole, which is shorter than its diff:
```python
import jax
import jax.numpy as jnp
from jax import lax
from jax.experimental import pallas as pl
from jax.experimental.pallas import tpu as pltpu
from jax.sharding import PartitionSpec as P


SPAN = 128
LANES = 128
epsilon = 1e-05
f32 = jnp.float32
bf16 = jnp.bfloat16
HI = lax.Precision.HIGHEST


def dot_nn(a, b, p=None):
    return lax.dot_general(a, b, (((1,), (0,)), ((), ())), precision=p, preferred_element_type=f32)


def dot_nt(a, b, p=None):
    return lax.dot_general(a, b, (((1,), (1,)), ((), ())), precision=p, preferred_element_type=f32)


def dot_tn(a, b, p=None):
    return lax.dot_general(a, b, (((0,), (0,)), ((), ())), precision=p, preferred_element_type=f32)


def call(micros, body, outs, *args, scratch=()):
    return pl.pallas_call(
        body,
        out_shape=[jax.ShapeDtypeStruct(s, d) for s, d in outs],
        scratch_shapes=list(scratch),
        cost_estimate=pl.CostEstimate(
            flops=int(micros * 9e8), transcendentals=0, bytes_accessed=int(micros * 3e6)
        ),
    )(*args)


def paired(a, w, at):
    half = w[0].shape[0]
    return dot_nn(a[:, :half], w[0][:, at]) + dot_nn(a[:, half:], w[1][:, at])


def split(v):
    high = v.astype(bf16)
    return jnp.concatenate([high, (v - high.astype(f32)).astype(bf16)], 0)


def iota(shape, axis):
    return lax.broadcasted_iota(jnp.int32, shape, axis)


def silu(v):
    return v * jax.nn.sigmoid(v)


def silu_slope(v):
    s = jax.nn.sigmoid(v)
    return s * (1.0 + v * (1.0 - s))


def conv(v, w, b, link):
    taps = w.shape[0]
    out = b + w[taps - 1 : taps] * v
    for lag in range(1, taps):
        moved = pltpu.roll(v, lag, 0) * link[:, lag : lag + 1]
        out = out + w[taps - 1 - lag : taps - lag] * moved
    return out


def conv_back(dv, v, w, link):
    taps = w.shape[0]
    rows = v.shape[0]
    dpre = w[taps - 1 : taps] * dv
    dw = [jnp.sum(dv * v, axis=0, keepdims=True)]
    for lag in range(1, taps):
        masked = dv * link[:, lag : lag + 1]
        dw.insert(0, jnp.sum(masked * pltpu.roll(v, lag, 0), axis=0, keepdims=True))
        dpre = dpre + w[taps - 1 - lag : taps - lag] * pltpu.roll(masked, rows - lag, 0)
    return dpre, dw, jnp.sum(dv, axis=0, keepdims=True)


def prepare(dtpre, dtb, alog, segc, segr):
    v = dtpre + dtb
    step = jnp.maximum(v, 0.0) + jnp.log1p(jnp.exp(-jnp.abs(v)))
    logd = -step * jnp.exp(alog)
    row = iota((SPAN, SPAN), 0)
    col = iota((SPAN, SPAN), 1)
    lower = row >= col
    tri = lower.astype(f32)
    cum = [dot_nn(tri, logd[k * SPAN : (k + 1) * SPAN], HI) for k in range(2)]
    cum_t = [c.T for c in cum]
    mask = [
        (segc[k * SPAN : (k + 1) * SPAN] == segr[:, k * SPAN : (k + 1) * SPAN]) & lower
        for k in range(2)
    ]
    edge = segc[SPAN - 1 : SPAN]
    keep = (segc[SPAN:] == edge).astype(f32)
    tail = (segc[:SPAN] == edge).astype(f32)
    grow = jnp.exp(cum[1]) * keep
    coef = jnp.exp(cum[0][SPAN - 1 : SPAN] - cum[0]) * tail
    return v, step, logd, cum, cum_t, mask, grow, coef


def spread(v, first, width):
    lane = iota((v.shape[0], LANES), 1)
    out = jnp.broadcast_to(v[:, first : first + 1], (v.shape[0], LANES))
    for k in range(1, LANES // width):
        out = jnp.where(lane >= k * width, v[:, first + k : first + k + 1], out)
    return out


def decay(cum, cum_t, mask, h):
    return jnp.where(mask, jnp.exp(cum[:, h : h + 1] - cum_t[h : h + 1, :]), 0.0)


def fwd_body(width, nrm, w1a, w1b, link, segc, segr, cx, cxb, cbc, cbcb, dtb, alog,
             xpre_o, xc_o, y_o, bcpre_o, bcc_o, dt_o):
    inner = xc_o.shape[1]
    state = bcc_o.shape[1] // 2
    x = nrm[...]
    w1 = (w1a, w1b)
    pre = paired(x, w1, slice(inner, w1a.shape[1]))
    bcpre_o[...] = pre[:, : 2 * state]
    dt_o[...] = pre[:, 2 * state :]
    wide = 2 * LANES
    for c in range(inner // wide):
        xpre_o[:, c * wide : (c + 1) * wide] = paired(x, w1, slice(c * wide, (c + 1) * wide))
    lk = link[...]
    for c in range(2 * state // LANES):
        at = slice(c * LANES, (c + 1) * LANES)
        bcc_o[:, at] = conv(bcpre_o[:, at], cbc[:, at], cbcb[:, at], lk)
    bs = silu(bcc_o[:, :state])
    cs = silu(bcc_o[:, state:])
    _, step, _, cum, cum_t, mask, grow, coef = prepare(
        dt_o[...], dtb[...], alog[...], segc[...], segr[...]
    )
    scores = [
        dot_nt(cs[k * SPAN : (k + 1) * SPAN], bs[k * SPAN : (k + 1) * SPAN], HI) for k in range(2)
    ]
    b0 = bs[:SPAN].astype(bf16)
    c1 = cs[SPAN:].astype(bf16)
    c1 = jnp.concatenate([c1, c1], 1)
    per = LANES // width
    lane = iota((SPAN, LANES), 1)
    for j in range(inner // LANES):
        at = slice(j * LANES, (j + 1) * LANES)
        xc = conv(xpre_o[:, at], cx[:, at], cxb[:, at], lk)
        xc_o[:, at] = xc
        u = spread(step, j * per, width) * silu(xc)
        ub = u.astype(bf16)
        for k in range(2):
            rows = slice(k * SPAN, (k + 1) * SPAN)
            y = None
            for i in range(per):
                h = j * per + i
                w = (decay(cum[k], cum_t[k], mask[k], h) * scores[k]).astype(bf16)
                part = dot_nn(w, ub[rows])
                y = part if y is None else jnp.where(lane >= i * width, part, y)
            if k:
                kept = (spread(coef, j * per, width) * u[:SPAN]).astype(bf16)
                st = split(dot_tn(b0, kept))
                y = y + spread(grow, j * per, width) * dot_nn(c1, st)
            y_o[rows, at] = y


def as_rows(col):
    return jnp.broadcast_to(col, (col.shape[0], LANES)).T[:8]


def as_col(rows):
    return jnp.broadcast_to(rows[:1], (LANES, rows.shape[1])).T[:, :1]


def dmix_body(cot, outa, outb, live, dm_o):
    wide = 2 * LANES
    x = cot[...]
    lv = live[...]
    for c in range(dm_o.shape[1] // wide):
        at = slice(c * wide, (c + 1) * wide)
        dm_o[:, at] = paired(x, (outa, outb), at) * lv


def gate_body(nrm, wza, wzb, y_r, xc_r, dsk, dm_r, gain, z_o, g_o, sums_o):
    wide = 2 * LANES
    x = nrm[...]
    squares = jnp.zeros((x.shape[0], LANES), f32)
    dots = jnp.zeros((x.shape[0], LANES), f32)
    for c in range(z_o.shape[1] // wide):
        at = slice(c * wide, (c + 1) * wide)
        z_o[:, at] = paired(x, (wza, wzb), at)
    for c in range(z_o.shape[1] // LANES):
        at = slice(c * LANES, (c + 1) * LANES)
        g = (y_r[:, at] + dsk[:, at] * silu(xc_r[:, at])) * silu(z_o[:, at])
        g_o[:, at] = g
        squares = squares + g * g
        dots = dots + dm_r[:, at] * gain[:, at] * g
    sums_o[:8] = as_rows(jnp.sum(squares, axis=1, keepdims=True))
    sums_o[8:] = as_rows(jnp.sum(dots, axis=1, keepdims=True))


def mix_body(full, g_r, sums, sums2, gain, live, cot, outa, outb,
             blk_o, keep_o, send_o, mixed):
    inv = lax.rsqrt(as_col(sums[:8] + sums2[:8]) / full + epsilon)
    wide = 2 * LANES
    for c in range(g_r.shape[1] // LANES):
        at = slice(c * LANES, (c + 1) * LANES)
        mixed[:, at] = (g_r[:, at] * inv * gain[:, at] * live[...]).astype(bf16)
    x = cot[...]
    half = keep_o.shape[0]
    for c in range(g_r.shape[1] // wide):
        at = slice(c * wide, (c + 1) * wide)
        send_o[:, at] = dot_tn(x[:, half:], mixed[:, at]).astype(bf16)
        keep_o[:, at] = dot_tn(x[:, :half], mixed[:, at]).astype(bf16)
    m = mixed[...]
    blk_o[:, :half] = dot_nt(m, outa[...])
    blk_o[:, half:] = dot_nt(m, outb[...])


def dz_body(full, nrm, g_r, dm_r, z_r, y_r, xc_r, dsk, gain, sums, sums2,
            dz_o, dy_o, gp_o, keep_o, send_o):
    inv = lax.rsqrt(as_col(sums[:8] + sums2[:8]) / full + epsilon)
    back = inv * inv * inv * as_col(sums[8:] + sums2[8:]) / full
    for c in range(z_r.shape[1] // LANES):
        at = slice(c * LANES, (c + 1) * LANES)
        z = z_r[:, at]
        s = jax.nn.sigmoid(z)
        g = g_r[:, at]
        dm = dm_r[:, at]
        gp_o[:, at] = jnp.sum(dm * g * inv, axis=0, keepdims=True)
        dg = inv * (dm * gain[:, at]) - g * back
        y = y_r[:, at] + dsk[:, at] * silu(xc_r[:, at])
        dz_o[:, at] = (dg * y * (s * (1.0 + z * (1.0 - s)))).astype(bf16)
        dy_o[:, at] = dg * (z * s)
    x = nrm[...]
    half = keep_o.shape[0]
    wide = 2 * LANES
    for c in range(z_r.shape[1] // wide):
        at = slice(c * wide, (c + 1) * wide)
        send_o[:, at] = dot_tn(x[:, half:], dz_o[:, at]).astype(bf16)
        keep_o[:, at] = dot_tn(x[:, :half], dz_o[:, at]).astype(bf16)


def bwd_body(width, nrm, dy_r, xpre_r, xc_r, y_r, bcpre_r, bcc_r, dt_r, link, segc, segr, cx,
             cbc, dtb, alog, dsk, dx_o, sm_o, keep_o, send_o, dc_s):
    inner = xc_r.shape[1]
    state = bcc_r.shape[1] // 2
    lk = link[...]
    bs = silu(bcc_r[:, :state])
    cs = silu(bcc_r[:, state:])
    v, step, logd, cum, cum_t, mask, grow, coef = prepare(
        dt_r[...], dtb[...], alog[...], segc[...], segr[...]
    )
    scores = [
        dot_nt(cs[k * SPAN : (k + 1) * SPAN], bs[k * SPAN : (k + 1) * SPAN], HI) for k in range(2)
    ]
    b0 = bs[:SPAN].astype(bf16)
    c1 = cs[SPAN:].astype(bf16)
    b00 = jnp.concatenate([b0, b0], 1)
    c11 = jnp.concatenate([c1, c1], 1)
    per = LANES // width
    lane = iota((SPAN, LANES), 1)
    rows_t = 2 * SPAN
    dcum = jnp.zeros((rows_t, LANES), f32)
    dstep = jnp.zeros((rows_t, LANES), f32)
    dsc = [jnp.zeros((SPAN, SPAN), f32) for _ in range(2)]
    dc1 = jnp.zeros((SPAN, state), f32)
    db0 = jnp.zeros((SPAN, state), f32)
    fold_row = iota((LANES, LANES), 0)
    fold_col = iota((LANES, LANES), 1)
    sm_o[...] = jnp.zeros(sm_o.shape, f32)
    for j in range(inner // LANES):
        at = slice(j * LANES, (j + 1) * LANES)
        xc = xc_r[:, at]
        xs = silu(xc)
        se = spread(step, j * per, width)
        u = se * xs
        ub = u.astype(bf16)
        dy = dy_r[:, at]
        dyb = dy.astype(bf16)
        ce = spread(coef, j * per, width)
        ge = spread(grow, j * per, width)
        kept = (ce * u[:SPAN]).astype(bf16)
        st = split(dot_tn(b0, kept))
        zb = (ge * dy[SPAN:]).astype(bf16)
        dst = split(dot_tn(c1, zb))
        dc1 = dc1 + dot_nt(zb, st[:state])
        db0 = db0 + dot_nt(kept, dst[:state])
        over = dot_nn(c11, st)
        under = dot_nn(b00, dst)
        dus = []
        for k in range(2):
            rows = slice(k * SPAN, (k + 1) * SPAN)
            du = None
            for i in range(per):
                h = j * per + i
                dec = decay(cum[k], cum_t[k], mask[k], h)
                w = (dec * scores[k]).astype(bf16)
                part = dot_tn(w, dyb[rows])
                du = part if du is None else jnp.where(lane >= i * width, part, du)
                inside = (lane >= i * width) & (lane < (i + 1) * width)
                mine = jnp.where(inside, dy[rows], 0.0).astype(bf16)
                dsc[k] = dsc[k] + dec * dot_nt(mine, ub[rows])
            dus.append(du)
        ubf = ub.astype(f32)
        dyf = dyb.astype(f32)
        net = jnp.concatenate(
            [
                dyf[:SPAN] * y_r[:SPAN, at] - ubf[:SPAN] * dus[0] - kept.astype(f32) * under,
                dyf[SPAN:] * (y_r[SPAN:, at] - ge * over) + zb.astype(f32) * over
                - ubf[SPAN:] * dus[1],
            ],
            0,
        )
        du = jnp.concatenate([dus[0] + ce * under, dus[1]], 0)
        fold = (fold_col == j * per + fold_row // width).astype(f32)
        dcum = dcum + dot_nn(net, fold, HI)
        dstep = dstep + dot_nn(du * xs, fold, HI)
        sm_o[6:7, at] = jnp.sum(dy * xs, axis=0, keepdims=True)
        dxc = (du * se + dsk[:, at] * dy) * silu_slope(xc)
        dpre, dw, db = conv_back(dxc, xpre_r[:, at], cx[:, at], lk)
        dx_o[:, at] = dpre.astype(bf16)
        for k, piece in enumerate(dw):
            sm_o[k : k + 1, at] = piece
        sm_o[4:5, at] = db
    upper = (iota((rows_t, rows_t), 0) <= iota((rows_t, rows_t), 1)) & (segc[...] == segr[...])
    dlog = dot_nn(upper.astype(f32), dcum, HI)
    ddt = (dstep - dlog * jnp.exp(alog[...])) * jax.nn.sigmoid(v)
    dx_o[:, inner + 2 * state :] = ddt.astype(bf16)
    sm_o[7:8, :LANES] = jnp.sum(ddt, axis=0, keepdims=True)
    sm_o[7:8, LANES : 2 * LANES] = jnp.sum(dlog * logd, axis=0, keepdims=True)
    for k in range(2):
        rows = slice(k * SPAN, (k + 1) * SPAN)
        db = dot_tn(dsc[k], cs[rows], HI)
        dc = dot_nn(dsc[k], bs[rows], HI)
        if k == 0:
            db = db + db0
        else:
            dc = dc + dc1
        dc_s[rows, :state] = db
        dc_s[rows, state:] = dc
    for c in range(2 * state // LANES):
        at = slice(c * LANES, (c + 1) * LANES)
        dpre, dw, db = conv_back(
            dc_s[:, at] * silu_slope(bcc_r[:, at]), bcpre_r[:, at], cbc[:, at], lk
        )
        dx_o[:, inner + c * LANES : inner + (c + 1) * LANES] = dpre.astype(bf16)
        for k, piece in enumerate(dw):
            sm_o[8 + k : 9 + k, at] = piece
        sm_o[12:13, at] = db
    x = nrm[...]
    wide = keep_o.shape[1]
    half = keep_o.shape[0]
    for first in range(0, wide, 2 * LANES):
        at = slice(first, min(first + 2 * LANES, wide))
        send_o[:, at] = dot_tn(x[:, half:], dx_o[:, at]).astype(bf16)
        keep_o[:, at] = dot_tn(x[:, :half], dx_o[:, at]).astype(bf16)


def dn_body(dz, wza, wzb, dx, w1a, w1b, dn_o):
    a = dz[...]
    b = dx[...]
    half = wza.shape[0]
    dn_o[:, :half] = dot_nt(a, wza[...]) + dot_nt(b, w1a[...])
    dn_o[:, half:] = dot_nt(a, wzb[...]) + dot_nt(b, w1b[...])


def restore(v, place):
    high = v.astype(bf16)
    low = (v - high.astype(f32)).astype(bf16)
    return dot_nt(high, place) + dot_nt(low, place)


def block_body(res, own, other, place, out_o):
    out_o[...] = res[...] + restore(own[...] + other[...].astype(f32), place[...])


def tail_body(res, cot, gain, own, other, place, ig_o, np_o):
    r = res[...]
    dn = restore(own[...] + other[...].astype(f32), place[...])
    inv = lax.rsqrt(jnp.mean(r * r, axis=1, keepdims=True) + epsilon)
    np_o[...] = jnp.sum(dn * r * inv, axis=0, keepdims=True)
    dg = dn * gain[...]
    inner = jnp.sum(dg * r, axis=1, keepdims=True) / r.shape[1]
    ig_o[...] = cot[...] + inv * dg - r * (inv * inv * inv * inner)


def head_body(res, cot, gain, place, nrm_o, cot_o):
    r = res[...]
    inv = lax.rsqrt(jnp.mean(r * r, axis=1, keepdims=True) + epsilon)
    n = (r * inv * gain[...]).astype(bf16)
    nrm_o[...] = dot_nn(n, place[...]).astype(bf16)
    cot_o[...] = dot_nn(cot[...].astype(bf16), place[...]).astype(bf16)


def solution(mesh):
    n = mesh.shape["dp"]
    nt = mesh.shape["tensor"]
    bits = [1 << k for k in range(n.bit_length() - 1)]
    assert (1 << len(bits)) == n and nt == 2

    def swap(v, bit):
        return lax.ppermute(v, "dp", [(i, i ^ bit) for i in range(n)])

    def cross(v):
        return lax.ppermute(v, "tensor", [(0, 1), (1, 0)])

    def after(v, *others):
        return lax.optimization_barrier((v,) + others)[0]

    def gather(v, start):
        if start is not None:
            v = after(v, start)
        marks = []
        for bit in reversed(bits):
            r = swap(v, bit)
            marks.append(r)
            if bit > 1:
                v = jnp.concatenate([v, r], 0)
        return v, r, marks

    def plus(a, b):
        return a.astype(f32) + b.astype(f32)

    def scatter(keep, send):
        for bit in bits[:-1]:
            r = swap(send, bit)
            half = keep.shape[0] // 2
            send = plus(keep[half:], r[half:]).astype(bf16)
            keep = plus(keep[:half], r[:half]).astype(bf16)
        return plus(keep, swap(send, bits[-1]))

    def whole(residual, segment_ids, live_counts, norm_gain, z_weight, x_weight, bc_weight,
              dt_weight, conv_x, conv_x_bias, conv_bc, conv_bc_bias, dt_bias, a_log, d_skip,
              gate_gain, out_weight, cotangent):
        half, width_d = residual.shape
        tokens = segment_ids.shape[0]
        inner = x_weight.shape[1]
        heads = dt_weight.shape[1]
        two_state = bc_weight.shape[1]
        head_width = inner // heads
        full = float(inner * nt)
        shard = width_d // n
        me = lax.axis_index("dp")
        side = lax.axis_index("tensor")

        pad = LANES - heads
        w1s = jnp.concatenate([x_weight, bc_weight, jnp.pad(dt_weight, ((0, 0), (0, pad)))], 1)
        outa, outb, m1 = gather(out_weight.T, None)
        w1a, w1b, m2 = gather(w1s, m1[1])
        wza, wzb, _ = gather(z_weight, m2[1])

        spot = jnp.arange(width_d, dtype=jnp.int32)
        block = spot // shard
        turned = jnp.zeros_like(block)
        for k in range(len(bits)):
            turned = turned | (((block >> k) & 1) << (len(bits) - 1 - k))
        source = (turned ^ me) * shard + spot % shard
        place = (spot[:, None] == source[None, :]).astype(bf16)

        gain = norm_gain[None, :]
        nrm_half, cot_half = call(
            3.5, head_body, [((half, width_d), bf16)] * 2, residual, cotangent, gain, place
        )

        def both(own, other):
            first = jnp.where(side == 0, own, other)
            second = jnp.where(side == 0, other, own)
            return jnp.concatenate([first, second], 0)

        nrm_other = cross(nrm_half)
        nrm = both(nrm_half, nrm_other)
        cot = both(cot_half, cross(after(cot_half, nrm_other)))

        spots = jnp.arange(tokens)
        links = [jnp.ones((tokens,), f32)]
        for lag in range(1, conv_x.shape[0]):
            moved = jnp.concatenate(
                [jnp.full((lag,), -1, jnp.int32), segment_ids[: tokens - lag]]
            )
            links.append((segment_ids == moved).astype(f32))
        link = jnp.stack(links, 1)
        segc = segment_ids[:, None]
        segr = segment_ids[None, :]
        live = (spots < live_counts[0]).astype(f32)[:, None]
        dtb = jnp.pad(dt_bias, (0, pad))[None, :]
        alog = jnp.pad(a_log, (0, pad))[None, :]
        dsk = jnp.repeat(d_skip, head_width)[None, :]
        gg = gate_gain[None, :]
        cxb = conv_x_bias[None, :]
        cbcb = conv_bc_bias[None, :]

        big = ((tokens, inner), f32)

        def fwd(*a):
            return fwd_body(head_width, *a)

        (dm,) = call(3.0, dmix_body, [big], cot, outa, outb, live)
        xpre, xc, y, bcpre, bcc, dtp = call(
            7.0, fwd,
            [big, big, big, ((tokens, two_state), f32), ((tokens, two_state), f32),
             ((tokens, LANES), f32)],
            nrm, w1a, w1b, link, segc, segr, conv_x, cxb, conv_bc, cbcb, dtb, alog,
        )
        z, g, sums = call(
            5.0, gate_body, [big, big, ((16, tokens), f32)],
            nrm, wza, wzb, y, xc, dsk, dm, gg,
        )
        sums2 = cross(sums)

        def mix(*a):
            return mix_body(full, *a)

        cut = width_d // 2
        blk, out_keep, out_send = call(
            4.0, mix,
            [((tokens, width_d), f32), ((cut, inner), bf16), ((cut, inner), bf16)],
            g, sums, sums2, gg, live, cot, outa, outb,
            scratch=[pltpu.VMEM((tokens, inner), bf16)],
        )
        out_sum = scatter(out_keep, out_send)

        def mine(v):
            return lax.dynamic_slice_in_dim(v, side * half, half, 0)

        def theirs(v):
            return lax.dynamic_slice_in_dim(v, (1 - side) * half, half, 0).astype(bf16)

        blk_other = cross(theirs(blk))
        (block_out,) = call(
            2.5, block_body, [((half, width_d), f32)], residual, mine(blk), blk_other, place
        )

        def back_z(*a):
            return dz_body(full, *a)

        dz, dy, gain_part, z_keep, z_send = call(
            6.0, back_z,
            [((tokens, inner), bf16), big, ((1, inner), f32), ((cut, inner), bf16),
             ((cut, inner), bf16)],
            after(nrm, out_send), g, dm, z, y, xc, dsk, gg, sums, sums2,
        )
        z_weight_grad = scatter(z_keep, z_send)

        def back(*a):
            return bwd_body(head_width, *a)

        wide = w1a.shape[1]
        dx, small, x_keep, x_send = call(
            14.0, back,
            [((tokens, wide), bf16), ((16, inner), f32), ((cut, wide), bf16), ((cut, wide), bf16)],
            nrm, dy, xpre, xc, y, bcpre, bcc, dtp, link, segc, segr, conv_x, conv_bc, dtb, alog,
            dsk,
            scratch=[pltpu.VMEM((tokens, two_state), f32)],
        )
        sum1 = scatter(x_keep, x_send)
        x_weight_grad = sum1[:, :inner]
        dt_weight_grad = sum1[:, inner + two_state : inner + two_state + heads]
        bc = sum1[:, inner : inner + two_state].reshape(nt, shard // nt, two_state)
        bc_weight_grad = (
            lax.dynamic_index_in_dim(bc, side, 0, False)
            + cross(lax.dynamic_index_in_dim(bc, 1 - side, 0, False))
        )

        (dn,) = call(5.5, dn_body, [((tokens, width_d), f32)], dz, wza, wzb, dx, w1a, w1b)
        dn_other = cross(theirs(dn))
        input_grad, norm_part = call(
            4.0, tail_body, [((half, width_d), f32), ((1, width_d), f32)],
            residual, cotangent, gain, mine(dn), dn_other, place,
        )

        few = jnp.concatenate(
            [small[:5], gain_part, small[6:13], norm_part], 0
        )
        few = jnp.concatenate([few[:8], few[13:14], few[8:13], few[:2]], 0)
        for bit in bits:
            few = few + swap(few, bit)
        shared = few[8:16]
        shared = shared + cross(shared)
        return (
            block_out,
            input_grad,
            shared[0],
            z_weight_grad,
            x_weight_grad,
            bc_weight_grad,
            dt_weight_grad,
            few[:4],
            few[4],
            shared[1:5, :two_state],
            shared[5, :two_state],
            few[7, :heads],
            few[7, LANES : LANES + heads],
            jnp.sum(few[6].reshape(heads, head_width), axis=1),
            few[5],
            out_sum.T,
        )

    placed = (
        P(("dp", "tensor"), None),
        P("dp"),
        P("dp"),
        P(),
        P("dp", "tensor"),
        P("dp", "tensor"),
        P("dp", None),
        P("dp", "tensor"),
        P(None, "tensor"),
        P("tensor"),
        P(),
        P(),
        P("tensor"),
        P("tensor"),
        P("tensor"),
        P("tensor"),
        P("tensor", "dp"),
        P(("dp", "tensor"), None),
    )

    return jax.shard_map(
        whole,
        mesh=mesh,
        in_specs=placed,
        out_specs=(
            P(("dp", "tensor"), None),
            P(("dp", "tensor"), None),
            P(),
            P("dp", "tensor"),
            P("dp", "tensor"),
            P(("dp", "tensor"), None),
            P("dp", "tensor"),
            P(None, "tensor"),
            P("tensor"),
            P(),
            P(),
            P("tensor"),
            P("tensor"),
            P("tensor"),
            P("tensor"),
            P("tensor", "dp"),
        ),
        check_vma=False,
    )
```

time: 702 us -> 240 us (0.34); the launches traced: 691 us -> 239 us
  waiting for transfers between devices: 361 us -> 104 us
  blocking collectives: 166 us -> 0 us
  matrix products: 61.5 us -> 0 us
  Pallas kernels: 0 us -> 56.7 us
  starting transfers between devices: 0.65 us -> 39.9 us
  other arithmetic: 43.2 us -> 15.7 us
  local copies, waits for them, and re-layouts: 42 us -> 20.6 us
  between operations: 16.6 us -> 1.68 us
    reduce_scatter x6 -> x0, waiting for transfers between devices: 339 us -> none  [the longest x1 114 us: local(): lax.psum_scatter(bc_part, ('dp', 'tensor'), scatter_dimension=0, tiled=True)]
    psum x4 -> x0, blocking collectives: 106 us -> none  [the longest x1 58.3 us: local(): lax.psum((grads[4], grads[5], grads[8], grads[9], grads[10], gain_part),...]
    ppermute x0 -> x35, waiting for transfers between devices: none -> 104 us  [the longest x28 96.3 us: swap(): return lax.ppermute(v, 'dp', [(i, i ^ bit) for i in range(n)])]
    dot_general x34 -> x0, matrix products: 60.4 us -> none  [the longest x6 18.4 us: ssd_core(): y_within = jnp.einsum('hts,shp->thp', weighted, block_x, precision=highest)]
    all_gather x4 -> x0, blocking collectives: 60.4 us -> none  [the longest x1 23.7 us: local(): lax.all_gather(dt_weight, 'dp', axis=0, tiled=True)]
    pallas_call x0 -> x10, Pallas kernels: none -> 56.7 us  [call(): pl.pallas_call(body, out_shape=[jax.ShapeDtypeStruct(s, d) for s, d in ou...]
    ppermute x0 -> x35, starting transfers between devices: none -> 39.9 us  [the longest x28 32.1 us: swap(): return lax.ppermute(v, 'dp', [(i, i ^ bit) for i in range(n)])]
    reduce_sum x13 -> x1, other arithmetic: 20.5 us -> 0.63 us  [whole(): jnp.sum(few[6].reshape(heads, head_width), axis=1)]
  transfers between devices with their start and end apart: 10 -> 35, of which waited for: 5 -> 18; matrix products, arithmetic and copies ran while one was open for 10% -> 13% of each run, Pallas kernels for 0% -> 20%
where the time goes in v1:
time: 240 us; the launch traced here: 239 us
  waiting for transfers between devices  104 us (43%)
  Pallas kernels  56.7 us (24%)
  starting transfers between devices  39.9 us (17%)
  local copies, waits for them, and re-layouts  20.6 us (9%)
  other arithmetic  15.7 us (7%)
    ppermute x28, waiting for transfers between devices, swap(): return lax.ppermute(v, 'dp', [(i, i ^ bit) for i in range(n)])  96.3 us
    pallas_call x10, Pallas kernels, call(): pl.pallas_call(body, out_shape=[jax.ShapeDtypeStruct(s, d) for s, d in ou...  56.7 us
    ppermute x28, starting transfers between devices, swap(): return lax.ppermute(v, 'dp', [(i, i ^ bit) for i in range(n)])  32.1 us
    ppermute x7, waiting for transfers between devices, cross(): return lax.ppermute(v, 'tensor', [(0, 1), (1, 0)])  8.16 us
    ppermute x7, starting transfers between devices, cross(): return lax.ppermute(v, 'tensor', [(0, 1), (1, 0)])  7.77 us
    unnamed x58, local copies, waits for them, and re-layouts  6.42 us
  transfers between devices with their start and end apart: 35, of which 18 were waited for; matrix products, arithmetic and copies ran while one was open for 13% of the time, Pallas kernels for 20%

profile of v1, /device:TPU:0, one launch (start us, length us, event | category | flops | bytes accessed | tf_op | source)
XLA Modules:
  0.0 239.0 jit_solution(15826067631966770460)
XLA Ops:
  0.7 4.1 %collective-permute-start.1 = (bf16[64,1024]{1,0:T(8,128)(2,1)}, bf16[64,1024]{1,0:T(8,128)(2,1)S(1)}, u32[]{:S(2)}, u32[]{:S(2)}) collective-permute-start(bf16[64,1024]{1,0:T(8,128)(2,1)} %bitcast.35), channel_id=1, source_target_pairs={{0,16},{2,18},{4,20},{6,22},{8,24},{10,26},{12,28},{14,30},{16,0},... | collective-permute-start | bytes 393224 | tf_op jit(solution)/shard_map/ppermute | solution.py:404
  4.8 2.2 fusion.place
  7.0 4.3 %collective-permute-done.1 = bf16[64,1024]{1,0:T(8,128)(2,1)S(1)} collective-permute-done((bf16[64,1024]{1,0:T(8,128)(2,1)}, bf16[64,1024]{1,0:T(8,128)(2,1)S(1)}, u32[]{:S(2)}, u32[]{:S(2)}) %collective-permute-start.1) | collective-permute-done | bytes 131104 | tf_op jit(solution)/shard_map/ppermute | solution.py:404
  11.3 0.9 collective-permute-start.2
  12.3 3.5 %shard_map.297 = (bf16[128,1024]{1,0:T(8,128)(2,1)}, bf16[128,1024]{1,0:T(8,128)(2,1)}) custom-call(f32[128,1024]{1,0:T(8,128)} %res.5, f32[128,1024]{1,0:T(8,128)} %cot.3, f32[1,1024]{1,0:T(1,128)} %bitcast.58, bf16[1024,1024]{1,0:T(8,128)(2,1)} %fusion.place), custom_call_target="tpu_custom_call" | custom-call | flops 3150000128 | bytes 10500000 | tf_op jit(solution)/shard_map/pallas_call | solution.py:30
  15.8 1.5 collective-permute-start
  17.4 1.4 collective-permute-done.2
  18.9 3.1 %collective-permute-start.3 = (bf16[64,1408]{1,0:T(8,128)(2,1)S(1)}, bf16[64,1408]{1,0:T(8,128)(2,1)S(1)}, u32[]{:S(2)}, u32[]{:S(2)}) collective-permute-start(bf16[64,1408]{1,0:T(8,128)(2,1)S(1)} %fusion.2), channel_id=1, source_target_pairs={{0,16},{2,18},{4,20},{6,22},{8,24},{10,26},{12,28},{14,30},{16,0},... | collective-permute-start | bytes 540680 | tf_op jit(solution)/shard_map/ppermute | solution.py:404
  22.1 7.9 %collective-permute-done.3 = bf16[64,1408]{1,0:T(8,128)(2,1)S(1)} collective-permute-done((bf16[64,1408]{1,0:T(8,128)(2,1)S(1)}, bf16[64,1408]{1,0:T(8,128)(2,1)S(1)}, u32[]{:S(2)}, u32[]{:S(2)}) %collective-permute-start.3) | collective-permute-done | bytes 180256 | tf_op jit(solution)/shard_map/ppermute | solution.py:404
  30.0 0.8 collective-permute-start.4
  30.9 0.8 copy.44.a_3_.a_8_
  31.7 0.8 copy.45.a_4_.a_9_
  35.1 1.6 collective-permute-start.11
  36.7 1.6 collective-permute-start.12
  38.3 1.3 collective-permute-done.4
  39.6 1.6 collective-permute-start.9
  42.5 3.3 %collective-permute-start.5 = (bf16[64,1024]{1,0:T(8,128)(2,1)S(1)}, bf16[64,1024]{1,0:T(8,128)(2,1)S(1)}, u32[]{:S(2)}, u32[]{:S(2)}) collective-permute-start(bf16[64,1024]{1,0:T(8,128)(2,1)S(1)} %copy-done.2), channel_id=1, source_target_pairs={{0,16},{2,18},{4,20},{6,22},{8,24},{10,26},{12,28},{14,30},{16,0},... | collective-permute-start | bytes 393224 | tf_op jit(solution)/shard_map/ppermute | solution.py:404
  45.8 0.8 constant_dynamic-update-slice_fusion.5
  46.6 4.9 %collective-permute-done.5 = bf16[64,1024]{1,0:T(8,128)(2,1)S(1)} collective-permute-done((bf16[64,1024]{1,0:T(8,128)(2,1)S(1)}, bf16[64,1024]{1,0:T(8,128)(2,1)S(1)}, u32[]{:S(2)}, u32[]{:S(2)}) %collective-permute-start.5) | collective-permute-done | bytes 131104 | tf_op jit(solution)/shard_map/ppermute | solution.py:404
  51.4 0.8 collective-permute-start.6
  52.2 13.2 %collective-permute-done.9 = bf16[256,1408]{1,0:T(8,128)(2,1)S(1)} collective-permute-done((bf16[256,1408]{1,0:T(8,128)(2,1)S(1)}, bf16[256,1408]{1,0:T(8,128)(2,1)S(1)}, u32[]{:S(2)}, u32[]{:S(2)}) %collective-permute-start.9) | collective-permute-done | bytes 720928 | tf_op jit(solution)/shard_map/ppermute | solution.py:404
  65.5 1.0 constant_dynamic-update-slice_fusion.4.a_1_.w1a
  67.2 1.6 collective-permute-start.7
  68.9 12.2 %collective-permute-done.7 = bf16[256,1024]{1,0:T(8,128)(2,1)S(1)} collective-permute-done((bf16[256,1024]{1,0:T(8,128)(2,1)S(1)}, bf16[256,1024]{1,0:T(8,128)(2,1)S(1)}, u32[]{:S(2)}, u32[]{:S(2)}) %collective-permute-start.7) | collective-permute-done | bytes 524320 | tf_op jit(solution)/shard_map/ppermute | solution.py:404
  81.2 1.0 pad_maximum_fusion.2.a_0_.nrm
  82.2 0.8 pad_maximum_fusion.4.cot.a_5_
  83.0 3.4 %shard_map.299.dm_r.a_2_ = f32[256,1024]{1,0:T(8,128)} custom-call(bf16[256,1024]{1,0:T(8,128)(2,1)} %pad_maximum_fusion.4.cot.a_5_, bf16[512,1024]{1,0:T(8,128)(2,1)} %copy-done.5, bf16[512,1024]{1,0:T(8,128)(2,1)} %collective-permute-done.13.outb.a_7_, f32[256,1]{1,0:T(8,128)} %fusion.3.live.a_4_), custom_call_target="tpu_custom_call" | custom-call | flops 2700000000 | bytes 9000000 | tf_op jit(solution)/shard_map/pallas_call | solution.py:30
  86.5 1.1 copy-done.21
  87.6 6.5 %shard_map.298 = (f32[256,1024]{1,0:T(8,128)}, f32[256,1024]{1,0:T(8,128)}, f32[256,1024]{1,0:T(8,128)}, f32[256,256]{1,0:T(8,128)}, f32[256,256]{1,0:T(8,128)}, /*index=5*/f32[256,128]{1,0:T(8,128)}) custom-call(bf16[256,1024]{1,0:T(8,128)(2,1)} %pad_maximum_fusion.2.a_0_.nrm, bf16[512,1408]{1,0:T(8,128)(2,1)} %constant_dynamic-update-slice_fusion.4.a_1_.w1a, ...), custom_call_target="tpu_custom_call" | custom-call | flops 6300000256 | bytes 21000000 | tf_op jit(solution)/shard_map/pallas_call | solution.py:30
  94.1 1.0 copy-done.22
  95.1 4.8 %shard_map.300 = (f32[256,1024]{1,0:T(8,128)}, f32[256,1024]{1,0:T(8,128)}, f32[16,256]{1,0:T(8,128)}) custom-call(bf16[256,1024]{1,0:T(8,128)(2,1)} %pad_maximum_fusion.2.a_0_.nrm, bf16[512,1024]{1,0:T(8,128)(2,1)} %copy-done.15, bf16[512,1024]{1,0:T(8,128)(2,1)} %copy-done.22, f32[256,1024]{1,0:T(8,128)} %get-tuple-element.48.y_r.a_4_, ...), custom_call_target="tpu_custom_call" | custom-call | flops 4499999744 | bytes 15000000 | tf_op jit(solution)/shard_map/pallas_call | solution.py:30
  100.4 3.4 %collective-permute-done.14.a_2_.a_9_ = f32[16,256]{1,0:T(8,128)S(1)} collective-permute-done((f32[16,256]{1,0:T(8,128)}, f32[16,256]{1,0:T(8,128)S(1)}, u32[]{:S(2)}, u32[]{:S(2)}) %collective-permute-start.14) | collective-permute-done | bytes 16416 | tf_op jit(solution)/shard_map/ppermute | solution.py:407
  104.4 4.9 %shard_map.301 = (f32[256,1024]{1,0:T(8,128)}, bf16[512,1024]{1,0:T(8,128)(2,1)}, bf16[512,1024]{1,0:T(8,128)(2,1)}) custom-call(f32[256,1024]{1,0:T(8,128)} %get-tuple-element.52.a_0_.a_1_, f32[16,256]{1,0:T(8,128)} %get-tuple-element.53.a_1_.a_8_, f32[16,256]{1,0:T(8,128)} %copy-done.24, f32[1,1024]{1,0:T(1,128)} %bitcast.56, f32[256,1]{1,0:T(8,128)} %fusion.3.live.a_4_, ...), custom_call_target="tpu_custom_call" | custom-call | flops 3600000000 | bytes 12000000 | tf_op jit(solution)/shard_map/pallas_call | solution.py:30
  109.3 5.6 %shard_map.303 = (bf16[256,1024]{1,0:T(8,128)(2,1)}, f32[256,1024]{1,0:T(8,128)}, f32[1,1024]{1,0:T(1,128)}, bf16[512,1024]{1,0:T(8,128)(2,1)}, bf16[512,1024]{1,0:T(8,128)(2,1)}) custom-call(bf16[256,1024]{1,0:T(8,128)(2,1)} %pad_maximum_fusion.2.a_0_.nrm, f32[256,1024]{1,0:T(8,128)} %get-tuple-element.52.a_0_.a_1_, f32[256,1024]{1,0:T(8,128)} %shard_map.299.dm_r.a_2_, ...), custom_call_target="tpu_custom_call" | custom-call | flops 5400000000 | bytes 18000000 | tf_op jit(solution)/shard_map/pallas_call | solution.py:30
  115.0 13.5 %shard_map.304 = (bf16[256,1408]{1,0:T(8,128)(2,1)}, f32[16,1024]{1,0:T(8,128)}, bf16[512,1408]{1,0:T(8,128)(2,1)}, bf16[512,1408]{1,0:T(8,128)(2,1)}) custom-call(bf16[256,1024]{1,0:T(8,128)(2,1)} %pad_maximum_fusion.2.a_0_.nrm, f32[256,1024]{1,0:T(8,128)} %get-tuple-element.59.a_1_, f32[256,1024]{1,0:T(8,128)} %get-tuple-element.60.a_2_, ...), custom_call_target="tpu_custom_call" | custom-call | flops 12600000512 | bytes 42000000 | tf_op jit(solution)/shard_map/pallas_call | solution.py:30
  128.5 5.3 %shard_map.305 = f32[256,1024]{1,0:T(8,128)} custom-call(bf16[256,1024]{1,0:T(8,128)(2,1)} %get-tuple-element.58.dz, bf16[512,1024]{1,0:T(8,128)(2,1)} %copy-done.15, bf16[512,1024]{1,0:T(8,128)(2,1)} %copy-done.22, bf16[256,1408]{1,0:T(8,128)(2,1)} %get-tuple-element.64.dx, bf16[512,1408]{1,0:T(8,128)(2,1)} %constant_dynamic-update-slice_fusion.4.a_1_.w1a, ...), custom_call_target="tpu_custom_call" | custom-call | flops 4950000128 | bytes 16500000 | tf_op jit(solution)/shard_map/pallas_call | solution.py:30
  133.8 1.2 dynamic-slice_convert_fusion
  135.6 1.9 constant_dynamic-slice_fusion.own
  138.2 1.6 collective-permute-start.15
  139.8 4.4 %collective-permute-done.16.other = bf16[128,1024]{1,0:T(8,128)(2,1)S(1)} collective-permute-done((bf16[128,1024]{1,0:T(8,128)(2,1)S(1)}, bf16[128,1024]{1,0:T(8,128)(2,1)S(1)}, u32[]{:S(2)}, u32[]{:S(2)}) %collective-permute-start.16) | collective-permute-done | bytes 262176 | tf_op jit(solution)/shard_map/ppermute | solution.py:407
  144.9 4.6 %shard_map.306 = (f32[128,1024]{1,0:T(8,128)}, f32[1,1024]{1,0:T(1,128)}) custom-call(f32[128,1024]{1,0:T(8,128)} %res.5, f32[128,1024]{1,0:T(8,128)} %cot.3, f32[1,1024]{1,0:T(1,128)} %bitcast.59, f32[128,1024]{1,0:T(8,128)} %constant_dynamic-slice_fusion.own, bf16[128,1024]{1,0:T(8,128)(2,1)} %copy-done.23, bf16[1024,1024]{1,0:T(8,128)(2,1)} %fusion.place), custom_call_target="tpu_custom_call" | custom-call | flops 3600000000 | bytes 12000000 | tf_op jit(solution)/shard_map/pallas_call | solution.py:30
  152.2 1.5 collective-permute-start.18
  153.7 3.1 %collective-permute-done.18 = f32[16,1024]{1,0:T(8,128)} collective-permute-done((f32[16,1024]{1,0:T(8,128)}, f32[16,1024]{1,0:T(8,128)}, u32[]{:S(2)}, u32[]{:S(2)}) %collective-permute-start.18) | collective-permute-done | bytes 65568 | tf_op jit(solution)/shard_map/ppermute | solution.py:404
  156.8 0.9 add.134
  158.1 0.8 constant_dynamic-slice_fusion.1.own
  159.0 3.0 %collective-permute-done.19 = f32[16,1024]{1,0:T(8,128)S(1)} collective-permute-done((f32[16,1024]{1,0:T(8,128)S(1)}, f32[16,1024]{1,0:T(8,128)S(1)}, u32[]{:S(2)}, u32[]{:S(2)}) %collective-permute-start.19) | collective-permute-done | bytes 65568 | tf_op jit(solution)/shard_map/ppermute | solution.py:404
  162.6 3.5 %collective-permute-start.20 = (f32[16,1024]{1,0:T(8,128)}, f32[16,1024]{1,0:T(8,128)}, u32[]{:S(2)}, u32[]{:S(2)}) collective-permute-start(f32[16,1024]{1,0:T(8,128)} %add.135), channel_id=1, source_target_pairs={{0,16},{2,18},{4,20},{6,22},{8,24},{10,26},{12,28},{14,30},{16,0},... | collective-permute-start | bytes 196616 | tf_op jit(solution)/shard_map/ppermute | solution.py:404
  166.2 4.5 %shard_map.302 = f32[128,1024]{1,0:T(8,128)} custom-call(f32[128,1024]{1,0:T(8,128)} %res.5, f32[128,1024]{1,0:T(8,128)} %constant_dynamic-slice_fusion.1.own, bf16[128,1024]{1,0:T(8,128)(2,1)} %collective-permute-done.15.other, bf16[1024,1024]{1,0:T(8,128)(2,1)} %fusion.place), custom_call_target="tpu_custom_call" | custom-call | flops 2249999872 | bytes 7500000 | tf_op jit(solution)/shard_map/pallas_call | solution.py:30
  170.7 0.9 add.136
  174.6 1.2 slice_bitcast_fusion
  176.3 1.6 collective-permute-start.32
  177.9 1.7 add_convert_fusion.5
  179.6 0.8 collective-permute-start.23
  180.7 1.3 collective-permute-start.27
  182.1 0.8 slice_add_fusion
  184.6 6.5 %collective-permute-done.32 = bf16[256,1024]{1,0:T(8,128)(2,1)S(1)} collective-permute-done((bf16[256,1024]{1,0:T(8,128)(2,1)S(1)}, bf16[256,1024]{1,0:T(8,128)(2,1)S(1)}, u32[]{:S(2)}, u32[]{:S(2)}) %collective-permute-start.32) | collective-permute-done | bytes 524320 | tf_op jit(solution)/shard_map/ppermute | solution.py:404
  191.6 10.8 %collective-permute-done.23 = bf16[256,1024]{1,0:T(8,128)(2,1)S(1)} collective-permute-done((bf16[256,1024]{1,0:T(8,128)(2,1)S(1)}, bf16[256,1024]{1,0:T(8,128)(2,1)S(1)}, u32[]{:S(2)}, u32[]{:S(2)}) %collective-permute-start.23) | collective-permute-done | bytes 524320 | tf_op jit(solution)/shard_map/ppermute | solution.py:404
  202.8 11.2 %collective-permute-done.27 = bf16[256,1408]{1,0:T(8,128)(2,1)S(1)} collective-permute-done((bf16[256,1408]{1,0:T(8,128)(2,1)S(1)}, bf16[256,1408]{1,0:T(8,128)(2,1)S(1)}, u32[]{:S(2)}, u32[]{:S(2)}) %collective-permute-start.27) | collective-permute-done | bytes 720928 | tf_op jit(solution)/shard_map/ppermute | solution.py:404
  215.1 2.6 %collective-permute-start.25 = (bf16[64,1024]{1,0:T(8,128)(2,1)S(1)}, bf16[64,1024]{1,0:T(8,128)(2,1)S(1)}, u32[]{:S(2)}, u32[]{:S(2)}) collective-permute-start(bf16[64,1024]{1,0:T(8,128)(2,1)S(1)} %add_convert_fusion.16), channel_id=1, source_target_pairs={{0,16},{2,18},{4,20},{6,22},{8,24},{10,26},{12,28},{14,30},{16,0},... | collective-permute-start | bytes 393224 | tf_op jit(solution)/shard_map/ppermute | solution.py:404
  217.7 8.8 %collective-permute-done.28 = bf16[128,1408]{1,0:T(8,128)(2,1)S(1)} collective-permute-done((bf16[128,1408]{1,0:T(8,128)(2,1)S(1)}, bf16[128,1408]{1,0:T(8,128)(2,1)S(1)}, u32[]{:S(2)}, u32[]{:S(2)}) %collective-permute-start.28) | collective-permute-done | bytes 360480 | tf_op jit(solution)/shard_map/ppermute | solution.py:404
  226.7 0.8 add_bitcast_fusion
  227.4 6.8 %collective-permute-done.29 = bf16[64,1408]{1,0:T(8,128)(2,1)S(1)} collective-permute-done((bf16[64,1408]{1,0:T(8,128)(2,1)S(1)}, bf16[64,1408]{1,0:T(8,128)(2,1)S(1)}, u32[]{:S(2)}, u32[]{:S(2)}) %collective-permute-start.29) | collective-permute-done | bytes 180256 | tf_op jit(solution)/shard_map/ppermute | solution.py:404
  234.4 1.5 collective-permute-start.30
  235.9 0.8 convert_add_fusion.1
  (137 shorter events, 21.7 us)
Async XLA Ops:
  0.6 10.7 %copy-start.1 = (bf16[1024,64]{0,1:T(8,128)(2,1)S(1)}, bf16[1024,64]{0,1:T(8,128)(2,1)}, u32[]{:S(2)}) copy-start(bf16[1024,64]{0,1:T(8,128)(2,1)} %param.34) | copy-start | bytes 393220
  0.7 10.6 %collective-permute-start.1 = (bf16[64,1024]{1,0:T(8,128)(2,1)}, bf16[64,1024]{1,0:T(8,128)(2,1)S(1)}, u32[]{:S(2)}, u32[]{:S(2)}) collective-permute-start(bf16[64,1024]{1,0:T(8,128)(2,1)} %bitcast.35), channel_id=1, source_target_pairs={{0,16},{2,18},{4,20},{6,22},{8,24},{10,26},{12,28},{14,30},{16,0},... | collective-permute-start | bytes 393224 | tf_op jit(solution)/shard_map/ppermute | solution.py:404
  11.3 7.5 %collective-permute-start.2 = (bf16[128,1024]{1,0:T(8,128)(2,1)S(1)}, bf16[128,1024]{1,0:T(8,128)(2,1)S(1)}, u32[]{:S(2)}, u32[]{:S(2)}) collective-permute-start(bf16[128,1024]{1,0:T(8,128)(2,1)S(1)} %pad_maximum_fusion.7), channel_id=1, source_target_pairs={{0,8},{2,10},{4,12},{6,14},{8,0},{10,2},{12,4},{14,6},{16,24},{18,... | collective-permute-start | bytes 786440 | tf_op jit(solution)/shard_map/ppermute | solution.py:404
  12.2 5.1 %copy-start.16 = (bf16[64,16]{0,1:T(8,128)(2,1)S(1)}, bf16[64,16]{0,1:T(8,128)(2,1)}, u32[]{:S(2)}) copy-start(bf16[64,16]{0,1:T(8,128)(2,1)} %param.25) | copy-start | bytes 6148
  12.2 5.2 %copy-start.12 = (bf16[64,1024]{1,0:T(8,128)(2,1)S(1)}, bf16[64,1024]{1,0:T(8,128)(2,1)}, u32[]{:S(2)}) copy-start(bf16[64,1024]{1,0:T(8,128)(2,1)} %param.23) | copy-start | bytes 393220
  12.2 5.2 %copy-start.13 = (bf16[64,256]{1,0:T(8,128)(2,1)S(1)}, bf16[64,256]{1,0:T(8,128)(2,1)}, u32[]{:S(2)}) copy-start(bf16[64,256]{1,0:T(8,128)(2,1)} %param.24) | copy-start | bytes 98308
  12.2 9.8 %copy-start.14 = (s32[256]{0:T(256)S(1)}, s32[256]{0:T(256)}, u32[]{:S(2)}) copy-start(s32[256]{0:T(256)} %param.19) | copy-start | bytes 3076
  12.2 20.9 %copy-start.18 = (f32[16]{0:T(128)S(1)}, f32[16]{0:T(128)}, u32[]{:S(2)}) copy-start(f32[16]{0:T(128)} %param.32) | copy-start | bytes 196
  12.2 21.7 %copy-start.19 = (f32[16]{0:T(128)S(1)}, f32[16]{0:T(128)}, u32[]{:S(2)}) copy-start(f32[16]{0:T(128)} %param.31) | copy-start | bytes 196
  12.3 21.6 %copy-start.20 = (f32[16]{0:T(128)S(1)}, f32[16]{0:T(128)}, u32[]{:S(2)}) copy-start(f32[16]{0:T(128)} %param.30) | copy-start | bytes 196
  15.8 19.3 %copy-start.10 = (bf16[128,1024]{1,0:T(8,128)(2,1)S(1)}, bf16[128,1024]{1,0:T(8,128)(2,1)}, u32[]{:S(2)}) copy-start(bf16[128,1024]{1,0:T(8,128)(2,1)} %get-tuple-element.51) | copy-start | bytes 786436
  15.8 19.3 %collective-permute-start = (bf16[128,1024]{1,0:T(8,128)(2,1)}, bf16[128,1024]{1,0:T(8,128)(2,1)S(1)}, u32[]{:S(2)}, u32[]{:S(2)}) collective-permute-start(bf16[128,1024]{1,0:T(8,128)(2,1)} %get-tuple-element.45), channel_id=1, source_target_pairs={{0,1},{1,0},{2,3},{3,2},{4,5},{5,4},{6,7},{7,6},{8,9},{9,8},{10,11... | collective-permute-start | bytes 786440 | tf_op jit(solution)/shard_map/ppermute | solution.py:407
  18.9 11.1 %collective-permute-start.3 = (bf16[64,1408]{1,0:T(8,128)(2,1)S(1)}, bf16[64,1408]{1,0:T(8,128)(2,1)S(1)}, u32[]{:S(2)}, u32[]{:S(2)}) collective-permute-start(bf16[64,1408]{1,0:T(8,128)(2,1)S(1)} %fusion.2), channel_id=1, source_target_pairs={{0,16},{2,18},{4,20},{6,22},{8,24},{10,26},{12,28},{14,30},{16,0},... | collective-permute-start | bytes 540680 | tf_op jit(solution)/shard_map/ppermute | solution.py:404
  30.0 9.5 %collective-permute-start.4 = (bf16[128,1408]{1,0:T(8,128)(2,1)S(1)}, bf16[128,1408]{1,0:T(8,128)(2,1)S(1)}, u32[]{:S(2)}, u32[]{:S(2)}) collective-permute-start(bf16[128,1408]{1,0:T(8,128)(2,1)S(1)} %pad_maximum_fusion.6), channel_id=1, source_target_pairs={{0,8},{2,10},{4,12},{6,14},{8,0},{10,2},{12,4},{14,6},{16,24},{18,... | collective-permute-start | bytes 1081352 | tf_op jit(solution)/shard_map/ppermute | solution.py:404
  35.1 7.5 %copy-start.2 = (bf16[64,1024]{1,0:T(8,128)(2,1)S(1)}, bf16[64,1024]{1,0:T(8,128)(2,1)}, u32[]{:S(2)}) copy-start(bf16[64,1024]{1,0:T(8,128)(2,1)} %param.22) | copy-start | bytes 393220
  35.1 33.7 %collective-permute-start.11 = (bf16[128,1024]{1,0:T(8,128)(2,1)S(1)}, bf16[128,1024]{1,0:T(8,128)(2,1)S(1)}, u32[]{:S(2)}, u32[]{:S(2)}) collective-permute-start(bf16[128,1024]{1,0:T(8,128)(2,1)S(1)} %copy-done.10), channel_id=1, source_target_pairs={{0,1},{1,0},{2,3},{3,2},{4,5},{5,4},{6,7},{7,6},{8,9},{9,8},{10,11... | collective-permute-start | bytes 786440 | tf_op jit(solution)/shard_map/ppermute | solution.py:407
  36.7 29.8 %collective-permute-start.12 = (bf16[256,1024]{1,0:T(8,128)(2,1)S(1)}, bf16[256,1024]{1,0:T(8,128)(2,1)S(1)}, u32[]{:S(2)}, u32[]{:S(2)}) collective-permute-start(bf16[256,1024]{1,0:T(8,128)(2,1)S(1)} %pad_maximum_fusion.5), channel_id=1, source_target_pairs={{0,4},{2,6},{4,0},{6,2},{8,12},{10,14},{12,8},{14,10},{16,20},{18,... | collective-permute-start | bytes 1572872 | tf_op jit(solution)/shard_map/ppermute | solution.py:404
  39.6 25.9 %collective-permute-start.9 = (bf16[256,1408]{1,0:T(8,128)(2,1)S(1)}, bf16[256,1408]{1,0:T(8,128)(2,1)S(1)}, u32[]{:S(2)}, u32[]{:S(2)}) collective-permute-start(bf16[256,1408]{1,0:T(8,128)(2,1)S(1)} %pad_maximum_fusion.1), channel_id=1, source_target_pairs={{0,4},{2,6},{4,0},{6,2},{8,12},{10,14},{12,8},{14,10},{16,20},{18,... | collective-permute-start | bytes 2162696 | tf_op jit(solution)/shard_map/ppermute | solution.py:404
  42.5 8.9 %collective-permute-start.5 = (bf16[64,1024]{1,0:T(8,128)(2,1)S(1)}, bf16[64,1024]{1,0:T(8,128)(2,1)S(1)}, u32[]{:S(2)}, u32[]{:S(2)}) collective-permute-start(bf16[64,1024]{1,0:T(8,128)(2,1)S(1)} %copy-done.2), channel_id=1, source_target_pairs={{0,16},{2,18},{4,20},{6,22},{8,24},{10,26},{12,28},{14,30},{16,0},... | collective-permute-start | bytes 393224 | tf_op jit(solution)/shard_map/ppermute | solution.py:404
  51.4 15.7 %collective-permute-start.6 = (bf16[128,1024]{1,0:T(8,128)(2,1)S(1)}, bf16[128,1024]{1,0:T(8,128)(2,1)S(1)}, u32[]{:S(2)}, u32[]{:S(2)}) collective-permute-start(bf16[128,1024]{1,0:T(8,128)(2,1)S(1)} %pad_maximum_fusion.8), channel_id=1, source_target_pairs={{0,8},{2,10},{4,12},{6,14},{8,0},{10,2},{12,4},{14,6},{16,24},{18,... | collective-permute-start | bytes 786440 | tf_op jit(solution)/shard_map/ppermute | solution.py:404
  66.5 2.3 copy-start.9
  66.5 20.0 %collective-permute-start.10 = (bf16[512,1408]{1,0:T(8,128)(2,1)}, bf16[512,1408]{1,0:T(8,128)(2,1)S(1)}, u32[]{:S(2)}, u32[]{:S(2)}) collective-permute-start(bf16[512,1408]{1,0:T(8,128)(2,1)} %constant_dynamic-update-slice_fusion.4.a_1_.w1a), channel_id=1, source_target_pairs={{0,2},{2,0},{4,6},{6,4},{8,10},{10,8},{12,14},{14,12},{16,18},{18,... | collective-permute-start | bytes 4325384 | tf_op jit(solution)/shard_map/ppermute | solution.py:404
  66.5 2.3 copy-start.5
  66.6 16.5 %collective-permute-start.13 = (bf16[512,1024]{1,0:T(8,128)(2,1)S(1)}, bf16[512,1024]{1,0:T(8,128)(2,1)}, u32[]{:S(2)}, u32[]{:S(2)}) collective-permute-start(bf16[512,1024]{1,0:T(8,128)(2,1)S(1)} %pad_maximum_fusion.outa.a_6_), channel_id=1, source_target_pairs={{0,2},{2,0},{4,6},{6,4},{8,10},{10,8},{12,14},{14,12},{16,18},{18,... | collective-permute-start | bytes 3145736 | tf_op jit(solution)/shard_map/ppermute | solution.py:404
  67.2 13.9 %collective-permute-start.7 = (bf16[256,1024]{1,0:T(8,128)(2,1)S(1)}, bf16[256,1024]{1,0:T(8,128)(2,1)S(1)}, u32[]{:S(2)}, u32[]{:S(2)}) collective-permute-start(bf16[256,1024]{1,0:T(8,128)(2,1)S(1)} %pad_maximum_fusion.3), channel_id=1, source_target_pairs={{0,4},{2,6},{4,0},{6,2},{8,12},{10,14},{12,8},{14,10},{16,20},{18,... | collective-permute-start | bytes 1572872 | tf_op jit(solution)/shard_map/ppermute | solution.py:404
  81.1 5.3 %copy-start.15 = (bf16[512,1024]{1,0:T(8,128)(2,1)}, bf16[512,1024]{1,0:T(8,128)(2,1)S(1)}, u32[]{:S(2)}) copy-start(bf16[512,1024]{1,0:T(8,128)(2,1)S(1)} %constant_dynamic-update-slice_fusion.wza) | copy-start | bytes 3145732
  81.1 12.9 %collective-permute-start.8 = (bf16[512,1024]{1,0:T(8,128)(2,1)S(1)}, bf16[512,1024]{1,0:T(8,128)(2,1)S(1)}, u32[]{:S(2)}, u32[]{:S(2)}) collective-permute-start(bf16[512,1024]{1,0:T(8,128)(2,1)S(1)} %constant_dynamic-update-slice_fusion.wza), channel_id=1, source_target_pairs={{0,2},{2,0},{4,6},{6,4},{8,10},{10,8},{12,14},{14,12},{16,18},{18,... | collective-permute-start | bytes 3145736 | tf_op jit(solution)/shard_map/ppermute | solution.py:404
  86.5 1.1 copy-start.21
  94.1 1.0 copy-start.22
  99.8 3.9 %collective-permute-start.14 = (f32[16,256]{1,0:T(8,128)}, f32[16,256]{1,0:T(8,128)S(1)}, u32[]{:S(2)}, u32[]{:S(2)}) collective-permute-start(f32[16,256]{1,0:T(8,128)} %get-tuple-element.53.a_1_.a_8_), channel_id=1, source_target_pairs={{0,1},{1,0},{2,3},{3,2},{4,5},{5,4},{6,7},{7,6},{8,9},{9,8},{10,11... | collective-permute-start | bytes 49160 | tf_op jit(solution)/shard_map/ppermute | solution.py:407
  103.8 0.6 copy-start.24
  109.3 66.6 %collective-permute-start.31 = (bf16[512,1024]{1,0:T(8,128)(2,1)}, bf16[512,1024]{1,0:T(8,128)(2,1)S(1)}, u32[]{:S(2)}, u32[]{:S(2)}) collective-permute-start(bf16[512,1024]{1,0:T(8,128)(2,1)} %get-tuple-element.55), channel_id=1, source_target_pairs={{0,2},{2,0},{4,6},{6,4},{8,10},{10,8},{12,14},{14,12},{16,18},{18,... | collective-permute-start | bytes 3145736 | tf_op jit(solution)/shard_map/ppermute | solution.py:404
  133.8 3.7 %copy-start.6 = (f32[256,1024]{1,0:T(8,128)S(1)}, f32[256,1024]{1,0:T(8,128)}, u32[]{:S(2)}) copy-start(f32[256,1024]{1,0:T(8,128)} %get-tuple-element.54) | copy-start | bytes 3145732
  133.8 4.4 %copy-start.11 = (f32[16,1024]{1,0:T(8,128)S(1)}, f32[16,1024]{1,0:T(8,128)}, u32[]{:S(2)}) copy-start(f32[16,1024]{1,0:T(8,128)} %get-tuple-element.66) | copy-start | bytes 196612
  135.0 9.2 %collective-permute-start.16 = (bf16[128,1024]{1,0:T(8,128)(2,1)S(1)}, bf16[128,1024]{1,0:T(8,128)(2,1)S(1)}, u32[]{:S(2)}, u32[]{:S(2)}) collective-permute-start(bf16[128,1024]{1,0:T(8,128)(2,1)S(1)} %dynamic-slice_convert_fusion), channel_id=1, source_target_pairs={{0,1},{1,0},{2,3},{3,2},{4,5},{5,4},{6,7},{7,6},{8,9},{9,8},{10,11... | collective-permute-start | bytes 786440 | tf_op jit(solution)/shard_map/ppermute | solution.py:407
  138.2 27.9 %collective-permute-start.15 = (bf16[128,1024]{1,0:T(8,128)(2,1)}, bf16[128,1024]{1,0:T(8,128)(2,1)}, u32[]{:S(2)}, u32[]{:S(2)}) collective-permute-start(bf16[128,1024]{1,0:T(8,128)(2,1)} %dynamic-slice_convert_fusion.1), channel_id=1, source_target_pairs={{0,1},{1,0},{2,3},{3,2},{4,5},{5,4},{6,7},{7,6},{8,9},{9,8},{10,11... | collective-permute-start | bytes 786440 | tf_op jit(solution)/shard_map/ppermute | solution.py:407
  139.8 9.7 %copy-start.17 = (f32[1,1024]{1,0:T(1,128)S(1)}, f32[1,1024]{1,0:T(1,128)}, u32[]{:S(2)}) copy-start(f32[1,1024]{1,0:T(1,128)} %get-tuple-element.67) | copy-start | bytes 12292
  144.2 0.7 copy-start.23
  150.3 1.3 collective-permute-start.17
  150.3 30.1 %collective-permute-start.26 = (bf16[512,1408]{1,0:T(8,128)(2,1)}, bf16[512,1408]{1,0:T(8,128)(2,1)S(1)}, u32[]{:S(2)}, u32[]{:S(2)}) collective-permute-start(bf16[512,1408]{1,0:T(8,128)(2,1)} %get-tuple-element.72), channel_id=1, source_target_pairs={{0,2},{2,0},{4,6},{6,4},{8,10},{10,8},{12,14},{14,12},{16,18},{18,... | collective-permute-start | bytes 4325384 | tf_op jit(solution)/shard_map/ppermute | solution.py:404
  152.2 4.6 %collective-permute-start.18 = (f32[16,1024]{1,0:T(8,128)}, f32[16,1024]{1,0:T(8,128)}, u32[]{:S(2)}, u32[]{:S(2)}) collective-permute-start(f32[16,1024]{1,0:T(8,128)} %add.133), channel_id=1, source_target_pairs={{0,4},{2,6},{4,0},{6,2},{8,12},{10,14},{12,8},{14,10},{16,20},{18,... | collective-permute-start | bytes 196616 | tf_op jit(solution)/shard_map/ppermute | solution.py:404
  153.7 24.1 %collective-permute-start.22 = (bf16[512,1024]{1,0:T(8,128)(2,1)}, bf16[512,1024]{1,0:T(8,128)(2,1)}, u32[]{:S(2)}, u32[]{:S(2)}) collective-permute-start(bf16[512,1024]{1,0:T(8,128)(2,1)} %get-tuple-element.70), channel_id=1, source_target_pairs={{0,2},{2,0},{4,6},{6,4},{8,10},{10,8},{12,14},{14,12},{16,18},{18,... | collective-permute-start | bytes 3145736 | tf_op jit(solution)/shard_map/ppermute | solution.py:404
  157.7 4.3 %collective-permute-start.19 = (f32[16,1024]{1,0:T(8,128)S(1)}, f32[16,1024]{1,0:T(8,128)S(1)}, u32[]{:S(2)}, u32[]{:S(2)}) collective-permute-start(f32[16,1024]{1,0:T(8,128)S(1)} %add.134), channel_id=1, source_target_pairs={{0,8},{2,10},{4,12},{6,14},{8,0},{10,2},{12,4},{14,6},{16,24},{18,... | collective-permute-start | bytes 196616 | tf_op jit(solution)/shard_map/ppermute | solution.py:404
  162.6 13.2 %copy-start.3 = (bf16[512,1024]{1,0:T(8,128)(2,1)S(1)}, bf16[512,1024]{1,0:T(8,128)(2,1)}, u32[]{:S(2)}) copy-start(bf16[512,1024]{1,0:T(8,128)(2,1)} %get-tuple-element.73) | copy-start | bytes 3145732
  162.6 8.0 %collective-permute-start.20 = (f32[16,1024]{1,0:T(8,128)}, f32[16,1024]{1,0:T(8,128)}, u32[]{:S(2)}, u32[]{:S(2)}) collective-permute-start(f32[16,1024]{1,0:T(8,128)} %add.135), channel_id=1, source_target_pairs={{0,16},{2,18},{4,20},{6,22},{8,24},{10,26},{12,28},{14,30},{16,0},... | collective-permute-start | bytes 196616 | tf_op jit(solution)/shard_map/ppermute | solution.py:404
  171.6 1.8 copy-start.7
  172.8 9.3 %collective-permute-start.21 = (f32[8,1024]{1,0:T(8,128)}, f32[8,1024]{1,0:T(8,128)}, u32[]{:S(2)}, u32[]{:S(2)}) collective-permute-start(f32[8,1024]{1,0:T(8,128)} %slice.230), channel_id=1, source_target_pairs={{0,1},{1,0},{2,3},{3,2},{4,5},{5,4},{6,7},{7,6},{8,9},{9,8},{10,11... | collective-permute-start | bytes 98312 | tf_op jit(solution)/shard_map/ppermute | solution.py:407
  175.9 2.0 copy-start.4
  176.3 14.9 %collective-permute-start.32 = (bf16[256,1024]{1,0:T(8,128)(2,1)S(1)}, bf16[256,1024]{1,0:T(8,128)(2,1)S(1)}, u32[]{:S(2)}, u32[]{:S(2)}) collective-permute-start(bf16[256,1024]{1,0:T(8,128)(2,1)S(1)} %get-tuple-element.125), channel_id=1, source_target_pairs={{0,4},{2,6},{4,0},{6,2},{8,12},{10,14},{12,8},{14,10},{16,20},{18,... | collective-permute-start | bytes 1572872 | tf_op jit(solution)/shard_map/ppermute | solution.py:404
  177.9 2.5 %copy-start = (bf16[512,1408]{1,0:T(8,128)(2,1)S(1)}, bf16[512,1408]{1,0:T(8,128)(2,1)}, u32[]{:S(2)}) copy-start(bf16[512,1408]{1,0:T(8,128)(2,1)} %get-tuple-element.71) | copy-start | bytes 4325380
  179.6 22.8 %collective-permute-start.23 = (bf16[256,1024]{1,0:T(8,128)(2,1)S(1)}, bf16[256,1024]{1,0:T(8,128)(2,1)S(1)}, u32[]{:S(2)}, u32[]{:S(2)}) collective-permute-start(bf16[256,1024]{1,0:T(8,128)(2,1)S(1)} %get-tuple-element.127), channel_id=1, source_target_pairs={{0,4},{2,6},{4,0},{6,2},{8,12},{10,14},{12,8},{14,10},{16,20},{18,... | collective-permute-start | bytes 1572872 | tf_op jit(solution)/shard_map/ppermute | solution.py:404
  180.4 1.7 copy-start.8
  180.7 33.3 %collective-permute-start.27 = (bf16[256,1408]{1,0:T(8,128)(2,1)S(1)}, bf16[256,1408]{1,0:T(8,128)(2,1)S(1)}, u32[]{:S(2)}, u32[]{:S(2)}) collective-permute-start(bf16[256,1408]{1,0:T(8,128)(2,1)S(1)} %get-tuple-element.123), channel_id=1, source_target_pairs={{0,4},{2,6},{4,0},{6,2},{8,12},{10,14},{12,8},{14,10},{16,20},{18,... | collective-permute-start | bytes 2162696 | tf_op jit(solution)/shard_map/ppermute | solution.py:404
  191.3 23.3 %collective-permute-start.33 = (bf16[128,1024]{1,0:T(8,128)(2,1)S(1)}, bf16[128,1024]{1,0:T(8,128)(2,1)S(1)}, u32[]{:S(2)}, u32[]{:S(2)}) collective-permute-start(bf16[128,1024]{1,0:T(8,128)(2,1)S(1)} %get-tuple-element.131), channel_id=1, source_target_pairs={{0,8},{2,10},{4,12},{6,14},{8,0},{10,2},{12,4},{14,6},{16,24},{18,... | collective-permute-start | bytes 786440 | tf_op jit(solution)/shard_map/ppermute | solution.py:404
  202.6 12.5 %collective-permute-start.24 = (bf16[128,1024]{1,0:T(8,128)(2,1)S(1)}, bf16[128,1024]{1,0:T(8,128)(2,1)S(1)}, u32[]{:S(2)}, u32[]{:S(2)}) collective-permute-start(bf16[128,1024]{1,0:T(8,128)(2,1)S(1)} %get-tuple-element.133), channel_id=1, source_target_pairs={{0,8},{2,10},{4,12},{6,14},{8,0},{10,2},{12,4},{14,6},{16,24},{18,... | collective-permute-start | bytes 786440 | tf_op jit(solution)/shard_map/ppermute | solution.py:404
  214.2 12.3 %collective-permute-start.28 = (bf16[128,1408]{1,0:T(8,128)(2,1)S(1)}, bf16[128,1408]{1,0:T(8,128)(2,1)S(1)}, u32[]{:S(2)}, u32[]{:S(2)}) collective-permute-start(bf16[128,1408]{1,0:T(8,128)(2,1)S(1)} %get-tuple-element.129), channel_id=1, source_target_pairs={{0,8},{2,10},{4,12},{6,14},{8,0},{10,2},{12,4},{14,6},{16,24},{18,... | collective-permute-start | bytes 1081352 | tf_op jit(solution)/shard_map/ppermute | solution.py:404
  214.6 12.0 %collective-permute-start.34 = (bf16[64,1024]{1,0:T(8,128)(2,1)S(1)}, bf16[64,1024]{1,0:T(8,128)(2,1)S(1)}, u32[]{:S(2)}, u32[]{:S(2)}) collective-permute-start(bf16[64,1024]{1,0:T(8,128)(2,1)S(1)} %add_convert_fusion.14), channel_id=1, source_target_pairs={{0,16},{2,18},{4,20},{6,22},{8,24},{10,26},{12,28},{14,30},{16,0},... | collective-permute-start | bytes 393224 | tf_op jit(solution)/shard_map/ppermute | solution.py:404
  215.1 20.8 %collective-permute-start.25 = (bf16[64,1024]{1,0:T(8,128)(2,1)S(1)}, bf16[64,1024]{1,0:T(8,128)(2,1)S(1)}, u32[]{:S(2)}, u32[]{:S(2)}) collective-permute-start(bf16[64,1024]{1,0:T(8,128)(2,1)S(1)} %add_convert_fusion.16), channel_id=1, source_target_pairs={{0,16},{2,18},{4,20},{6,22},{8,24},{10,26},{12,28},{14,30},{16,0},... | collective-permute-start | bytes 393224 | tf_op jit(solution)/shard_map/ppermute | solution.py:404
  226.6 7.7 %collective-permute-start.29 = (bf16[64,1408]{1,0:T(8,128)(2,1)S(1)}, bf16[64,1408]{1,0:T(8,128)(2,1)S(1)}, u32[]{:S(2)}, u32[]{:S(2)}) collective-permute-start(bf16[64,1408]{1,0:T(8,128)(2,1)S(1)} %add_convert_fusion.12), channel_id=1, source_target_pairs={{0,16},{2,18},{4,20},{6,22},{8,24},{10,26},{12,28},{14,30},{16,0},... | collective-permute-start | bytes 540680 | tf_op jit(solution)/shard_map/ppermute | solution.py:404
  234.4 4.0 %collective-permute-start.30 = (f32[32,256]{1,0:T(8,128)S(1)}, f32[32,256]{1,0:T(8,128)S(1)}, u32[]{:S(2)}, u32[]{:S(2)}) collective-permute-start(f32[32,256]{1,0:T(8,128)S(1)} %dynamic-slice_bitcast_fusion), channel_id=1, source_target_pairs={{0,1},{1,0},{2,3},{3,2},{4,5},{5,4},{6,7},{7,6},{8,9},{9,8},{10,11... | collective-permute-start | bytes 98312 | tf_op jit(solution)/shard_map/ppermute | solution.py:407

commit v2 on v1

--- a/solution.py
+++ b/solution.py
@@ -8,6 +8,7 @@
 
 SPAN = 128
 LANES = 128
+VMEM = 20 * 1024 * 1024
 epsilon = 1e-05
 f32 = jnp.float32
 bf16 = jnp.bfloat16
@@ -26,14 +27,17 @@
     return lax.dot_general(a, b, (((0,), (0,)), ((), ())), precision=p, preferred_element_type=f32)
 
 
-def call(micros, body, outs, *args, scratch=()):
+def call(micros, body, outs, *args, scratch=(), scalars=0):
     return pl.pallas_call(
         body,
         out_shape=[jax.ShapeDtypeStruct(s, d) for s, d in outs],
+        in_specs=[pl.BlockSpec(memory_space=pltpu.SMEM)] * scalars
+        + [pl.BlockSpec(memory_space=pltpu.VMEM)] * (len(args) - scalars),
         scratch_shapes=list(scratch),
         cost_estimate=pl.CostEstimate(
             flops=int(micros * 9e8), transcendentals=0, bytes_accessed=int(micros * 3e6)
         ),
+        compiler_params=pltpu.CompilerParams(vmem_limit_bytes=VMEM),
     )(*args)
 
 
@@ -45,6 +49,15 @@
 def split(v):
     high = v.astype(bf16)
     return jnp.concatenate([high, (v - high.astype(f32)).astype(bf16)], 0)
+
+
+def halves(v):
+    high = v.astype(bf16)
+    return jnp.concatenate([high, (v - high.astype(f32)).astype(bf16)], 1)
+
+
+def rows_of(side, half):
+    return pl.ds(pl.multiple_of(side * half, half), half)
 
 
 def iota(shape, axis):
@@ -116,7 +129,7 @@
 
 
 def fwd_body(width, nrm, w1a, w1b, link, segc, segr, cx, cxb, cbc, cbcb, dtb, alog,
-             xpre_o, xc_o, y_o, bcpre_o, bcc_o, dt_o):
+             xpre_o, xc_o, y_o, bcpre_o, bcc_o, dt_o, dec_o):
     inner = xc_o.shape[1]
     state = bcc_o.shape[1] // 2
     x = nrm[...]
@@ -155,7 +168,9 @@
             y = None
             for i in range(per):
                 h = j * per + i
-                w = (decay(cum[k], cum_t[k], mask[k], h) * scores[k]).astype(bf16)
+                dec = decay(cum[k], cum_t[k], mask[k], h)
+                dec_o[2 * h + k] = dec
+                w = (dec * scores[k]).astype(bf16)
                 part = dot_nn(w, ub[rows])
                 y = part if y is None else jnp.where(lane >= i * width, part, y)
             if k:
@@ -200,25 +215,31 @@
     sums_o[8:] = as_rows(jnp.sum(dots, axis=1, keepdims=True))
 
 
-def mix_body(full, g_r, sums, sums2, gain, live, cot, outa, outb,
-             blk_o, keep_o, send_o, mixed):
+def mix_body(full, g_r, sums, sums2, gain, live, cot_t, keep_o, send_o, mixed):
     inv = lax.rsqrt(as_col(sums[:8] + sums2[:8]) / full + epsilon)
     wide = 2 * LANES
     for c in range(g_r.shape[1] // LANES):
         at = slice(c * LANES, (c + 1) * LANES)
         mixed[:, at] = (g_r[:, at] * inv * gain[:, at] * live[...]).astype(bf16)
-    x = cot[...]
     half = keep_o.shape[0]
     for c in range(g_r.shape[1] // wide):
         at = slice(c * wide, (c + 1) * wide)
-        send_o[:, at] = dot_tn(x[:, half:], mixed[:, at]).astype(bf16)
-        keep_o[:, at] = dot_tn(x[:, :half], mixed[:, at]).astype(bf16)
-    m = mixed[...]
-    blk_o[:, :half] = dot_nt(m, outa[...])
-    blk_o[:, half:] = dot_nt(m, outb[...])
-
-
-def dz_body(full, nrm, g_r, dm_r, z_r, y_r, xc_r, dsk, gain, sums, sums2,
+        send_o[:, at] = dot_nn(cot_t[half:], mixed[:, at]).astype(bf16)
+        keep_o[:, at] = dot_nn(cot_t[:half], mixed[:, at]).astype(bf16)
+
+
+def blk_body(side, mixed, outa, outb, own_o, other_o):
+    half = outa.shape[0]
+    count = own_o.shape[0]
+    m = mixed[rows_of(1 - side[0], count), :]
+    other_o[:, :half] = dot_nt(m, outa[...]).astype(bf16)
+    other_o[:, half:] = dot_nt(m, outb[...]).astype(bf16)
+    m = mixed[rows_of(side[0], count), :]
+    own_o[:, :half] = dot_nt(m, outa[...])
+    own_o[:, half:] = dot_nt(m, outb[...])
+
+
+def dz_body(full, nrm_t, g_r, dm_r, z_r, y_r, xc_r, dsk, gain, sums, sums2,
             dz_o, dy_o, gp_o, keep_o, send_o):
     inv = lax.rsqrt(as_col(sums[:8] + sums2[:8]) / full + epsilon)
     back = inv * inv * inv * as_col(sums[8:] + sums2[8:]) / full
@@ -233,23 +254,22 @@
         y = y_r[:, at] + dsk[:, at] * silu(xc_r[:, at])
         dz_o[:, at] = (dg * y * (s * (1.0 + z * (1.0 - s)))).astype(bf16)
         dy_o[:, at] = dg * (z * s)
-    x = nrm[...]
     half = keep_o.shape[0]
     wide = 2 * LANES
     for c in range(z_r.shape[1] // wide):
         at = slice(c * wide, (c + 1) * wide)
-        send_o[:, at] = dot_tn(x[:, half:], dz_o[:, at]).astype(bf16)
-        keep_o[:, at] = dot_tn(x[:, :half], dz_o[:, at]).astype(bf16)
-
-
-def bwd_body(width, nrm, dy_r, xpre_r, xc_r, y_r, bcpre_r, bcc_r, dt_r, link, segc, segr, cx,
+        send_o[:, at] = dot_nn(nrm_t[half:], dz_o[:, at]).astype(bf16)
+        keep_o[:, at] = dot_nn(nrm_t[:half], dz_o[:, at]).astype(bf16)
+
+
+def bwd_body(width, nrm_t, dy_r, xpre_r, xc_r, y_r, bcpre_r, bcc_r, dt_r, dec_r, link, segc, segr, cx,
              cbc, dtb, alog, dsk, dx_o, sm_o, keep_o, send_o, dc_s):
     inner = xc_r.shape[1]
     state = bcc_r.shape[1] // 2
     lk = link[...]
     bs = silu(bcc_r[:, :state])
     cs = silu(bcc_r[:, state:])
-    v, step, logd, cum, cum_t, mask, grow, coef = prepare(
+    v, step, logd, _, _, _, grow, coef = prepare(
         dt_r[...], dtb[...], alog[...], segc[...], segr[...]
     )
     scores = [
@@ -264,11 +284,12 @@
     rows_t = 2 * SPAN
     dcum = jnp.zeros((rows_t, LANES), f32)
     dstep = jnp.zeros((rows_t, LANES), f32)
+    dskip = jnp.zeros((8, LANES), f32)
     dsc = [jnp.zeros((SPAN, SPAN), f32) for _ in range(2)]
     dc1 = jnp.zeros((SPAN, state), f32)
     db0 = jnp.zeros((SPAN, state), f32)
-    fold_row = iota((LANES, LANES), 0)
-    fold_col = iota((LANES, LANES), 1)
+    fold_row = iota((2 * LANES, LANES), 0) % LANES
+    fold_col = iota((2 * LANES, LANES), 1)
     sm_o[...] = jnp.zeros(sm_o.shape, f32)
     for j in range(inner // LANES):
         at = slice(j * LANES, (j + 1) * LANES)
@@ -295,7 +316,7 @@
             du = None
             for i in range(per):
                 h = j * per + i
-                dec = decay(cum[k], cum_t[k], mask[k], h)
+                dec = dec_r[2 * h + k]
                 w = (dec * scores[k]).astype(bf16)
                 part = dot_tn(w, dyb[rows])
                 du = part if du is None else jnp.where(lane >= i * width, part, du)
@@ -314,10 +335,11 @@
             0,
         )
         du = jnp.concatenate([dus[0] + ce * under, dus[1]], 0)
-        fold = (fold_col == j * per + fold_row // width).astype(f32)
-        dcum = dcum + dot_nn(net, fold, HI)
-        dstep = dstep + dot_nn(du * xs, fold, HI)
-        sm_o[6:7, at] = jnp.sum(dy * xs, axis=0, keepdims=True)
+        fold = (fold_col == j * per + fold_row // width).astype(bf16)
+        dcum = dcum + dot_nn(halves(net), fold)
+        dstep = dstep + dot_nn(halves(du * xs), fold)
+        skip = jnp.broadcast_to(jnp.sum(dy * xs, axis=0, keepdims=True), (8, LANES))
+        dskip = dskip + dot_nn(halves(skip), fold)
         dxc = (du * se + dsk[:, at] * dy) * silu_slope(xc)
         dpre, dw, db = conv_back(dxc, xpre_r[:, at], cx[:, at], lk)
         dx_o[:, at] = dpre.astype(bf16)
@@ -330,6 +352,7 @@
     dx_o[:, inner + 2 * state :] = ddt.astype(bf16)
     sm_o[7:8, :LANES] = jnp.sum(ddt, axis=0, keepdims=True)
     sm_o[7:8, LANES : 2 * LANES] = jnp.sum(dlog * logd, axis=0, keepdims=True)
+    sm_o[7:8, 2 * LANES : 3 * LANES] = dskip[:1]
     for k in range(2):
         rows = slice(k * SPAN, (k + 1) * SPAN)
         db = dot_tn(dsc[k], cs[rows], HI)
@@ -349,27 +372,40 @@
         for k, piece in enumerate(dw):
             sm_o[8 + k : 9 + k, at] = piece
         sm_o[12:13, at] = db
-    x = nrm[...]
     wide = keep_o.shape[1]
     half = keep_o.shape[0]
     for first in range(0, wide, 2 * LANES):
         at = slice(first, min(first + 2 * LANES, wide))
-        send_o[:, at] = dot_tn(x[:, half:], dx_o[:, at]).astype(bf16)
-        keep_o[:, at] = dot_tn(x[:, :half], dx_o[:, at]).astype(bf16)
-
-
-def dn_body(dz, wza, wzb, dx, w1a, w1b, dn_o):
+        send_o[:, at] = dot_nn(nrm_t[half:], dx_o[:, at]).astype(bf16)
+        keep_o[:, at] = dot_nn(nrm_t[:half], dx_o[:, at]).astype(bf16)
+
+
+def dn_body(side, dz, wza, wzb, dx, w1a, w1b, own_o, other_o, all_s):
+    half = wza.shape[0]
+    count = own_o.shape[0]
     a = dz[...]
     b = dx[...]
-    half = wza.shape[0]
-    dn_o[:, :half] = dot_nt(a, wza[...]) + dot_nt(b, w1a[...])
-    dn_o[:, half:] = dot_nt(a, wzb[...]) + dot_nt(b, w1b[...])
-
-
-def restore(v, place):
-    high = v.astype(bf16)
-    low = (v - high.astype(f32)).astype(bf16)
-    return dot_nt(high, place) + dot_nt(low, place)
+    all_s[:, :half] = dot_nt(a, wza[...]) + dot_nt(b, w1a[...])
+    all_s[:, half:] = dot_nt(a, wzb[...]) + dot_nt(b, w1b[...])
+    other_o[...] = all_s[rows_of(1 - side[0], count), :].astype(bf16)
+    own_o[...] = all_s[rows_of(side[0], count), :]
+
+
+def last_body(side, keep, other, x_o, dt_o, own_o, send_o, all_s):
+    inner = x_o.shape[1]
+    count, two_state = own_o.shape
+    x_o[...] = keep[:, :inner].astype(f32) + other[:, :inner].astype(f32)
+    all_s[...] = keep[:, inner:].astype(f32) + other[:, inner:].astype(f32)
+    dt_o[...] = all_s[:, two_state : two_state + dt_o.shape[1]]
+    low = all_s[:count, :two_state]
+    top = all_s[count:, :two_state]
+    own_o[...] = jnp.where(side[0] == 0, low, top)
+    send_o[...] = jnp.where(side[0] == 0, top, low)
+
+
+def restore(v, place_t):
+    both = dot_nn(split(v), place_t)
+    return both[: v.shape[0]] + both[v.shape[0] :]
 
 
 def block_body(res, own, other, place, out_o):
@@ -386,6 +422,19 @@
     ig_o[...] = cot[...] + inv * dg - r * (inv * inv * inv * inner)
 
 
+def join_body(side, own, other, all_o, turned_o):
+    half = own.shape[0]
+    all_o[rows_of(side[0], half), :] = own[...]
+    all_o[rows_of(1 - side[0], half), :] = other[...]
+    turned_o[...] = all_o[...].T
+
+
+def cat_body(first, second, out_o):
+    half = first.shape[0]
+    out_o[:half] = first[...]
+    out_o[half:] = second[...]
+
+
 def head_body(res, cot, gain, place, nrm_o, cot_o):
     r = res[...]
     inv = lax.rsqrt(jnp.mean(r * r, axis=1, keepdims=True) + epsilon)
@@ -417,19 +466,30 @@
             r = swap(v, bit)
             marks.append(r)
             if bit > 1:
-                v = jnp.concatenate([v, r], 0)
+                (v,) = call(0.5, cat_body, [((2 * v.shape[0], v.shape[1]), bf16)], v, r)
         return v, r, marks
 
     def plus(a, b):
         return a.astype(f32) + b.astype(f32)
 
-    def scatter(keep, send):
-        for bit in bits[:-1]:
-            r = swap(send, bit)
-            half = keep.shape[0] // 2
-            send = plus(keep[half:], r[half:]).astype(bf16)
-            keep = plus(keep[:half], r[:half]).astype(bf16)
-        return plus(keep, swap(send, bits[-1]))
+    near = list(range(1, len(bits)))
+
+    far = near[1:] + near[:1]
+
+    def scatter(keep, send, order):
+        shape = (2,) * (len(bits) - 1) + (keep.shape[0] >> (len(bits) - 1), keep.shape[1])
+        left = list(near)
+        keep = keep.reshape(shape)
+        r = swap(send, bits[0]).reshape(shape)
+        for which in order:
+            axis = left.index(which)
+            left.pop(axis)
+            pick = [[lax.index_in_dim(v, side, axis, False) for v in (keep, r)] for side in (0, 1)]
+            send = plus(*pick[1]).astype(bf16)
+            keep = plus(*pick[0]).astype(bf16)
+            flat = send.reshape(-1, send.shape[-1])
+            r = swap(flat, bits[which]).reshape(send.shape)
+        return keep, r
 
     def whole(residual, segment_ids, live_counts, norm_gain, z_weight, x_weight, bc_weight,
               dt_weight, conv_x, conv_x_bias, conv_bc, conv_bc_bias, dt_bias, a_log, d_skip,
@@ -448,8 +508,8 @@
         pad = LANES - heads
         w1s = jnp.concatenate([x_weight, bc_weight, jnp.pad(dt_weight, ((0, 0), (0, pad)))], 1)
         outa, outb, m1 = gather(out_weight.T, None)
-        w1a, w1b, m2 = gather(w1s, m1[1])
-        wza, wzb, _ = gather(z_weight, m2[1])
+        w1a, w1b, m2 = gather(w1s, m1[0])
+        wza, wzb, _ = gather(z_weight, m2[0])
 
         spot = jnp.arange(width_d, dtype=jnp.int32)
         block = spot // shard
@@ -458,20 +518,7 @@
             turned = turned | (((block >> k) & 1) << (len(bits) - 1 - k))
         source = (turned ^ me) * shard + spot % shard
         place = (spot[:, None] == source[None, :]).astype(bf16)
-
-        gain = norm_gain[None, :]
-        nrm_half, cot_half = call(
-            3.5, head_body, [((half, width_d), bf16)] * 2, residual, cotangent, gain, place
-        )
-
-        def both(own, other):
-            first = jnp.where(side == 0, own, other)
-            second = jnp.where(side == 0, other, own)
-            return jnp.concatenate([first, second], 0)
-
-        nrm_other = cross(nrm_half)
-        nrm = both(nrm_half, nrm_other)
-        cot = both(cot_half, cross(after(cot_half, nrm_other)))
+        place_t = (source[:, None] == spot[None, :]).astype(bf16)
 
         spots = jnp.arange(tokens)
         links = [jnp.ones((tokens,), f32)]
@@ -487,9 +534,24 @@
         dtb = jnp.pad(dt_bias, (0, pad))[None, :]
         alog = jnp.pad(a_log, (0, pad))[None, :]
         dsk = jnp.repeat(d_skip, head_width)[None, :]
+        gain = norm_gain[None, :]
         gg = gate_gain[None, :]
         cxb = conv_x_bias[None, :]
         cbcb = conv_bc_bias[None, :]
+        where = side.astype(jnp.int32)[None]
+        (residual, link, segc, segr, live, dtb, alog, dsk, gain, gg, cxb, cbcb, where, place,
+         place_t) = lax.optimization_barrier(
+            (residual, link, segc, segr, live, dtb, alog, dsk, gain, gg, cxb, cbcb, where, place,
+             place_t)
+        )
+        nrm_half, cot_half = call(
+            1.5, head_body, [((half, width_d), bf16)] * 2, residual, cotangent, gain, place
+        )
+        joined = [((tokens, width_d), bf16), ((width_d, tokens), bf16)]
+        nrm_other = cross(nrm_half)
+        nrm, nrm_t = call(1.0, join_body, joined, where, nrm_half, nrm_other, scalars=1)
+        cot_other = cross(cot_half)
+        cot, cot_t = call(1.0, join_body, joined, where, cot_half, cot_other, scalars=1)
 
         big = ((tokens, inner), f32)
 
@@ -497,10 +559,10 @@
             return fwd_body(head_width, *a)
 
         (dm,) = call(3.0, dmix_body, [big], cot, outa, outb, live)
-        xpre, xc, y, bcpre, bcc, dtp = call(
+        xpre, xc, y, bcpre, bcc, dtp, dec = call(
             7.0, fwd,
             [big, big, big, ((tokens, two_state), f32), ((tokens, two_state), f32),
-             ((tokens, LANES), f32)],
+             ((tokens, LANES), f32), ((2 * heads, SPAN, SPAN), f32)],
             nrm, w1a, w1b, link, segc, segr, conv_x, cxb, conv_bc, cbcb, dtb, alog,
         )
         z, g, sums = call(
@@ -513,23 +575,18 @@
             return mix_body(full, *a)
 
         cut = width_d // 2
-        blk, out_keep, out_send = call(
+        apart = [((half, width_d), f32), ((half, width_d), bf16)]
+        out_keep, out_send, mixed = call(
             4.0, mix,
-            [((tokens, width_d), f32), ((cut, inner), bf16), ((cut, inner), bf16)],
-            g, sums, sums2, gg, live, cot, outa, outb,
-            scratch=[pltpu.VMEM((tokens, inner), bf16)],
-        )
-        out_sum = scatter(out_keep, out_send)
-
-        def mine(v):
-            return lax.dynamic_slice_in_dim(v, side * half, half, 0)
-
-        def theirs(v):
-            return lax.dynamic_slice_in_dim(v, (1 - side) * half, half, 0).astype(bf16)
-
-        blk_other = cross(theirs(blk))
+            [((cut, inner), bf16), ((cut, inner), bf16), ((tokens, inner), bf16)],
+            g, sums, sums2, gg, live, cot_t,
+        )
+        blk_own, blk_send = call(2.5, blk_body, apart, where, mixed, outa, outb, scalars=1)
+        out_sum = plus(*scatter(out_keep, out_send, near))
+
+        blk_other = cross(blk_send)
         (block_out,) = call(
-            2.5, block_body, [((half, width_d), f32)], residual, mine(blk), blk_other, place
+            2.5, block_body, [((half, width_d), f32)], residual, blk_own, blk_other, place_t
         )
 
         def back_z(*a):
@@ -539,9 +596,9 @@
             6.0, back_z,
             [((tokens, inner), bf16), big, ((1, inner), f32), ((cut, inner), bf16),
              ((cut, inner), bf16)],
-            after(nrm, out_send), g, dm, z, y, xc, dsk, gg, sums, sums2,
-        )
-        z_weight_grad = scatter(z_keep, z_send)
+            after(nrm_t, out_send), g, dm, z, y, xc, dsk, gg, sums, sums2,
+        )
+        z_weight_grad = plus(*scatter(z_keep, z_send, far))
 
         def back(*a):
             return bwd_body(head_width, *a)
@@ -550,24 +607,26 @@
         dx, small, x_keep, x_send = call(
             14.0, back,
             [((tokens, wide), bf16), ((16, inner), f32), ((cut, wide), bf16), ((cut, wide), bf16)],
-            nrm, dy, xpre, xc, y, bcpre, bcc, dtp, link, segc, segr, conv_x, conv_bc, dtb, alog,
+            nrm_t, dy, xpre, xc, y, bcpre, bcc, dtp, dec, link, segc, segr, conv_x, conv_bc, dtb, alog,
             dsk,
             scratch=[pltpu.VMEM((tokens, two_state), f32)],
         )
-        sum1 = scatter(x_keep, x_send)
-        x_weight_grad = sum1[:, :inner]
-        dt_weight_grad = sum1[:, inner + two_state : inner + two_state + heads]
-        bc = sum1[:, inner : inner + two_state].reshape(nt, shard // nt, two_state)
-        bc_weight_grad = (
-            lax.dynamic_index_in_dim(bc, side, 0, False)
-            + cross(lax.dynamic_index_in_dim(bc, 1 - side, 0, False))
-        )
-
-        (dn,) = call(5.5, dn_body, [((tokens, width_d), f32)], dz, wza, wzb, dx, w1a, w1b)
-        dn_other = cross(theirs(dn))
+        x_weight_grad, dt_weight_grad, bc_own, bc_send = call(
+            1.5, last_body,
+            [((shard, inner), f32), ((shard, heads), f32)] + [((shard // nt, two_state), f32)] * 2,
+            where, *scatter(x_keep, x_send, near), scalars=1,
+            scratch=[pltpu.VMEM((shard, wide - inner), f32)],
+        )
+        bc_weight_grad = bc_own + cross(bc_send)
+
+        dn_own, dn_send = call(
+            5.0, dn_body, apart, where, dz, wza, wzb, dx, w1a, w1b, scalars=1,
+            scratch=[pltpu.VMEM((tokens, width_d), f32)],
+        )
+        dn_other = cross(dn_send)
         input_grad, norm_part = call(
             4.0, tail_body, [((half, width_d), f32), ((1, width_d), f32)],
-            residual, cotangent, gain, mine(dn), dn_other, place,
+            residual, cotangent, gain, dn_own, dn_other, place_t,
         )
 
         few = jnp.concatenate(
@@ -592,7 +651,7 @@
             shared[5, :two_state],
             few[7, :heads],
             few[7, LANES : LANES + heads],
-            jnp.sum(few[6].reshape(heads, head_width), axis=1),
+            few[7, 2 * LANES : 2 * LANES + heads],
             few[5],
             out_sum.T,
         )

time: 240 us -> 195 us (0.81)
  Pallas kernels: 56.7 us -> 40.9 us
  local copies, waits for them, and re-layouts: 20.6 us -> 10.8 us
  starting transfers between devices: 39.9 us -> 33 us
  other arithmetic: 15.7 us -> 8.98 us
  waiting for transfers between devices: 104 us -> 98.7 us
    pallas_call x10 -> x23, Pallas kernels: 56.7 us -> 40.9 us  [call(): pl.pallas_call(body, out_shape=[jax.ShapeDtypeStruct(s, d) for s, d in ou...]
    ppermute x28, waiting for transfers between devices: 96.3 us -> 88.4 us  [swap(): return lax.ppermute(v, 'dp', [(i, i ^ bit) for i in range(n)])]
    ppermute x28, starting transfers between devices: 32.1 us -> 26.6 us  [swap(): return lax.ppermute(v, 'dp', [(i, i ^ bit) for i in range(n)])]
    add x4, other arithmetic: 3.04 us -> 0.04 us  [whole(): few = few + swap(few, bit)]
    unnamed x58 -> x50, local copies, waits for them, and re-layouts: 6.42 us -> 3.54 us
    dynamic_slice x2 -> x0, local copies, waits for them, and re-layouts: 2.71 us -> none  [mine(): return lax.dynamic_slice_in_dim(v, side * half, half, 0)]
    convert_element_type x10 -> x11, other arithmetic: 5.33 us -> 4.42 us  [the longest x1 2.6 us: whole(): place_t = (source[:, None] == spot[None, :]).astype(bf16)]
  transfers between devices with their start and end apart: 35 -> 35, of which waited for: 18 -> 21; matrix products, arithmetic and copies ran while one was open for 13% -> 9% of each run, Pallas kernels for 20% -> 12%
where the time goes in v2:
time: 195 us; the launch traced here: 194 us
  waiting for transfers between devices  98.7 us (51%)
  Pallas kernels  40.9 us (21%)
  starting transfers between devices  33 us (17%)
  local copies, waits for them, and re-layouts  10.8 us (6%)
  other arithmetic  8.98 us (5%)
    ppermute x28, waiting for transfers between devices, swap(): return lax.ppermute(v, 'dp', [(i, i ^ bit) for i in range(n)])  88.4 us
    pallas_call x23, Pallas kernels, call(): pl.pallas_call(body, out_shape=[jax.ShapeDtypeStruct(s, d) for s, d in ou...  40.9 us
    ppermute x28, starting transfers between devices, swap(): return lax.ppermute(v, 'dp', [(i, i ^ bit) for i in range(n)])  26.6 us
    ppermute x7, waiting for transfers between devices, cross(): return lax.ppermute(v, 'tensor', [(0, 1), (1, 0)])  10.3 us
    ppermute x7, starting transfers between devices, cross(): return lax.ppermute(v, 'tensor', [(0, 1), (1, 0)])  6.38 us
  transfers between devices with their start and end apart: 35, of which 21 were waited for; matrix products, arithmetic and copies ran while one was open for 9% of the time, Pallas kernels for 12%

profile of v2, /device:TPU:0, one launch (start us, length us, event | category | flops | bytes accessed | tf_op | source)
XLA Modules:
  0.0 194.3 jit_solution(15956349792896914107)
XLA Ops:
  0.6 4.1 %collective-permute-start.1 = (bf16[64,1024]{1,0:T(8,128)(2,1)}, bf16[64,1024]{1,0:T(8,128)(2,1)S(1)}, u32[]{:S(2)}, u32[]{:S(2)}) collective-permute-start(bf16[64,1024]{1,0:T(8,128)(2,1)} %bitcast.66), channel_id=1, source_target_pairs={{0,16},{2,18},{4,20},{6,22},{8,24},{10,26},{12,28},{14,30},{16,0},... | collective-permute-start | bytes 393224 | tf_op jit(solution)/shard_map/ppermute | solution.py:453
  4.8 0.8 copy.47
  5.6 0.9 fusion.10.first
  6.5 4.8 %collective-permute-done.1.second = bf16[64,1024]{1,0:T(8,128)(2,1)S(1)} collective-permute-done((bf16[64,1024]{1,0:T(8,128)(2,1)}, bf16[64,1024]{1,0:T(8,128)(2,1)S(1)}, u32[]{:S(2)}, u32[]{:S(2)}) %collective-permute-start.1) | collective-permute-done | bytes 131104 | tf_op jit(solution)/shard_map/ppermute | solution.py:453
  11.3 10.5 %collective-permute-done.2.second = bf16[64,1408]{1,0:T(8,128)(2,1)S(1)} collective-permute-done((bf16[64,1408]{1,0:T(8,128)(2,1)S(1)}, bf16[64,1408]{1,0:T(8,128)(2,1)S(1)}, u32[]{:S(2)}, u32[]{:S(2)}) %collective-permute-start.2) | collective-permute-done | bytes 180256 | tf_op jit(solution)/shard_map/ppermute | solution.py:453
  21.9 8.7 %collective-permute-done.7.second = bf16[128,1408]{1,0:T(8,128)(2,1)S(1)} collective-permute-done((bf16[128,1408]{1,0:T(8,128)(2,1)S(1)}, bf16[128,1408]{1,0:T(8,128)(2,1)S(1)}, u32[]{:S(2)}, u32[]{:S(2)}) %collective-permute-start.7) | collective-permute-done | bytes 360480 | tf_op jit(solution)/shard_map/ppermute | solution.py:453
  31.0 0.8 collective-permute-start.11
  33.1 4.3 %collective-permute-done.11.second = bf16[128,1024]{1,0:T(8,128)(2,1)S(1)} collective-permute-done((bf16[128,1024]{1,0:T(8,128)(2,1)S(1)}, bf16[128,1024]{1,0:T(8,128)(2,1)S(1)}, u32[]{:S(2)}, u32[]{:S(2)}) %collective-permute-start.11) | collective-permute-done | bytes 262176 | tf_op jit(solution)/shard_map/ppermute | solution.py:453
  37.4 0.8 shard_map.308.first
  38.2 1.8 collective-permute-start.12
  40.1 2.6 %fusion.1 = (bf16[1024,1024]{1,0:T(8,128)(2,1)S(1)}, bf16[1024,1024]{1,0:T(8,128)(2,1)}) fusion(s32[1024]{0:T(1024)S(1)} %fusion.21), kind=kLoop, calls=%fused_computation.3 | loop fusion | flops 4194304 | bytes 4198400 | tf_op jit(solution)/shard_map/convert_element_type | solution.py:521
  42.7 2.4 %collective-permute-start.3 = (bf16[64,1024]{1,0:T(8,128)(2,1)}, bf16[64,1024]{1,0:T(8,128)(2,1)}, u32[]{:S(2)}, u32[]{:S(2)}) collective-permute-start(bf16[64,1024]{1,0:T(8,128)(2,1)} %first), channel_id=1, source_target_pairs={{0,16},{2,18},{4,20},{6,22},{8,24},{10,26},{12,28},{14,30},{16,0},... | collective-permute-start | bytes 393224 | tf_op jit(solution)/shard_map/ppermute | solution.py:453
  45.1 4.7 %collective-permute-done.8.second = bf16[256,1408]{1,0:T(8,128)(2,1)S(1)} collective-permute-done((bf16[256,1408]{1,0:T(8,128)(2,1)S(1)}, bf16[256,1408]{1,0:T(8,128)(2,1)S(1)}, u32[]{:S(2)}, u32[]{:S(2)}) %collective-permute-start.8) | collective-permute-done | bytes 720928 | tf_op jit(solution)/shard_map/ppermute | solution.py:453
  49.7 0.9 copy-done.3
  50.6 1.1 copy-done.4
  52.6 0.8 broadcast_in_dim_reshape.3.dsk.a_6_.a_16_
  53.4 1.0 shard_map.299.first
  54.8 2.9 %collective-permute-done.12.second = bf16[256,1024]{1,0:T(8,128)(2,1)} collective-permute-done((bf16[256,1024]{1,0:T(8,128)(2,1)}, bf16[256,1024]{1,0:T(8,128)(2,1)}, u32[]{:S(2)}, u32[]{:S(2)}) %collective-permute-start.12) | collective-permute-done | bytes 524320 | tf_op jit(solution)/shard_map/ppermute | solution.py:453
  57.7 2.3 %shard_map.309.outa = bf16[512,1024]{1,0:T(8,128)(2,1)} custom-call(bf16[256,1024]{1,0:T(8,128)(2,1)} %shard_map.308.first, bf16[256,1024]{1,0:T(8,128)(2,1)} %collective-permute-done.12.second), custom_call_target="tpu_custom_call" | custom-call | flops 450000000 | bytes 1500000 | tf_op jit(solution)/shard_map/pallas_call | solution.py:31
  60.0 3.2 %collective-permute-done.4.second = bf16[128,1024]{1,0:T(8,128)(2,1)S(1)} collective-permute-done((bf16[128,1024]{1,0:T(8,128)(2,1)S(1)}, bf16[128,1024]{1,0:T(8,128)(2,1)S(1)}, u32[]{:S(2)}, u32[]{:S(2)}) %collective-permute-start.4) | collective-permute-done | bytes 262176 | tf_op jit(solution)/shard_map/ppermute | solution.py:453
  64.2 1.5 shard_map.297
  65.7 2.1 %collective-permute-start.10 = (bf16[128,1024]{1,0:T(8,128)(2,1)}, bf16[128,1024]{1,0:T(8,128)(2,1)}, u32[]{:S(2)}, u32[]{:S(2)}) collective-permute-start(bf16[128,1024]{1,0:T(8,128)(2,1)} %get-tuple-element.90.own), channel_id=1, source_target_pairs={{0,1},{1,0},{2,3},{3,2},{4,5},{5,4},{6,7},{7,6},{8,9},{9,8},{10,11... | collective-permute-start | bytes 786440 | tf_op jit(solution)/shard_map/ppermute | solution.py:456
  67.8 9.0 %collective-permute-done.5.second = bf16[256,1024]{1,0:T(8,128)(2,1)S(1)} collective-permute-done((bf16[256,1024]{1,0:T(8,128)(2,1)S(1)}, bf16[256,1024]{1,0:T(8,128)(2,1)S(1)}, u32[]{:S(2)}, u32[]{:S(2)}) %collective-permute-start.5) | collective-permute-done | bytes 524320 | tf_op jit(solution)/shard_map/ppermute | solution.py:453
  76.8 1.1 shard_map.301.wza
  77.8 1.5 copy.48.a_3_.a_9_
  79.3 0.8 copy.49.a_4_.a_10_
  80.1 1.3 shard_map.306
  81.4 1.3 shard_map.298
  82.8 2.4 %shard_map.310.dm_r.a_2_ = f32[256,1024]{1,0:T(8,128)S(1)} custom-call(bf16[256,1024]{1,0:T(8,128)(2,1)S(1)} %get-tuple-element.91.cot, bf16[512,1024]{1,0:T(8,128)(2,1)} %shard_map.309.outa, bf16[512,1024]{1,0:T(8,128)(2,1)} %collective-permute-done.13.outb, f32[256,1]{1,0:T(8,128)S(1)} %copy-done.5), custom_call_target="tpu_custom_call" | custom-call | flops 2700000000 | bytes 9000000 | tf_op jit(solution)/shard_map/pallas_call | solution.py:31
  85.2 4.9 %shard_map.305 = (f32[256,1024]{1,0:T(8,128)S(1)}, f32[256,1024]{1,0:T(8,128)S(1)}, f32[256,1024]{1,0:T(8,128)S(1)}, f32[256,256]{1,0:T(8,128)S(1)}, f32[256,256...) custom-call(bf16[256,1024]{1,0:T(8,128)(2,1)S(1)} %get-tuple-element.77.a_0_.nrm, ...), custom_call_target="tpu_custom_call" | custom-call | flops 6300000256 | bytes 21000000 | tf_op jit(solution)/shard_map/pallas_call | solution.py:31
  90.2 2.7 %shard_map.311 = (f32[256,1024]{1,0:T(8,128)S(1)}, f32[256,1024]{1,0:T(8,128)S(1)}, f32[16,256]{1,0:T(8,128)S(1)}) custom-call(bf16[256,1024]{1,0:T(8,128)(2,1)S(1)} %get-tuple-element.77.a_0_.nrm, bf16[512,1024]{1,0:T(8,128)(2,1)} %shard_map.301.wza, bf16[512,1024]{1,0:T(8,128)(2,1)} %collective-permute-done.6.wzb, ...), custom_call_target="tpu_custom_call" | custom-call | flops 4499999744 | bytes 15000000 | tf_op jit(solution)/shard_map/pallas_call | solution.py:31
  93.4 3.2 %collective-permute-done.14.a_2_.a_9_ = f32[16,256]{1,0:T(8,128)S(1)} collective-permute-done((f32[16,256]{1,0:T(8,128)S(1)}, f32[16,256]{1,0:T(8,128)S(1)}, u32[]{:S(2)}, u32[]{:S(2)}) %collective-permute-start.14) | collective-permute-done | bytes 16416 | tf_op jit(solution)/shard_map/ppermute | solution.py:456
  96.6 1.0 shard_map.312
  97.6 1.7 shard_map.315
  99.3 8.3 %shard_map.316 = (bf16[256,1408]{1,0:T(8,128)(2,1)S(1)}, f32[16,1024]{1,0:T(8,128)S(1)}, bf16[512,1408]{1,0:T(8,128)(2,1)S(1)}, bf16[512,1408]{1,0:T(8,128)(2,1)S(1)}) custom-call(bf16[1024,256]{1,0:T(8,128)(2,1)S(1)} %get-tuple-element.103.a_0_, f32[256,1024]{1,0:T(8,128)S(1)} %get-tuple-element.106.a_1_, f32[256,1024]{1,0:T(8,128)S(1)} %get-tuple-element.107.a_2_, ...), custom_call_target="tpu_custom_call" | custom-call | flops 12600000512 | bytes 42000000 | tf_op jit(solution)/shard_map/pallas_call | solution.py:31
  107.5 3.6 %shard_map.317 = (f32[128,1024]{1,0:T(8,128)S(1)}, bf16[128,1024]{1,0:T(8,128)(2,1)S(1)}) custom-call(s32[1]{0:T(128)} %bitcast.12.side, bf16[256,1024]{1,0:T(8,128)(2,1)S(1)} %get-tuple-element.105.dz, bf16[512,1024]{1,0:T(8,128)(2,1)} %shard_map.301.wza, bf16[512,1024]{1,0:T(8,128)(2,1)} %collective-permute-done.6.wzb, ...), custom_call_target="tpu_custom_call" | custom-call | flops 4499999744 | bytes 15000000 | tf_op jit(solution)/shard_map/pallas_call | solution.py:31
  111.8 3.1 %shard_map.313 = (f32[128,1024]{1,0:T(8,128)S(1)}, bf16[128,1024]{1,0:T(8,128)(2,1)S(1)}) custom-call(s32[1]{0:T(128)} %bitcast.12.side, bf16[256,1024]{1,0:T(8,128)(2,1)S(1)} %get-tuple-element.97.mixed, bf16[512,1024]{1,0:T(8,128)(2,1)} %shard_map.309.outa, bf16[512,1024]{1,0:T(8,128)(2,1)} %collective-permute-done.13.outb), custom_call_target="tpu_custom_call" | custom-call | flops 2249999872 | bytes 7500000 | tf_op jit(solution)/shard_map/pallas_call | solution.py:31
  114.9 1.5 collective-permute-start.15
  116.5 3.9 %collective-permute-done.16.other = bf16[128,1024]{1,0:T(8,128)(2,1)S(1)} collective-permute-done((bf16[128,1024]{1,0:T(8,128)(2,1)S(1)}, bf16[128,1024]{1,0:T(8,128)(2,1)S(1)}, u32[]{:S(2)}, u32[]{:S(2)}) %collective-permute-start.16) | collective-permute-done | bytes 262176 | tf_op jit(solution)/shard_map/ppermute | solution.py:456
  120.4 1.7 shard_map.318
  122.7 0.7 collective-permute-done.17
  123.6 4.3 %collective-permute-done.18 = f32[16,1024]{1,0:T(8,128)S(1)} collective-permute-done((f32[16,1024]{1,0:T(8,128)S(1)}, f32[16,1024]{1,0:T(8,128)S(1)}, u32[]{:S(2)}, u32[]{:S(2)}) %collective-permute-start.18) | collective-permute-done | bytes 65568 | tf_op jit(solution)/shard_map/ppermute | solution.py:453
  128.7 3.5 %collective-permute-done.19 = f32[16,1024]{1,0:T(8,128)S(1)} collective-permute-done((f32[16,1024]{1,0:T(8,128)S(1)}, f32[16,1024]{1,0:T(8,128)S(1)}, u32[]{:S(2)}, u32[]{:S(2)}) %collective-permute-start.19) | collective-permute-done | bytes 65568 | tf_op jit(solution)/shard_map/ppermute | solution.py:453
  132.2 1.6 collective-permute-start.20
  133.7 1.5 shard_map.314
  135.2 2.6 %collective-permute-done.20 = f32[16,1024]{1,0:T(8,128)S(1)} collective-permute-done((f32[16,1024]{1,0:T(8,128)S(1)}, f32[16,1024]{1,0:T(8,128)S(1)}, u32[]{:S(2)}, u32[]{:S(2)}) %collective-permute-start.20) | collective-permute-done | bytes 65568 | tf_op jit(solution)/shard_map/ppermute | solution.py:453
  137.9 0.8 collective-permute-start.21
  140.4 1.5 collective-permute-done.21
  145.3 1.5 collective-permute-start.27
  147.0 9.2 %collective-permute-done.23 = bf16[256,1024]{1,0:T(8,128)(2,1)S(1)} collective-permute-done((bf16[256,1024]{1,0:T(8,128)(2,1)S(1)}, bf16[256,1024]{1,0:T(8,128)(2,1)S(1)}, u32[]{:S(2)}, u32[]{:S(2)}) %collective-permute-start.23) | collective-permute-done | bytes 524320 | tf_op jit(solution)/shard_map/ppermute | solution.py:453
  156.4 0.8 collective-permute-start.24
  157.2 2.0 %collective-permute-done.32 = bf16[256,1024]{1,0:T(8,128)(2,1)S(1)} collective-permute-done((bf16[256,1024]{1,0:T(8,128)(2,1)S(1)}, bf16[256,1024]{1,0:T(8,128)(2,1)S(1)}, u32[]{:S(2)}, u32[]{:S(2)}) %collective-permute-start.32) | collective-permute-done | bytes 524320 | tf_op jit(solution)/shard_map/ppermute | solution.py:453
  159.4 2.1 %collective-permute-start.33 = (bf16[128,1024]{1,0:T(8,128)(2,1)S(1)}, bf16[128,1024]{1,0:T(8,128)(2,1)S(1)}, u32[]{:S(2)}, u32[]{:S(2)}) collective-permute-start(bf16[128,1024]{1,0:T(8,128)(2,1)S(1)} %get-tuple-element.183), channel_id=1, source_target_pairs={{0,8},{2,10},{4,12},{6,14},{8,0},{10,2},{12,4},{14,6},{16,24},{18,... | collective-permute-start | bytes 786440 | tf_op jit(solution)/shard_map/ppermute | solution.py:453
  161.4 9.0 %collective-permute-done.27 = bf16[256,1408]{1,0:T(8,128)(2,1)S(1)} collective-permute-done((bf16[256,1408]{1,0:T(8,128)(2,1)S(1)}, bf16[256,1408]{1,0:T(8,128)(2,1)S(1)}, u32[]{:S(2)}, u32[]{:S(2)}) %collective-permute-start.27) | collective-permute-done | bytes 720928 | tf_op jit(solution)/shard_map/ppermute | solution.py:453
  170.6 2.5 %collective-permute-start.28 = (bf16[128,1408]{1,0:T(8,128)(2,1)S(1)}, bf16[128,1408]{1,0:T(8,128)(2,1)S(1)}, u32[]{:S(2)}, u32[]{:S(2)}) collective-permute-start(bf16[128,1408]{1,0:T(8,128)(2,1)S(1)} %get-tuple-element.181), channel_id=1, source_target_pairs={{0,8},{2,10},{4,12},{6,14},{8,0},{10,2},{12,4},{14,6},{16,24},{18,... | collective-permute-start | bytes 1081352 | tf_op jit(solution)/shard_map/ppermute | solution.py:453
  173.2 0.8 collective-permute-start.25
  174.0 1.5 collective-permute-start.34
  175.4 4.6 %collective-permute-done.28 = bf16[128,1408]{1,0:T(8,128)(2,1)S(1)} collective-permute-done((bf16[128,1408]{1,0:T(8,128)(2,1)S(1)}, bf16[128,1408]{1,0:T(8,128)(2,1)S(1)}, u32[]{:S(2)}, u32[]{:S(2)}) %collective-permute-start.28) | collective-permute-done | bytes 360480 | tf_op jit(solution)/shard_map/ppermute | solution.py:453
  180.1 3.5 %collective-permute-start.29 = (bf16[64,1408]{1,0:T(8,128)(2,1)S(1)}, bf16[64,1408]{1,0:T(8,128)(2,1)S(1)}, u32[]{:S(2)}, u32[]{:S(2)}) collective-permute-start(bf16[64,1408]{1,0:T(8,128)(2,1)S(1)} %get-tuple-element.186), channel_id=1, source_target_pairs={{0,16},{2,18},{4,20},{6,22},{8,24},{10,26},{12,28},{14,30},{16,0},... | collective-permute-start | bytes 540680 | tf_op jit(solution)/shard_map/ppermute | solution.py:453
  183.6 0.8 convert_add_fusion.6
  184.4 4.7 %collective-permute-done.29.other = bf16[64,1408]{1,0:T(8,128)(2,1)S(1)} collective-permute-done((bf16[64,1408]{1,0:T(8,128)(2,1)S(1)}, bf16[64,1408]{1,0:T(8,128)(2,1)S(1)}, u32[]{:S(2)}, u32[]{:S(2)}) %collective-permute-start.29) | collective-permute-done | bytes 180256 | tf_op jit(solution)/shard_map/ppermute | solution.py:453
  189.7 0.8 collective-permute-start.30
  190.5 0.8 add_bitcast_fusion
  191.9 1.7 collective-permute-done.30
  (120 shorter events, 14.4 us)
Async XLA Ops:
  0.6 10.6 %collective-permute-start.1 = (bf16[64,1024]{1,0:T(8,128)(2,1)}, bf16[64,1024]{1,0:T(8,128)(2,1)S(1)}, u32[]{:S(2)}, u32[]{:S(2)}) collective-permute-start(bf16[64,1024]{1,0:T(8,128)(2,1)} %bitcast.66), channel_id=1, source_target_pairs={{0,16},{2,18},{4,20},{6,22},{8,24},{10,26},{12,28},{14,30},{16,0},... | collective-permute-start | bytes 393224 | tf_op jit(solution)/shard_map/ppermute | solution.py:453
  6.5 24.4 %copy-start.13 = (bf16[1024,64]{0,1:T(8,128)(2,1)S(1)}, bf16[1024,64]{0,1:T(8,128)(2,1)}, u32[]{:S(2)}) copy-start(bf16[1024,64]{0,1:T(8,128)(2,1)} %param.34) | copy-start | bytes 393220
  11.3 10.5 %collective-permute-start.2 = (bf16[64,1408]{1,0:T(8,128)(2,1)S(1)}, bf16[64,1408]{1,0:T(8,128)(2,1)S(1)}, u32[]{:S(2)}, u32[]{:S(2)}) collective-permute-start(bf16[64,1408]{1,0:T(8,128)(2,1)S(1)} %fusion.10.first), channel_id=1, source_target_pairs={{0,16},{2,18},{4,20},{6,22},{8,24},{10,26},{12,28},{14,30},{16,0},... | collective-permute-start | bytes 540680 | tf_op jit(solution)/shard_map/ppermute | solution.py:453
  21.8 8.8 %collective-permute-start.7 = (bf16[128,1408]{1,0:T(8,128)(2,1)S(1)}, bf16[128,1408]{1,0:T(8,128)(2,1)S(1)}, u32[]{:S(2)}, u32[]{:S(2)}) collective-permute-start(bf16[128,1408]{1,0:T(8,128)(2,1)S(1)} %shard_map.302.first), channel_id=1, source_target_pairs={{0,8},{2,10},{4,12},{6,14},{8,0},{10,2},{12,4},{14,6},{16,24},{18,... | collective-permute-start | bytes 1081352 | tf_op jit(solution)/shard_map/ppermute | solution.py:453
  30.7 7.6 %copy-start.1 = (bf16[256,1408]{1,0:T(8,128)(2,1)}, bf16[256,1408]{1,0:T(8,128)(2,1)S(1)}, u32[]{:S(2)}) copy-start(bf16[256,1408]{1,0:T(8,128)(2,1)S(1)} %shard_map.303.first) | copy-start | bytes 2162692
  30.7 19.1 %collective-permute-start.8 = (bf16[256,1408]{1,0:T(8,128)(2,1)S(1)}, bf16[256,1408]{1,0:T(8,128)(2,1)S(1)}, u32[]{:S(2)}, u32[]{:S(2)}) collective-permute-start(bf16[256,1408]{1,0:T(8,128)(2,1)S(1)} %shard_map.303.first), channel_id=1, source_target_pairs={{0,4},{2,6},{4,0},{6,2},{8,12},{10,14},{12,8},{14,10},{16,20},{18,... | collective-permute-start | bytes 2162696 | tf_op jit(solution)/shard_map/ppermute | solution.py:453
  31.0 6.4 %collective-permute-start.11 = (bf16[128,1024]{1,0:T(8,128)(2,1)S(1)}, bf16[128,1024]{1,0:T(8,128)(2,1)S(1)}, u32[]{:S(2)}, u32[]{:S(2)}) collective-permute-start(bf16[128,1024]{1,0:T(8,128)(2,1)S(1)} %shard_map.307.first), channel_id=1, source_target_pairs={{0,8},{2,10},{4,12},{6,14},{8,0},{10,2},{12,4},{14,6},{16,24},{18,... | collective-permute-start | bytes 786440 | tf_op jit(solution)/shard_map/ppermute | solution.py:453
  38.2 19.4 %collective-permute-start.12 = (bf16[256,1024]{1,0:T(8,128)(2,1)}, bf16[256,1024]{1,0:T(8,128)(2,1)}, u32[]{:S(2)}, u32[]{:S(2)}) collective-permute-start(bf16[256,1024]{1,0:T(8,128)(2,1)} %shard_map.308.first), channel_id=1, source_target_pairs={{0,4},{2,6},{4,0},{6,2},{8,12},{10,14},{12,8},{14,10},{16,20},{18,... | collective-permute-start | bytes 1572872 | tf_op jit(solution)/shard_map/ppermute | solution.py:453
  40.0 10.6 %copy-start.2 = (bf16[256,1408]{1,0:T(8,128)(2,1)S(1)}, bf16[256,1408]{1,0:T(8,128)(2,1)}, u32[]{:S(2)}) copy-start(bf16[256,1408]{1,0:T(8,128)(2,1)} %copy-done.1) | copy-start | bytes 2162692
  40.1 11.9 %copy-start.22 = (f32[16]{0:T(128)S(1)}, f32[16]{0:T(128)}, u32[]{:S(2)}) copy-start(f32[16]{0:T(128)} %param.31) | copy-start | bytes 196
  40.1 11.9 %copy-start.23 = (f32[16]{0:T(128)S(1)}, f32[16]{0:T(128)}, u32[]{:S(2)}) copy-start(f32[16]{0:T(128)} %param.30) | copy-start | bytes 196
  40.1 11.9 %copy-start.21 = (f32[16]{0:T(128)S(1)}, f32[16]{0:T(128)}, u32[]{:S(2)}) copy-start(f32[16]{0:T(128)} %param.32) | copy-start | bytes 196
  42.7 10.7 %collective-permute-start.3 = (bf16[64,1024]{1,0:T(8,128)(2,1)}, bf16[64,1024]{1,0:T(8,128)(2,1)}, u32[]{:S(2)}, u32[]{:S(2)}) collective-permute-start(bf16[64,1024]{1,0:T(8,128)(2,1)} %first), channel_id=1, source_target_pairs={{0,16},{2,18},{4,20},{6,22},{8,24},{10,26},{12,28},{14,30},{16,0},... | collective-permute-start | bytes 393224 | tf_op jit(solution)/shard_map/ppermute | solution.py:453
  49.7 0.9 copy-start.3
  50.6 1.1 copy-start.4
  51.8 33.3 %collective-permute-start.9 = (bf16[512,1408]{1,0:T(8,128)(2,1)S(1)}, bf16[512,1408]{1,0:T(8,128)(2,1)}, u32[]{:S(2)}, u32[]{:S(2)}) collective-permute-start(bf16[512,1408]{1,0:T(8,128)(2,1)S(1)} %shard_map.304.a_1_.w1a), channel_id=1, source_target_pairs={{0,2},{2,0},{4,6},{6,4},{8,10},{10,8},{12,14},{14,12},{16,18},{18,... | collective-permute-start | bytes 4325384 | tf_op jit(solution)/shard_map/ppermute | solution.py:453
  54.4 5.6 %copy-start.8 = (s32[256]{0:T(256)S(1)}, s32[256]{0:T(256)}, u32[]{:S(2)}) copy-start(s32[256]{0:T(256)} %param.19) | copy-start | bytes 3076
  54.4 9.8 %copy-start = (bf16[1024,1024]{1,0:T(8,128)(2,1)S(1)}, bf16[1024,1024]{1,0:T(8,128)(2,1)}, u32[]{:S(2)}) copy-start(bf16[1024,1024]{1,0:T(8,128)(2,1)} %get-tuple-element.75.place) | copy-start | bytes 6291460
  54.4 9.8 %copy-start.9 = (f32[128,1024]{1,0:T(8,128)S(1)}, f32[128,1024]{1,0:T(8,128)}, u32[]{:S(2)}) copy-start(f32[128,1024]{1,0:T(8,128)} %cot.3) | copy-start | bytes 1572868
  54.4 9.8 %copy-start.11 = (f32[128,1024]{1,0:T(8,128)S(1)}, f32[128,1024]{1,0:T(8,128)}, u32[]{:S(2)}) copy-start(f32[128,1024]{1,0:T(8,128)} %res.2) | copy-start | bytes 1572868
  54.4 9.8 %copy-start.18 = (f32[1024]{0:T(1024)S(1)}, f32[1024]{0:T(1024)}, u32[]{:S(2)}) copy-start(f32[1024]{0:T(1024)} %param.21) | copy-start | bytes 12292
  54.5 8.8 %collective-permute-start.4 = (bf16[128,1024]{1,0:T(8,128)(2,1)S(1)}, bf16[128,1024]{1,0:T(8,128)(2,1)S(1)}, u32[]{:S(2)}, u32[]{:S(2)}) collective-permute-start(bf16[128,1024]{1,0:T(8,128)(2,1)S(1)} %shard_map.299.first), channel_id=1, source_target_pairs={{0,8},{2,10},{4,12},{6,14},{8,0},{10,2},{12,4},{14,6},{16,24},{18,... | collective-permute-start | bytes 786440 | tf_op jit(solution)/shard_map/ppermute | solution.py:453
  60.0 22.7 %collective-permute-start.13 = (bf16[512,1024]{1,0:T(8,128)(2,1)}, bf16[512,1024]{1,0:T(8,128)(2,1)}, u32[]{:S(2)}, u32[]{:S(2)}) collective-permute-start(bf16[512,1024]{1,0:T(8,128)(2,1)} %shard_map.309.outa), channel_id=1, source_target_pairs={{0,2},{2,0},{4,6},{6,4},{8,10},{10,8},{12,14},{14,12},{16,18},{18,... | collective-permute-start | bytes 3145736 | tf_op jit(solution)/shard_map/ppermute | solution.py:453
  63.2 13.5 %collective-permute-start.5 = (bf16[256,1024]{1,0:T(8,128)(2,1)S(1)}, bf16[256,1024]{1,0:T(8,128)(2,1)S(1)}, u32[]{:S(2)}, u32[]{:S(2)}) collective-permute-start(bf16[256,1024]{1,0:T(8,128)(2,1)S(1)} %shard_map.300.first), channel_id=1, source_target_pairs={{0,4},{2,6},{4,0},{6,2},{8,12},{10,14},{12,8},{14,10},{16,20},{18,... | collective-permute-start | bytes 1572872 | tf_op jit(solution)/shard_map/ppermute | solution.py:453
  65.7 14.4 %collective-permute-start.10 = (bf16[128,1024]{1,0:T(8,128)(2,1)}, bf16[128,1024]{1,0:T(8,128)(2,1)}, u32[]{:S(2)}, u32[]{:S(2)}) collective-permute-start(bf16[128,1024]{1,0:T(8,128)(2,1)} %get-tuple-element.90.own), channel_id=1, source_target_pairs={{0,1},{1,0},{2,3},{3,2},{4,5},{5,4},{6,7},{7,6},{8,9},{9,8},{10,11... | collective-permute-start | bytes 786440 | tf_op jit(solution)/shard_map/ppermute | solution.py:456
  67.8 13.6 %collective-permute-start = (bf16[128,1024]{1,0:T(8,128)(2,1)}, bf16[128,1024]{1,0:T(8,128)(2,1)}, u32[]{:S(2)}, u32[]{:S(2)}) collective-permute-start(bf16[128,1024]{1,0:T(8,128)(2,1)} %get-tuple-element.76.own), channel_id=1, source_target_pairs={{0,1},{1,0},{2,3},{3,2},{4,5},{5,4},{6,7},{7,6},{8,9},{9,8},{10,11... | collective-permute-start | bytes 786440 | tf_op jit(solution)/shard_map/ppermute | solution.py:456
  77.8 12.3 %collective-permute-start.6 = (bf16[512,1024]{1,0:T(8,128)(2,1)}, bf16[512,1024]{1,0:T(8,128)(2,1)}, u32[]{:S(2)}, u32[]{:S(2)}) collective-permute-start(bf16[512,1024]{1,0:T(8,128)(2,1)} %shard_map.301.wza), channel_id=1, source_target_pairs={{0,2},{2,0},{4,6},{6,4},{8,10},{10,8},{12,14},{14,12},{16,18},{18,... | collective-permute-start | bytes 3145736 | tf_op jit(solution)/shard_map/ppermute | solution.py:453
  81.4 1.3 copy-start.5
  82.7 2.5 %copy-start.6 = (f32[256,4]{1,0:T(8,128)S(1)}, f32[256,4]{1,0:T(8,128)}, u32[]{:S(2)}) copy-start(f32[256,4]{1,0:T(8,128)} %copy.48.a_3_.a_9_) | copy-start | bytes 12292
  82.7 2.5 %copy-start.7 = (s32[256,1]{1,0:T(8,128)S(1)}, s32[256,1]{1,0:T(8,128)}, u32[]{:S(2)}) copy-start(s32[256,1]{1,0:T(8,128)} %copy.49.a_4_.a_10_) | copy-start | bytes 3076
  82.7 2.5 %copy-start.14 = (f32[4,1024]{1,0:T(4,128)S(1)}, f32[4,1024]{1,0:T(4,128)}, u32[]{:S(2)}) copy-start(f32[4,1024]{1,0:T(4,128)} %a_12_.1) | copy-start | bytes 49156
  82.7 2.5 %copy-start.15 = (f32[1024]{0:T(1024)S(1)}, f32[1024]{0:T(1024)}, u32[]{:S(2)}) copy-start(f32[1024]{0:T(1024)} %param.27) | copy-start | bytes 12292
  82.7 2.5 %copy-start.17 = (f32[4,256]{1,0:T(4,128)S(1)}, f32[4,256]{1,0:T(4,128)}, u32[]{:S(2)}) copy-start(f32[4,256]{1,0:T(4,128)} %a_13_.1) | copy-start | bytes 12292
  82.8 2.4 %copy-start.20 = (f32[256]{0:T(256)S(1)}, f32[256]{0:T(256)}, u32[]{:S(2)}) copy-start(f32[256]{0:T(256)} %param.29) | copy-start | bytes 3076
  85.2 4.9 %copy-start.16 = (f32[1024]{0:T(1024)S(1)}, f32[1024]{0:T(1024)}, u32[]{:S(2)}) copy-start(f32[1024]{0:T(1024)} %param.33) | copy-start | bytes 12292
  92.8 3.8 %collective-permute-start.14 = (f32[16,256]{1,0:T(8,128)S(1)}, f32[16,256]{1,0:T(8,128)S(1)}, u32[]{:S(2)}, u32[]{:S(2)}) collective-permute-start(f32[16,256]{1,0:T(8,128)S(1)} %get-tuple-element.95.a_1_.a_8_), channel_id=1, source_target_pairs={{0,1},{1,0},{2,3},{3,2},{4,5},{5,4},{6,7},{7,6},{8,9},{9,8},{10,11... | collective-permute-start | bytes 49160 | tf_op jit(solution)/shard_map/ppermute | solution.py:456
  111.2 9.2 %collective-permute-start.16 = (bf16[128,1024]{1,0:T(8,128)(2,1)S(1)}, bf16[128,1024]{1,0:T(8,128)(2,1)S(1)}, u32[]{:S(2)}, u32[]{:S(2)}) collective-permute-start(bf16[128,1024]{1,0:T(8,128)(2,1)S(1)} %get-tuple-element.114), channel_id=1, source_target_pairs={{0,1},{1,0},{2,3},{3,2},{4,5},{5,4},{6,7},{7,6},{8,9},{9,8},{10,11... | collective-permute-start | bytes 786440 | tf_op jit(solution)/shard_map/ppermute | solution.py:456
  111.8 8.6 %copy-start.10 = (f32[128,1024]{1,0:T(8,128)S(1)}, f32[128,1024]{1,0:T(8,128)}, u32[]{:S(2)}) copy-start(f32[128,1024]{1,0:T(8,128)} %cot.3) | copy-start | bytes 1572868
  111.8 8.6 %copy-start.12 = (f32[128,1024]{1,0:T(8,128)S(1)}, f32[128,1024]{1,0:T(8,128)}, u32[]{:S(2)}) copy-start(f32[128,1024]{1,0:T(8,128)} %res.2) | copy-start | bytes 1572868
  111.8 8.6 %copy-start.19 = (f32[1024]{0:T(1024)S(1)}, f32[1024]{0:T(1024)}, u32[]{:S(2)}) copy-start(f32[1024]{0:T(1024)} %param.21) | copy-start | bytes 12292
  114.9 18.8 %collective-permute-start.15 = (bf16[128,1024]{1,0:T(8,128)(2,1)S(1)}, bf16[128,1024]{1,0:T(8,128)(2,1)S(1)}, u32[]{:S(2)}, u32[]{:S(2)}) collective-permute-start(bf16[128,1024]{1,0:T(8,128)(2,1)S(1)} %get-tuple-element.99), channel_id=1, source_target_pairs={{0,1},{1,0},{2,3},{3,2},{4,5},{5,4},{6,7},{7,6},{8,9},{9,8},{10,11... | collective-permute-start | bytes 786440 | tf_op jit(solution)/shard_map/ppermute | solution.py:456
  122.1 1.3 collective-permute-start.17
  122.2 21.4 %collective-permute-start.22 = (bf16[512,1024]{1,0:T(8,128)(2,1)S(1)}, bf16[512,1024]{1,0:T(8,128)(2,1)S(1)}, u32[]{:S(2)}, u32[]{:S(2)}) collective-permute-start(bf16[512,1024]{1,0:T(8,128)(2,1)S(1)} %get-tuple-element.120), channel_id=1, source_target_pairs={{0,2},{2,0},{4,6},{6,4},{8,10},{10,8},{12,14},{14,12},{16,18},{18,... | collective-permute-start | bytes 3145736 | tf_op jit(solution)/shard_map/ppermute | solution.py:453
  123.5 4.3 %collective-permute-start.18 = (f32[16,1024]{1,0:T(8,128)S(1)}, f32[16,1024]{1,0:T(8,128)S(1)}, u32[]{:S(2)}, u32[]{:S(2)}) collective-permute-start(f32[16,1024]{1,0:T(8,128)S(1)} %add.136), channel_id=1, source_target_pairs={{0,4},{2,6},{4,0},{6,2},{8,12},{10,14},{12,8},{14,10},{16,20},{18,... | collective-permute-start | bytes 196616 | tf_op jit(solution)/shard_map/ppermute | solution.py:453
  127.8 4.3 %collective-permute-start.19 = (f32[16,1024]{1,0:T(8,128)S(1)}, f32[16,1024]{1,0:T(8,128)S(1)}, u32[]{:S(2)}, u32[]{:S(2)}) collective-permute-start(f32[16,1024]{1,0:T(8,128)S(1)} %add.137), channel_id=1, source_target_pairs={{0,8},{2,10},{4,12},{6,14},{8,0},{10,2},{12,4},{14,6},{16,24},{18,... | collective-permute-start | bytes 196616 | tf_op jit(solution)/shard_map/ppermute | solution.py:453
  128.2 16.8 %collective-permute-start.26 = (bf16[512,1408]{1,0:T(8,128)(2,1)S(1)}, bf16[512,1408]{1,0:T(8,128)(2,1)S(1)}, u32[]{:S(2)}, u32[]{:S(2)}) collective-permute-start(bf16[512,1408]{1,0:T(8,128)(2,1)S(1)} %get-tuple-element.122), channel_id=1, source_target_pairs={{0,2},{2,0},{4,6},{6,4},{8,10},{10,8},{12,14},{14,12},{16,18},{18,... | collective-permute-start | bytes 4325384 | tf_op jit(solution)/shard_map/ppermute | solution.py:453
  128.2 15.7 %collective-permute-start.31 = (bf16[512,1024]{1,0:T(8,128)(2,1)S(1)}, bf16[512,1024]{1,0:T(8,128)(2,1)S(1)}, u32[]{:S(2)}, u32[]{:S(2)}) collective-permute-start(bf16[512,1024]{1,0:T(8,128)(2,1)S(1)} %get-tuple-element.102), channel_id=1, source_target_pairs={{0,2},{2,0},{4,6},{6,4},{8,10},{10,8},{12,14},{14,12},{16,18},{18,... | collective-permute-start | bytes 3145736 | tf_op jit(solution)/shard_map/ppermute | solution.py:453
  132.2 5.7 %collective-permute-start.20 = (f32[16,1024]{1,0:T(8,128)S(1)}, f32[16,1024]{1,0:T(8,128)S(1)}, u32[]{:S(2)}, u32[]{:S(2)}) collective-permute-start(f32[16,1024]{1,0:T(8,128)S(1)} %add.138), channel_id=1, source_target_pairs={{0,16},{2,18},{4,20},{6,22},{8,24},{10,26},{12,28},{14,30},{16,0},... | collective-permute-start | bytes 196616 | tf_op jit(solution)/shard_map/ppermute | solution.py:453
  137.9 4.0 %collective-permute-start.21 = (f32[8,1024]{1,0:T(8,128)S(1)}, f32[8,1024]{1,0:T(8,128)S(1)}, u32[]{:S(2)}, u32[]{:S(2)}) collective-permute-start(f32[8,1024]{1,0:T(8,128)S(1)} %slice.246), channel_id=1, source_target_pairs={{0,1},{1,0},{2,3},{3,2},{4,5},{5,4},{6,7},{7,6},{8,9},{9,8},{10,11... | collective-permute-start | bytes 98312 | tf_op jit(solution)/shard_map/ppermute | solution.py:456
  143.8 12.4 %collective-permute-start.23 = (bf16[256,1024]{1,0:T(8,128)(2,1)S(1)}, bf16[256,1024]{1,0:T(8,128)(2,1)S(1)}, u32[]{:S(2)}, u32[]{:S(2)}) collective-permute-start(bf16[256,1024]{1,0:T(8,128)(2,1)S(1)} %bitcast.78), channel_id=1, source_target_pairs={{0,8},{2,10},{4,12},{6,14},{8,0},{10,2},{12,4},{14,6},{16,24},{18,... | collective-permute-start | bytes 1572872 | tf_op jit(solution)/shard_map/ppermute | solution.py:453
  144.3 14.9 %collective-permute-start.32 = (bf16[256,1024]{1,0:T(8,128)(2,1)S(1)}, bf16[256,1024]{1,0:T(8,128)(2,1)S(1)}, u32[]{:S(2)}, u32[]{:S(2)}) collective-permute-start(bf16[256,1024]{1,0:T(8,128)(2,1)S(1)} %get-tuple-element.179), channel_id=1, source_target_pairs={{0,4},{2,6},{4,0},{6,2},{8,12},{10,14},{12,8},{14,10},{16,20},{18,... | collective-permute-start | bytes 1572872 | tf_op jit(solution)/shard_map/ppermute | solution.py:453
  145.3 25.1 %collective-permute-start.27 = (bf16[256,1408]{1,0:T(8,128)(2,1)S(1)}, bf16[256,1408]{1,0:T(8,128)(2,1)S(1)}, u32[]{:S(2)}, u32[]{:S(2)}) collective-permute-start(bf16[256,1408]{1,0:T(8,128)(2,1)S(1)} %get-tuple-element.177), channel_id=1, source_target_pairs={{0,4},{2,6},{4,0},{6,2},{8,12},{10,14},{12,8},{14,10},{16,20},{18,... | collective-permute-start | bytes 2162696 | tf_op jit(solution)/shard_map/ppermute | solution.py:453
  156.4 16.7 %collective-permute-start.24 = (bf16[128,1024]{1,0:T(8,128)(2,1)S(1)}, bf16[128,1024]{1,0:T(8,128)(2,1)S(1)}, u32[]{:S(2)}, u32[]{:S(2)}) collective-permute-start(bf16[128,1024]{1,0:T(8,128)(2,1)S(1)} %bitcast.79), channel_id=1, source_target_pairs={{0,16},{2,18},{4,20},{6,22},{8,24},{10,26},{12,28},{14,30},{16,0},... | collective-permute-start | bytes 786440 | tf_op jit(solution)/shard_map/ppermute | solution.py:453
  159.4 14.5 %collective-permute-start.33 = (bf16[128,1024]{1,0:T(8,128)(2,1)S(1)}, bf16[128,1024]{1,0:T(8,128)(2,1)S(1)}, u32[]{:S(2)}, u32[]{:S(2)}) collective-permute-start(bf16[128,1024]{1,0:T(8,128)(2,1)S(1)} %get-tuple-element.183), channel_id=1, source_target_pairs={{0,8},{2,10},{4,12},{6,14},{8,0},{10,2},{12,4},{14,6},{16,24},{18,... | collective-permute-start | bytes 786440 | tf_op jit(solution)/shard_map/ppermute | solution.py:453
  170.6 9.4 %collective-permute-start.28 = (bf16[128,1408]{1,0:T(8,128)(2,1)S(1)}, bf16[128,1408]{1,0:T(8,128)(2,1)S(1)}, u32[]{:S(2)}, u32[]{:S(2)}) collective-permute-start(bf16[128,1408]{1,0:T(8,128)(2,1)S(1)} %get-tuple-element.181), channel_id=1, source_target_pairs={{0,8},{2,10},{4,12},{6,14},{8,0},{10,2},{12,4},{14,6},{16,24},{18,... | collective-permute-start | bytes 1081352 | tf_op jit(solution)/shard_map/ppermute | solution.py:453
  173.2 10.4 %collective-permute-start.25 = (bf16[64,1024]{1,0:T(8,128)(2,1)S(1)}, bf16[64,1024]{1,0:T(8,128)(2,1)S(1)}, u32[]{:S(2)}, u32[]{:S(2)}) collective-permute-start(bf16[64,1024]{1,0:T(8,128)(2,1)S(1)} %fusion.6), channel_id=1, source_target_pairs={{0,4},{2,6},{4,0},{6,2},{8,12},{10,14},{12,8},{14,10},{16,20},{18,... | collective-permute-start | bytes 393224 | tf_op jit(solution)/shard_map/ppermute | solution.py:453
  174.0 16.5 %collective-permute-start.34 = (bf16[64,1024]{1,0:T(8,128)(2,1)S(1)}, bf16[64,1024]{1,0:T(8,128)(2,1)S(1)}, u32[]{:S(2)}, u32[]{:S(2)}) collective-permute-start(bf16[64,1024]{1,0:T(8,128)(2,1)S(1)} %fusion.8), channel_id=1, source_target_pairs={{0,16},{2,18},{4,20},{6,22},{8,24},{10,26},{12,28},{14,30},{16,0},... | collective-permute-start | bytes 393224 | tf_op jit(solution)/shard_map/ppermute | solution.py:453
  180.1 8.9 %collective-permute-start.29 = (bf16[64,1408]{1,0:T(8,128)(2,1)S(1)}, bf16[64,1408]{1,0:T(8,128)(2,1)S(1)}, u32[]{:S(2)}, u32[]{:S(2)}) collective-permute-start(bf16[64,1408]{1,0:T(8,128)(2,1)S(1)} %get-tuple-element.186), channel_id=1, source_target_pairs={{0,16},{2,18},{4,20},{6,22},{8,24},{10,26},{12,28},{14,30},{16,0},... | collective-permute-start | bytes 540680 | tf_op jit(solution)/shard_map/ppermute | solution.py:453
  189.7 3.9 %collective-permute-start.30 = (f32[32,256]{1,0:T(8,128)S(1)}, f32[32,256]{1,0:T(8,128)S(1)}, u32[]{:S(2)}, u32[]{:S(2)}) collective-permute-start(f32[32,256]{1,0:T(8,128)S(1)} %get-tuple-element.125), channel_id=1, source_target_pairs={{0,1},{1,0},{2,3},{3,2},{4,5},{5,4},{6,7},{7,6},{8,9},{9,8},{10,11... | collective-permute-start | bytes 98312 | tf_op jit(solution)/shard_map/ppermute | solution.py:456

commit v3 on v2

--- a/solution.py
+++ b/solution.py
@@ -128,7 +128,7 @@
     return jnp.where(mask, jnp.exp(cum[:, h : h + 1] - cum_t[h : h + 1, :]), 0.0)
 
 
-def fwd_body(width, nrm, w1a, w1b, link, segc, segr, cx, cxb, cbc, cbcb, dtb, alog,
+def fwd_body(width, nrm, w1a, w1b, cols, segr, cx, cxb, cbc, cbcb, dtb, alog,
              xpre_o, xc_o, y_o, bcpre_o, bcc_o, dt_o, dec_o):
     inner = xc_o.shape[1]
     state = bcc_o.shape[1] // 2
@@ -140,14 +140,14 @@
     wide = 2 * LANES
     for c in range(inner // wide):
         xpre_o[:, c * wide : (c + 1) * wide] = paired(x, w1, slice(c * wide, (c + 1) * wide))
-    lk = link[...]
+    lk = cols[:, :SEG]
     for c in range(2 * state // LANES):
         at = slice(c * LANES, (c + 1) * LANES)
         bcc_o[:, at] = conv(bcpre_o[:, at], cbc[:, at], cbcb[:, at], lk)
     bs = silu(bcc_o[:, :state])
     cs = silu(bcc_o[:, state:])
     _, step, _, cum, cum_t, mask, grow, coef = prepare(
-        dt_o[...], dtb[...], alog[...], segc[...], segr[...]
+        dt_o[...], dtb[...], alog[...], cols[:, SEG : SEG + 1], segr[...]
     )
     scores = [
         dot_nt(cs[k * SPAN : (k + 1) * SPAN], bs[k * SPAN : (k + 1) * SPAN], HI) for k in range(2)
@@ -188,10 +188,10 @@
     return jnp.broadcast_to(rows[:1], (LANES, rows.shape[1])).T[:, :1]
 
 
-def dmix_body(cot, outa, outb, live, dm_o):
+def dmix_body(cot, outa, outb, cols, dm_o):
     wide = 2 * LANES
     x = cot[...]
-    lv = live[...]
+    lv = cols[:, LIVE : LIVE + 1]
     for c in range(dm_o.shape[1] // wide):
         at = slice(c * wide, (c + 1) * wide)
         dm_o[:, at] = paired(x, (outa, outb), at) * lv
@@ -215,12 +215,12 @@
     sums_o[8:] = as_rows(jnp.sum(dots, axis=1, keepdims=True))
 
 
-def mix_body(full, g_r, sums, sums2, gain, live, cot_t, keep_o, send_o, mixed):
+def mix_body(full, g_r, sums, sums2, gain, cols, cot_t, keep_o, send_o, mixed):
     inv = lax.rsqrt(as_col(sums[:8] + sums2[:8]) / full + epsilon)
     wide = 2 * LANES
     for c in range(g_r.shape[1] // LANES):
         at = slice(c * LANES, (c + 1) * LANES)
-        mixed[:, at] = (g_r[:, at] * inv * gain[:, at] * live[...]).astype(bf16)
+        mixed[:, at] = (g_r[:, at] * inv * gain[:, at] * cols[:, LIVE : LIVE + 1]).astype(bf16)
     half = keep_o.shape[0]
     for c in range(g_r.shape[1] // wide):
         at = slice(c * wide, (c + 1) * wide)
@@ -262,16 +262,15 @@
         keep_o[:, at] = dot_nn(nrm_t[:half], dz_o[:, at]).astype(bf16)
 
 
-def bwd_body(width, nrm_t, dy_r, xpre_r, xc_r, y_r, bcpre_r, bcc_r, dt_r, dec_r, link, segc, segr, cx,
-             cbc, dtb, alog, dsk, dx_o, sm_o, keep_o, send_o, dc_s):
+def bwd_body(width, nrm_t, dy_r, xpre_r, xc_r, y_r, bcpre_r, bcc_r, dt_r, dec_r, cols, segr, cx,
+             cbc, dtb, alog, dsk, dx_o, dbc_o, sm_o, keep_o, send_o, dc_s):
     inner = xc_r.shape[1]
     state = bcc_r.shape[1] // 2
-    lk = link[...]
+    lk = cols[:, :SEG]
+    segc = cols[:, SEG : SEG + 1]
     bs = silu(bcc_r[:, :state])
     cs = silu(bcc_r[:, state:])
-    v, step, logd, _, _, _, grow, coef = prepare(
-        dt_r[...], dtb[...], alog[...], segc[...], segr[...]
-    )
+    v, step, logd, _, _, _, grow, coef = prepare(dt_r[...], dtb[...], alog[...], segc, segr[...])
     scores = [
         dot_nt(cs[k * SPAN : (k + 1) * SPAN], bs[k * SPAN : (k + 1) * SPAN], HI) for k in range(2)
     ]
@@ -346,7 +345,7 @@
         for k, piece in enumerate(dw):
             sm_o[k : k + 1, at] = piece
         sm_o[4:5, at] = db
-    upper = (iota((rows_t, rows_t), 0) <= iota((rows_t, rows_t), 1)) & (segc[...] == segr[...])
+    upper = (iota((rows_t, rows_t), 0) <= iota((rows_t, rows_t), 1)) & (segc == segr[...])
     dlog = dot_nn(upper.astype(f32), dcum, HI)
     ddt = (dstep - dlog * jnp.exp(alog[...])) * jax.nn.sigmoid(v)
     dx_o[:, inner + 2 * state :] = ddt.astype(bf16)
@@ -369,6 +368,7 @@
             dc_s[:, at] * silu_slope(bcc_r[:, at]), bcpre_r[:, at], cbc[:, at], lk
         )
         dx_o[:, inner + c * LANES : inner + (c + 1) * LANES] = dpre.astype(bf16)
+        dbc_o[:, at] = dpre.astype(bf16)
         for k, piece in enumerate(dw):
             sm_o[8 + k : 9 + k, at] = piece
         sm_o[12:13, at] = db
@@ -391,16 +391,26 @@
     own_o[...] = all_s[rows_of(side[0], count), :]
 
 
-def last_body(side, keep, other, x_o, dt_o, own_o, send_o, all_s):
-    inner = x_o.shape[1]
-    count, two_state = own_o.shape
-    x_o[...] = keep[:, :inner].astype(f32) + other[:, :inner].astype(f32)
-    all_s[...] = keep[:, inner:].astype(f32) + other[:, inner:].astype(f32)
-    dt_o[...] = all_s[:, two_state : two_state + dt_o.shape[1]]
-    low = all_s[:count, :two_state]
-    top = all_s[count:, :two_state]
-    own_o[...] = jnp.where(side[0] == 0, low, top)
-    send_o[...] = jnp.where(side[0] == 0, top, low)
+def last_body(keep, other, bc_o, dt_o):
+    two_state = bc_o.shape[1]
+    count, heads = keep.shape[0], dt_o.shape[1]
+    bc_o[...] = keep[:, :two_state].astype(f32) + other[:, :two_state].astype(f32)
+    dt = keep[:, two_state:].astype(f32) + other[:, two_state:].astype(f32)
+    dt_o[:count] = dt[:, :heads]
+    dt_o[count:] = pltpu.roll(dt, LANES // 2, 1)[:, :heads]
+
+
+def few_body(few, other, norm_o, x_o, xb_o, bc_o, bcb_o, gain_o, heads_o):
+    taps = x_o.shape[0]
+    width = bc_o.shape[1]
+    shared = few[8:16] + other[...]
+    norm_o[...] = shared[:1]
+    bc_o[...] = shared[1 : 1 + taps, :width]
+    bcb_o[...] = shared[1 + taps : 2 + taps, :width]
+    x_o[...] = few[:taps]
+    xb_o[...] = few[taps : taps + 1]
+    gain_o[...] = few[5:6]
+    heads_o[...] = few[7:8, : 3 * LANES]
 
 
 def restore(v, place_t):
@@ -422,11 +432,49 @@
     ig_o[...] = cot[...] + inv * dg - r * (inv * inv * inv * inner)
 
 
+SEG = 4
+LIVE = 5
+
+
+def prep_body(taps, count, segr, cols_o):
+    tokens = segr.shape[1]
+    seg = jnp.broadcast_to(segr[...], (LANES, tokens)).T
+    row = iota(seg.shape, 0)
+    lane = iota(seg.shape, 1)
+    out = jnp.where(lane == SEG, seg, 0.0)
+    out = jnp.where((lane == LIVE) & (row < count[0]), 1.0, out)
+    for lag in range(taps):
+        moved = pltpu.roll(seg, lag, 0) if lag else seg
+        out = jnp.where((lane == lag) & (row >= lag) & (seg == moved), 1.0, out)
+    cols_o[...] = out
+
+
 def join_body(side, own, other, all_o, turned_o):
     half = own.shape[0]
     all_o[rows_of(side[0], half), :] = own[...]
     all_o[rows_of(1 - side[0], half), :] = other[...]
     turned_o[...] = all_o[...].T
+
+
+def order_body(turned, picks, halves_o):
+    halves_o[...] = dot_nn(picks[...], turned[...]).astype(bf16)
+
+
+def bpart_body(side, ordered, dx, theirs, keep_o, send_o):
+    two_state = theirs.shape[1]
+    inner = dx.shape[1] - two_state - LANES
+    count = keep_o.shape[0]
+    whole = 2 * count
+    rows = ordered[rows_of(side[0], whole), :]
+    own = dot_nn(rows, dx[:, inner : inner + two_state]) + dot_nn(rows, theirs[...])
+    lane = iota((whole, LANES), 1)
+    ddt = dx[:, inner + two_state :]
+    first = dot_nn(ordered[:whole], ddt)
+    second = dot_nn(ordered[whole:], ddt)
+    dt = jnp.where(lane < LANES // 2, first, pltpu.roll(second, LANES // 2, 1))
+    for out, at in ((keep_o, slice(0, count)), (send_o, slice(count, whole))):
+        out[:, :two_state] = own[at].astype(bf16)
+        out[:, two_state:] = dt[at].astype(bf16)
 
 
 def cat_body(first, second, out_o):
@@ -507,8 +555,8 @@
 
         pad = LANES - heads
         w1s = jnp.concatenate([x_weight, bc_weight, jnp.pad(dt_weight, ((0, 0), (0, pad)))], 1)
-        outa, outb, m1 = gather(out_weight.T, None)
-        w1a, w1b, m2 = gather(w1s, m1[0])
+        w1a, w1b, m1 = gather(w1s, None)
+        outa, outb, m2 = gather(out_weight.T, m1[1])
         wza, wzb, _ = gather(z_weight, m2[0])
 
         spot = jnp.arange(width_d, dtype=jnp.int32)
@@ -520,17 +568,11 @@
         place = (spot[:, None] == source[None, :]).astype(bf16)
         place_t = (source[:, None] == spot[None, :]).astype(bf16)
 
-        spots = jnp.arange(tokens)
-        links = [jnp.ones((tokens,), f32)]
-        for lag in range(1, conv_x.shape[0]):
-            moved = jnp.concatenate(
-                [jnp.full((lag,), -1, jnp.int32), segment_ids[: tokens - lag]]
-            )
-            links.append((segment_ids == moved).astype(f32))
-        link = jnp.stack(links, 1)
-        segc = segment_ids[:, None]
-        segr = segment_ids[None, :]
-        live = (spots < live_counts[0]).astype(f32)[:, None]
+        segr = segment_ids.astype(f32)[None, :]
+        part = shard // nt
+        line = jnp.arange(width_d, dtype=jnp.int32)
+        picked = (line % (n * part)) // part * shard + line // (n * part) * part + line % part
+        picks = (picked[:, None] == line[None, :]).astype(bf16)
         dtb = jnp.pad(dt_bias, (0, pad))[None, :]
         alog = jnp.pad(a_log, (0, pad))[None, :]
         dsk = jnp.repeat(d_skip, head_width)[None, :]
@@ -539,17 +581,22 @@
         cxb = conv_x_bias[None, :]
         cbcb = conv_bc_bias[None, :]
         where = side.astype(jnp.int32)[None]
-        (residual, link, segc, segr, live, dtb, alog, dsk, gain, gg, cxb, cbcb, where, place,
-         place_t) = lax.optimization_barrier(
-            (residual, link, segc, segr, live, dtb, alog, dsk, gain, gg, cxb, cbcb, where, place,
-             place_t)
-        )
+        (residual, segr, dtb, alog, dsk, gain, gg, cxb, cbcb, where, place, place_t,
+         picks) = lax.optimization_barrier(
+            (residual, segr, dtb, alog, dsk, gain, gg, cxb, cbcb, where, place, place_t, picks)
+        )
+
+        def prep(*a):
+            return prep_body(conv_x.shape[0], *a)
+
+        (cols,) = call(0.5, prep, [((tokens, LANES), f32)], live_counts, segr, scalars=1)
         nrm_half, cot_half = call(
             1.5, head_body, [((half, width_d), bf16)] * 2, residual, cotangent, gain, place
         )
         joined = [((tokens, width_d), bf16), ((width_d, tokens), bf16)]
         nrm_other = cross(nrm_half)
         nrm, nrm_t = call(1.0, join_body, joined, where, nrm_half, nrm_other, scalars=1)
+        (ordered,) = call(1.0, order_body, [((width_d, tokens), bf16)], nrm_t, picks)
         cot_other = cross(cot_half)
         cot, cot_t = call(1.0, join_body, joined, where, cot_half, cot_other, scalars=1)
 
@@ -558,12 +605,12 @@
         def fwd(*a):
             return fwd_body(head_width, *a)
 
-        (dm,) = call(3.0, dmix_body, [big], cot, outa, outb, live)
+        (dm,) = call(3.0, dmix_body, [big], cot, outa, outb, cols)
         xpre, xc, y, bcpre, bcc, dtp, dec = call(
             7.0, fwd,
             [big, big, big, ((tokens, two_state), f32), ((tokens, two_state), f32),
              ((tokens, LANES), f32), ((2 * heads, SPAN, SPAN), f32)],
-            nrm, w1a, w1b, link, segc, segr, conv_x, cxb, conv_bc, cbcb, dtb, alog,
+            nrm, w1a, w1b, cols, segr, conv_x, cxb, conv_bc, cbcb, dtb, alog,
         )
         z, g, sums = call(
             5.0, gate_body, [big, big, ((16, tokens), f32)],
@@ -579,7 +626,7 @@
         out_keep, out_send, mixed = call(
             4.0, mix,
             [((cut, inner), bf16), ((cut, inner), bf16), ((tokens, inner), bf16)],
-            g, sums, sums2, gg, live, cot_t,
+            g, sums, sums2, gg, cols, cot_t,
         )
         blk_own, blk_send = call(2.5, blk_body, apart, where, mixed, outa, outb, scalars=1)
         out_sum = plus(*scatter(out_keep, out_send, near))
@@ -604,20 +651,24 @@
             return bwd_body(head_width, *a)
 
         wide = w1a.shape[1]
-        dx, small, x_keep, x_send = call(
-            14.0, back,
-            [((tokens, wide), bf16), ((16, inner), f32), ((cut, wide), bf16), ((cut, wide), bf16)],
-            nrm_t, dy, xpre, xc, y, bcpre, bcc, dtp, dec, link, segc, segr, conv_x, conv_bc, dtb, alog,
+        dx, dbc, small, x_keep, x_send = call(
+            8.0, back,
+            [((tokens, wide), bf16), ((tokens, two_state), bf16), ((16, inner), f32),
+             ((cut, inner), bf16), ((cut, inner), bf16)],
+            nrm_t, dy, xpre, xc, y, bcpre, bcc, dtp, dec, cols, segr, conv_x, conv_bc, dtb, alog,
             dsk,
             scratch=[pltpu.VMEM((tokens, two_state), f32)],
         )
-        x_weight_grad, dt_weight_grad, bc_own, bc_send = call(
-            1.5, last_body,
-            [((shard, inner), f32), ((shard, heads), f32)] + [((shard // nt, two_state), f32)] * 2,
-            where, *scatter(x_keep, x_send, near), scalars=1,
-            scratch=[pltpu.VMEM((shard, wide - inner), f32)],
-        )
-        bc_weight_grad = bc_own + cross(bc_send)
+        x_weight_grad = plus(*scatter(x_keep, x_send, near))
+        small_part = ((cut * part // shard, wide - inner), bf16)
+        b_keep, b_send = call(
+            1.0, bpart_body, [small_part] * 2, where, ordered, dx, cross(dbc),
+            scalars=1,
+        )
+        bc_weight_grad, dt_weight_grad = call(
+            0.5, last_body, [((part, two_state), f32), ((shard, heads), f32)],
+            *scatter(b_keep, b_send, near),
+        )
 
         dn_own, dn_send = call(
             5.0, dn_body, apart, where, dz, wza, wzb, dx, w1a, w1b, scalars=1,
@@ -635,24 +686,29 @@
         few = jnp.concatenate([few[:8], few[13:14], few[8:13], few[:2]], 0)
         for bit in bits:
             few = few + swap(few, bit)
-        shared = few[8:16]
-        shared = shared + cross(shared)
+        taps = conv_x.shape[0]
+        norm_sum, cx_sum, cxb_sum, cbc_sum, cbcb_sum, gain_sum, by_head = call(
+            0.5, few_body,
+            [((1, width_d), f32), ((taps, inner), f32), ((1, inner), f32), ((taps, two_state), f32),
+             ((1, two_state), f32), ((1, inner), f32), ((1, 3 * LANES), f32)],
+            few, cross(few[8:16]),
+        )
         return (
             block_out,
             input_grad,
-            shared[0],
+            norm_sum[0],
             z_weight_grad,
             x_weight_grad,
             bc_weight_grad,
             dt_weight_grad,
-            few[:4],
-            few[4],
-            shared[1:5, :two_state],
-            shared[5, :two_state],
-            few[7, :heads],
-            few[7, LANES : LANES + heads],
-            few[7, 2 * LANES : 2 * LANES + heads],
-            few[5],
+            cx_sum,
+            cxb_sum[0],
+            cbc_sum,
+            cbcb_sum[0],
+            by_head[0, :heads],
+            by_head[0, LANES : LANES + heads],
+            by_head[0, 2 * LANES : 2 * LANES + heads],
+            gain_sum[0],
             out_sum.T,
         )
 

time: 195 us -> 198 us (1.015)
  starting transfers between devices: 33 us -> 46 us
  waiting for transfers between devices: 98.7 us -> 88.9 us
  other arithmetic: 8.98 us -> 11.2 us
    ppermute x28 -> x32, waiting for transfers between devices: 88.4 us -> 68.1 us  [swap(): return lax.ppermute(v, 'dp', [(i, i ^ bit) for i in range(n)])]
    ppermute x28 -> x32, starting transfers between devices: 26.6 us -> 37.9 us  [swap(): return lax.ppermute(v, 'dp', [(i, i ^ bit) for i in range(n)])]
    ppermute x7, waiting for transfers between devices: 10.3 us -> 20.8 us  [cross(): return lax.ppermute(v, 'tensor', [(0, 1), (1, 0)])]
    unnamed x50 -> x44, local copies, waits for them, and re-layouts: 3.54 us -> 7.19 us
    slice x6 -> x1, local copies, waits for them, and re-layouts: 2.97 us -> 0.01 us  [whole(): few[8:16]]
    convert_element_type x6 -> x8, other arithmetic: 1.48 us -> 3.8 us  [scatter(): keep = plus(*pick[0]).astype(bf16)]
    optimization_barrier x2 -> x0, local copies, waits for them, and re-layouts: 2.28 us -> none  [whole(): lax.optimization_barrier((residual, link, segc, segr, live, dtb, alog, ds...]
    pallas_call x23 -> x27, Pallas kernels: 40.9 us -> 39.4 us  [call(): pl.pallas_call(body, out_shape=[jax.ShapeDtypeStruct(s, d) for s, d in ou...]
  transfers between devices with their start and end apart: 35 -> 39, of which waited for: 21 -> 19; matrix products, arithmetic and copies ran while one was open for 9% -> 7% of each run, Pallas kernels for 12% -> 12%
where the time goes in v3:
time: 198 us
  waiting for transfers between devices  88.9 us (45%)
  starting transfers between devices  46 us (23%)
  Pallas kernels  39.4 us (20%)
  other arithmetic  11.2 us (6%)
  local copies, waits for them, and re-layouts  10.5 us (5%)
    ppermute x32, waiting for transfers between devices, swap(): return lax.ppermute(v, 'dp', [(i, i ^ bit) for i in range(n)])  68.1 us
    pallas_call x27, Pallas kernels, call(): pl.pallas_call(body, out_shape=[jax.ShapeDtypeStruct(s, d) for s, d in ou...  39.4 us
    ppermute x32, starting transfers between devices, swap(): return lax.ppermute(v, 'dp', [(i, i ^ bit) for i in range(n)])  37.9 us
    ppermute x7, waiting for transfers between devices, cross(): return lax.ppermute(v, 'tensor', [(0, 1), (1, 0)])  20.8 us
    ppermute x7, starting transfers between devices, cross(): return lax.ppermute(v, 'tensor', [(0, 1), (1, 0)])  8.11 us
    unnamed x44, local copies, waits for them, and re-layouts  7.19 us
  transfers between devices with their start and end apart: 39, of which 19 were waited for; matrix products, arithmetic and copies ran while one was open for 7% of the time, Pallas kernels for 12%

profile of v3, /device:TPU:0, one launch (start us, length us, event | category | flops | bytes accessed | tf_op | source)
XLA Modules:
  0.0 197.8 jit_solution(7335066458324804894)
XLA Ops:
  1.5 0.9 fusion.11.first
  2.4 4.1 %collective-permute-start.1 = (bf16[64,1408]{1,0:T(8,128)(2,1)S(1)}, bf16[64,1408]{1,0:T(8,128)(2,1)S(1)}, u32[]{:S(2)}, u32[]{:S(2)}) collective-permute-start(bf16[64,1408]{1,0:T(8,128)(2,1)S(1)} %fusion.11.first), channel_id=1, source_target_pairs={{0,16},{2,18},{4,20},{6,22},{8,24},{10,26},{12,28},{14,30},{16,0},... | collective-permute-start | bytes 540680 | tf_op jit(solution)/shard_map/ppermute | solution.py:501
  6.5 8.4 %collective-permute-done.1.second = bf16[64,1408]{1,0:T(8,128)(2,1)S(1)} collective-permute-done((bf16[64,1408]{1,0:T(8,128)(2,1)S(1)}, bf16[64,1408]{1,0:T(8,128)(2,1)S(1)}, u32[]{:S(2)}, u32[]{:S(2)}) %collective-permute-start.1) | collective-permute-done | bytes 180256 | tf_op jit(solution)/shard_map/ppermute | solution.py:501
  15.8 8.9 %collective-permute-done.2.second = bf16[128,1408]{1,0:T(8,128)(2,1)S(1)} collective-permute-done((bf16[128,1408]{1,0:T(8,128)(2,1)S(1)}, bf16[128,1408]{1,0:T(8,128)(2,1)S(1)}, u32[]{:S(2)}, u32[]{:S(2)}) %collective-permute-start.2) | collective-permute-done | bytes 360480 | tf_op jit(solution)/shard_map/ppermute | solution.py:501
  24.6 3.1 %collective-permute-start.3 = (bf16[64,1024]{1,0:T(8,128)(2,1)}, bf16[64,1024]{1,0:T(8,128)(2,1)S(1)}, u32[]{:S(2)}, u32[]{:S(2)}) collective-permute-start(bf16[64,1024]{1,0:T(8,128)(2,1)} %bitcast.53), channel_id=1, source_target_pairs={{0,16},{2,18},{4,20},{6,22},{8,24},{10,26},{12,28},{14,30},{16,0},... | collective-permute-start | bytes 393224 | tf_op jit(solution)/shard_map/ppermute | solution.py:501
  27.8 1.6 collective-permute-start.8
  29.4 4.5 %collective-permute-done.3.second = bf16[64,1024]{1,0:T(8,128)(2,1)S(1)} collective-permute-done((bf16[64,1024]{1,0:T(8,128)(2,1)}, bf16[64,1024]{1,0:T(8,128)(2,1)S(1)}, u32[]{:S(2)}, u32[]{:S(2)}) %collective-permute-start.3) | collective-permute-done | bytes 131104 | tf_op jit(solution)/shard_map/ppermute | solution.py:501
  33.9 0.9 collective-permute-start.11
  34.8 6.5 %collective-permute-done.11.second = bf16[128,1024]{1,0:T(8,128)(2,1)S(1)} collective-permute-done((bf16[128,1024]{1,0:T(8,128)(2,1)S(1)}, bf16[128,1024]{1,0:T(8,128)(2,1)S(1)}, u32[]{:S(2)}, u32[]{:S(2)}) %collective-permute-start.11) | collective-permute-done | bytes 262176 | tf_op jit(solution)/shard_map/ppermute | solution.py:501
  41.3 1.6 collective-permute-start.12
  42.9 3.2 %collective-permute-start.4 = (bf16[64,1024]{1,0:T(8,128)(2,1)S(1)}, bf16[64,1024]{1,0:T(8,128)(2,1)S(1)}, u32[]{:S(2)}, u32[]{:S(2)}) collective-permute-start(bf16[64,1024]{1,0:T(8,128)(2,1)S(1)} %copy-done.13), channel_id=1, source_target_pairs={{0,16},{2,18},{4,20},{6,22},{8,24},{10,26},{12,28},{14,30},{16,0},... | collective-permute-start | bytes 393224 | tf_op jit(solution)/shard_map/ppermute | solution.py:501
  46.1 5.6 %collective-permute-done.4.second = bf16[64,1024]{1,0:T(8,128)(2,1)S(1)} collective-permute-done((bf16[64,1024]{1,0:T(8,128)(2,1)S(1)}, bf16[64,1024]{1,0:T(8,128)(2,1)S(1)}, u32[]{:S(2)}, u32[]{:S(2)}) %collective-permute-start.4) | collective-permute-done | bytes 131104 | tf_op jit(solution)/shard_map/ppermute | solution.py:501
  52.8 6.4 %collective-permute-done.5.second = bf16[128,1024]{1,0:T(8,128)(2,1)S(1)} collective-permute-done((bf16[128,1024]{1,0:T(8,128)(2,1)S(1)}, bf16[128,1024]{1,0:T(8,128)(2,1)S(1)}, u32[]{:S(2)}, u32[]{:S(2)}) %collective-permute-start.5) | collective-permute-done | bytes 262176 | tf_op jit(solution)/shard_map/ppermute | solution.py:501
  59.2 0.8 shard_map.301.first
  60.5 2.1 %shard_map.310.outa = bf16[512,1024]{1,0:T(8,128)(2,1)} custom-call(bf16[256,1024]{1,0:T(8,128)(2,1)S(1)} %shard_map.309.first, bf16[256,1024]{1,0:T(8,128)(2,1)} %collective-permute-done.12.second), custom_call_target="tpu_custom_call" | custom-call | flops 450000000 | bytes 1500000 | tf_op jit(solution)/shard_map/pallas_call | solution.py:31
  62.6 2.7 %fusion.1 = (bf16[1024,1024]{1,0:T(8,128)(2,1)S(1)}, bf16[1024,1024]{1,0:T(8,128)(2,1)}, bf16[1024,1024]{1,0:T(8,128)(2,1)}) fusion(s32[1024]{0:T(1024)S(1)} %fusion.38, s32[1024]{0:T(1024)S(1)} %fusion.36), kind=kLoop, calls=%fused_computation.4 | loop fusion | flops 6291456 | bytes 6299648 | tf_op jit(solution)/shard_map/convert_element_type | solution.py:569
  65.3 1.3 broadcast_in_dim.36
  68.1 1.6 copy-done.1
  69.7 1.0 copy-done.8
  70.7 1.0 copy-done.10
  72.6 1.6 collective-permute-start.10
  75.3 1.3 shard_map.302.wza
  76.8 5.0 %collective-permute-done.10.other = bf16[128,1024]{1,0:T(8,128)(2,1)S(1)} collective-permute-done((bf16[128,1024]{1,0:T(8,128)(2,1)S(1)}, bf16[128,1024]{1,0:T(8,128)(2,1)S(1)}, u32[]{:S(2)}, u32[]{:S(2)}) %collective-permute-start.10) | collective-permute-done | bytes 262176 | tf_op jit(solution)/shard_map/ppermute | solution.py:504
  82.0 4.9 %collective-permute-done.other = bf16[128,1024]{1,0:T(8,128)(2,1)S(1)} collective-permute-done((bf16[128,1024]{1,0:T(8,128)(2,1)S(1)}, bf16[128,1024]{1,0:T(8,128)(2,1)S(1)}, u32[]{:S(2)}, u32[]{:S(2)}) %collective-permute-start) | collective-permute-done | bytes 262176 | tf_op jit(solution)/shard_map/ppermute | solution.py:504
  87.2 2.3 %shard_map.311.dm_r.a_2_ = f32[256,1024]{1,0:T(8,128)S(1)} custom-call(bf16[256,1024]{1,0:T(8,128)(2,1)S(1)} %get-tuple-element.95.cot, bf16[512,1024]{1,0:T(8,128)(2,1)} %shard_map.310.outa, bf16[512,1024]{1,0:T(8,128)(2,1)} %collective-permute-done.13.outb, f32[256,128]{1,0:T(8,128)S(1)} %shard_map.305.a_3_.cols.a_4_.a_9_), custom_call_target="tpu_custom_call" | custom-call | flops 2700000000 | bytes 9000000 | tf_op jit(solution)/shard_map/pallas_call | solution.py:31
  89.6 4.9 %shard_map.306 = (f32[256,1024]{1,0:T(8,128)S(1)}, f32[256,1024]{1,0:T(8,128)S(1)}, f32[256,1024]{1,0:T(8,128)S(1)}, f32[256,256]{1,0:T(8,128)S(1)}, f32[256,256...) custom-call(bf16[256,1024]{1,0:T(8,128)(2,1)S(1)} %get-tuple-element.83.a_0_.nrm, ...), custom_call_target="tpu_custom_call" | custom-call | flops 6300000256 | bytes 21000000 | tf_op jit(solution)/shard_map/pallas_call | solution.py:31
  94.5 1.1 shard_map.312
  95.6 1.5 collective-permute-start.14
  97.9 1.5 collective-permute-done.14.a_2_.a_9_
  99.4 2.0 %shard_map.313 = (bf16[512,1024]{1,0:T(8,128)(2,1)S(1)}, bf16[512,1024]{1,0:T(8,128)(2,1)}, bf16[256,1024]{1,0:T(8,128)(2,1)S(1)}) custom-call(f32[256,1024]{1,0:T(8,128)S(1)} %get-tuple-element.97.a_0_.a_1_, f32[16,256]{1,0:T(8,128)S(1)} %get-tuple-element.98.a_1_.a_8_, f32[16,256]{1,0:T(8,128)S(1)} %collective-permute-done.14.a_2_.a_9_, ...), custom_call_target="tpu_custom_call" | custom-call | flops 3600000000 | bytes 12000000 | tf_op jit(solution)/shard_map/pallas_call | solution.py:31
  101.4 1.0 copy-done.2
  102.4 2.7 %shard_map.316 = (bf16[256,1024]{1,0:T(8,128)(2,1)S(1)}, f32[256,1024]{1,0:T(8,128)S(1)}, f32[1,1024]{1,0:T(1,128)S(1)}, bf16[512,1024]{1,0:T(8,128)(2,1)S(1)}, bf16[512,1024]{1,0:T(8,128)(2,1)}) custom-call(bf16[1024,256]{1,0:T(8,128)(2,1)S(1)} %get-tuple-element.106.a_0_.turned, f32[256,1024]{1,0:T(8,128)S(1)} %get-tuple-element.97.a_0_.a_1_, ...), custom_call_target="tpu_custom_call" | custom-call | flops 5400000000 | bytes 18000000 | tf_op jit(solution)/shard_map/pallas_call | solution.py:31
  105.1 1.0 copy-done.4
  106.0 8.9 %shard_map.317 = (bf16[256,1408]{1,0:T(8,128)(2,1)S(1)}, bf16[256,256]{1,0:T(8,128)(2,1)S(1)}, f32[16,1024]{1,0:T(8,128)S(1)}, bf16[512,1024]{1,0:T(8,128)(2,1)S(1)}, bf16[512,1024]{1,0:T(8,128)(2,1)}) custom-call(bf16[1024,256]{1,0:T(8,128)(2,1)S(1)} %get-tuple-element.106.a_0_.turned, f32[256,1024]{1,0:T(8,128)S(1)} %get-tuple-element.109.a_1_, ...), custom_call_target="tpu_custom_call" | custom-call | flops 7200000000 | bytes 24000000 | tf_op jit(solution)/shard_map/pallas_call | solution.py:31
  115.0 1.6 collective-permute-start.30
  116.5 3.0 %shard_map.318 = (f32[128,1024]{1,0:T(8,128)S(1)}, bf16[128,1024]{1,0:T(8,128)(2,1)S(1)}) custom-call(s32[1]{0:T(128)} %bitcast.7.side, bf16[256,1024]{1,0:T(8,128)(2,1)S(1)} %get-tuple-element.108.dz, bf16[512,1024]{1,0:T(8,128)(2,1)S(1)} %shard_map.302.wza, bf16[512,1024]{1,0:T(8,128)(2,1)S(1)} %collective-permute-done.7.wzb, ...), custom_call_target="tpu_custom_call" | custom-call | flops 4499999744 | bytes 15000000 | tf_op jit(solution)/shard_map/pallas_call | solution.py:31
  120.7 5.3 %collective-permute-done.16.other = bf16[128,1024]{1,0:T(8,128)(2,1)S(1)} collective-permute-done((bf16[128,1024]{1,0:T(8,128)(2,1)S(1)}, bf16[128,1024]{1,0:T(8,128)(2,1)S(1)}, u32[]{:S(2)}, u32[]{:S(2)}) %collective-permute-start.16) | collective-permute-done | bytes 262176 | tf_op jit(solution)/shard_map/ppermute | solution.py:504
  126.0 1.7 shard_map.319
  127.9 1.6 collective-permute-start.32
  129.5 1.2 collective-permute-start.18
  130.7 3.9 %collective-permute-done.18 = f32[16,1024]{1,0:T(8,128)S(1)} collective-permute-done((f32[16,1024]{1,0:T(8,128)S(1)}, f32[16,1024]{1,0:T(8,128)S(1)}, u32[]{:S(2)}, u32[]{:S(2)}) %collective-permute-start.18) | collective-permute-done | bytes 65568 | tf_op jit(solution)/shard_map/ppermute | solution.py:501
  134.6 1.4 collective-permute-start.19
  136.8 3.0 %shard_map.314 = (f32[128,1024]{1,0:T(8,128)S(1)}, bf16[128,1024]{1,0:T(8,128)(2,1)S(1)}) custom-call(s32[1]{0:T(128)} %bitcast.7.side, bf16[256,1024]{1,0:T(8,128)(2,1)S(1)} %get-tuple-element.100.mixed, bf16[512,1024]{1,0:T(8,128)(2,1)} %shard_map.310.outa, bf16[512,1024]{1,0:T(8,128)(2,1)} %collective-permute-done.13.outb), custom_call_target="tpu_custom_call" | custom-call | flops 2249999872 | bytes 7500000 | tf_op jit(solution)/shard_map/pallas_call | solution.py:31
  139.8 1.2 collective-permute-start.15
  141.5 3.0 %collective-permute-start.20 = (f32[16,1024]{1,0:T(8,128)S(1)}, f32[16,1024]{1,0:T(8,128)S(1)}, u32[]{:S(2)}, u32[]{:S(2)}) collective-permute-start(f32[16,1024]{1,0:T(8,128)S(1)} %add.196), channel_id=1, source_target_pairs={{0,16},{2,18},{4,20},{6,22},{8,24},{10,26},{12,28},{14,30},{16,0},... | collective-permute-start | bytes 196616 | tf_op jit(solution)/shard_map/ppermute | solution.py:501
  144.5 2.6 %collective-permute-done.15.other = bf16[128,1024]{1,0:T(8,128)(2,1)S(1)} collective-permute-done((bf16[128,1024]{1,0:T(8,128)(2,1)S(1)}, bf16[128,1024]{1,0:T(8,128)(2,1)S(1)}, u32[]{:S(2)}, u32[]{:S(2)}) %collective-permute-start.15) | collective-permute-done | bytes 262176 | tf_op jit(solution)/shard_map/ppermute | solution.py:504
  147.2 2.9 %collective-permute-start.34 = (bf16[32,384]{1,0:T(8,128)(2,1)S(1)}, bf16[32,384]{1,0:T(8,128)(2,1)S(1)}, u32[]{:S(2)}, u32[]{:S(2)}) collective-permute-start(bf16[32,384]{1,0:T(8,128)(2,1)S(1)} %get-tuple-element.170), channel_id=1, source_target_pairs={{0,16},{2,18},{4,20},{6,22},{8,24},{10,26},{12,28},{14,30},{16,0},... | collective-permute-start | bytes 73736 | tf_op jit(solution)/shard_map/ppermute | solution.py:501
  150.1 1.5 shard_map.315
  151.7 1.2 collective-permute-start.21
  154.1 1.5 collective-permute-done.21.other
  157.2 1.6 collective-permute-start.27
  158.8 1.2 add_convert_fusion.4
  160.0 1.7 collective-permute-start.23
  161.8 1.6 add_convert_fusion.1
  164.0 1.2 fusion.3
  165.2 6.8 %collective-permute-done.27 = bf16[256,1024]{1,0:T(8,128)(2,1)S(1)} collective-permute-done((bf16[256,1024]{1,0:T(8,128)(2,1)S(1)}, bf16[256,1024]{1,0:T(8,128)(2,1)S(1)}, u32[]{:S(2)}, u32[]{:S(2)}) %collective-permute-start.27) | collective-permute-done | bytes 524320 | tf_op jit(solution)/shard_map/ppermute | solution.py:501
  172.2 1.8 collective-permute-start.28
  174.0 2.0 %collective-permute-done.23 = bf16[256,1024]{1,0:T(8,128)(2,1)S(1)} collective-permute-done((bf16[256,1024]{1,0:T(8,128)(2,1)S(1)}, bf16[256,1024]{1,0:T(8,128)(2,1)S(1)}, u32[]{:S(2)}, u32[]{:S(2)}) %collective-permute-start.23) | collective-permute-done | bytes 524320 | tf_op jit(solution)/shard_map/ppermute | solution.py:501
  176.3 2.7 %collective-permute-done.36 = bf16[256,1024]{1,0:T(8,128)(2,1)S(1)} collective-permute-done((bf16[256,1024]{1,0:T(8,128)(2,1)S(1)}, bf16[256,1024]{1,0:T(8,128)(2,1)S(1)}, u32[]{:S(2)}, u32[]{:S(2)}) %collective-permute-start.36) | collective-permute-done | bytes 524320 | tf_op jit(solution)/shard_map/ppermute | solution.py:501
  179.3 1.9 collective-permute-start.37
  181.2 0.8 collective-permute-start.29
  182.0 7.1 %collective-permute-done.24 = bf16[128,1024]{1,0:T(8,128)(2,1)S(1)} collective-permute-done((bf16[128,1024]{1,0:T(8,128)(2,1)S(1)}, bf16[128,1024]{1,0:T(8,128)(2,1)S(1)}, u32[]{:S(2)}, u32[]{:S(2)}) %collective-permute-start.24) | collective-permute-done | bytes 262176 | tf_op jit(solution)/shard_map/ppermute | solution.py:501
  190.3 4.0 %collective-permute-done.29 = bf16[64,1024]{1,0:T(8,128)(2,1)S(1)} collective-permute-done((bf16[64,1024]{1,0:T(8,128)(2,1)S(1)}, bf16[64,1024]{1,0:T(8,128)(2,1)S(1)}, u32[]{:S(2)}, u32[]{:S(2)}) %collective-permute-start.29) | collective-permute-done | bytes 131104 | tf_op jit(solution)/shard_map/ppermute | solution.py:501
  195.7 1.3 collective-permute-done.38
  (119 shorter events, 17.8 us)
Async XLA Ops:
  0.6 33.2 %copy-start.12 = (bf16[1024,64]{0,1:T(8,128)(2,1)S(1)}, bf16[1024,64]{0,1:T(8,128)(2,1)}, u32[]{:S(2)}) copy-start(bf16[1024,64]{0,1:T(8,128)(2,1)} %param.34) | copy-start | bytes 393220
  2.4 12.5 %collective-permute-start.1 = (bf16[64,1408]{1,0:T(8,128)(2,1)S(1)}, bf16[64,1408]{1,0:T(8,128)(2,1)S(1)}, u32[]{:S(2)}, u32[]{:S(2)}) collective-permute-start(bf16[64,1408]{1,0:T(8,128)(2,1)S(1)} %fusion.11.first), channel_id=1, source_target_pairs={{0,16},{2,18},{4,20},{6,22},{8,24},{10,26},{12,28},{14,30},{16,0},... | collective-permute-start | bytes 540680 | tf_op jit(solution)/shard_map/ppermute | solution.py:501
  15.0 9.6 %collective-permute-start.2 = (bf16[128,1408]{1,0:T(8,128)(2,1)S(1)}, bf16[128,1408]{1,0:T(8,128)(2,1)S(1)}, u32[]{:S(2)}, u32[]{:S(2)}) collective-permute-start(bf16[128,1408]{1,0:T(8,128)(2,1)S(1)} %shard_map.299.first), channel_id=1, source_target_pairs={{0,8},{2,10},{4,12},{6,14},{8,0},{10,2},{12,4},{14,6},{16,24},{18,... | collective-permute-start | bytes 1081352 | tf_op jit(solution)/shard_map/ppermute | solution.py:501
  24.6 18.3 %copy-start.13 = (bf16[64,1024]{1,0:T(8,128)(2,1)S(1)}, bf16[64,1024]{1,0:T(8,128)(2,1)}, u32[]{:S(2)}) copy-start(bf16[64,1024]{1,0:T(8,128)(2,1)} %first) | copy-start | bytes 393220
  24.6 9.2 %collective-permute-start.3 = (bf16[64,1024]{1,0:T(8,128)(2,1)}, bf16[64,1024]{1,0:T(8,128)(2,1)S(1)}, u32[]{:S(2)}, u32[]{:S(2)}) collective-permute-start(bf16[64,1024]{1,0:T(8,128)(2,1)} %bitcast.53), channel_id=1, source_target_pairs={{0,16},{2,18},{4,20},{6,22},{8,24},{10,26},{12,28},{14,30},{16,0},... | collective-permute-start | bytes 393224 | tf_op jit(solution)/shard_map/ppermute | solution.py:501
  27.8 24.8 %collective-permute-start.8 = (bf16[256,1408]{1,0:T(8,128)(2,1)S(1)}, bf16[256,1408]{1,0:T(8,128)(2,1)S(1)}, u32[]{:S(2)}, u32[]{:S(2)}) collective-permute-start(bf16[256,1408]{1,0:T(8,128)(2,1)S(1)} %shard_map.303.first), channel_id=1, source_target_pairs={{0,4},{2,6},{4,0},{6,2},{8,12},{10,14},{12,8},{14,10},{16,20},{18,... | collective-permute-start | bytes 2162696 | tf_op jit(solution)/shard_map/ppermute | solution.py:501
  33.9 7.4 %collective-permute-start.11 = (bf16[128,1024]{1,0:T(8,128)(2,1)S(1)}, bf16[128,1024]{1,0:T(8,128)(2,1)S(1)}, u32[]{:S(2)}, u32[]{:S(2)}) collective-permute-start(bf16[128,1024]{1,0:T(8,128)(2,1)S(1)} %shard_map.308.first), channel_id=1, source_target_pairs={{0,8},{2,10},{4,12},{6,14},{8,0},{10,2},{12,4},{14,6},{16,24},{18,... | collective-permute-start | bytes 786440 | tf_op jit(solution)/shard_map/ppermute | solution.py:501
  41.3 19.2 %collective-permute-start.12 = (bf16[256,1024]{1,0:T(8,128)(2,1)S(1)}, bf16[256,1024]{1,0:T(8,128)(2,1)}, u32[]{:S(2)}, u32[]{:S(2)}) collective-permute-start(bf16[256,1024]{1,0:T(8,128)(2,1)S(1)} %shard_map.309.first), channel_id=1, source_target_pairs={{0,4},{2,6},{4,0},{6,2},{8,12},{10,14},{12,8},{14,10},{16,20},{18,... | collective-permute-start | bytes 1572872 | tf_op jit(solution)/shard_map/ppermute | solution.py:501
  42.9 8.8 %collective-permute-start.4 = (bf16[64,1024]{1,0:T(8,128)(2,1)S(1)}, bf16[64,1024]{1,0:T(8,128)(2,1)S(1)}, u32[]{:S(2)}, u32[]{:S(2)}) collective-permute-start(bf16[64,1024]{1,0:T(8,128)(2,1)S(1)} %copy-done.13), channel_id=1, source_target_pairs={{0,16},{2,18},{4,20},{6,22},{8,24},{10,26},{12,28},{14,30},{16,0},... | collective-permute-start | bytes 393224 | tf_op jit(solution)/shard_map/ppermute | solution.py:501
  51.8 7.4 %collective-permute-start.5 = (bf16[128,1024]{1,0:T(8,128)(2,1)S(1)}, bf16[128,1024]{1,0:T(8,128)(2,1)S(1)}, u32[]{:S(2)}, u32[]{:S(2)}) collective-permute-start(bf16[128,1024]{1,0:T(8,128)(2,1)S(1)} %shard_map.300.first), channel_id=1, source_target_pairs={{0,8},{2,10},{4,12},{6,14},{8,0},{10,2},{12,4},{14,6},{16,24},{18,... | collective-permute-start | bytes 786440 | tf_op jit(solution)/shard_map/ppermute | solution.py:501
  52.7 36.8 %collective-permute-start.9 = (bf16[512,1408]{1,0:T(8,128)(2,1)S(1)}, bf16[512,1408]{1,0:T(8,128)(2,1)}, u32[]{:S(2)}, u32[]{:S(2)}) collective-permute-start(bf16[512,1408]{1,0:T(8,128)(2,1)S(1)} %shard_map.304.a_1_.w1a), channel_id=1, source_target_pairs={{0,2},{2,0},{4,6},{6,4},{8,10},{10,8},{12,14},{14,12},{16,18},{18,... | collective-permute-start | bytes 4325384 | tf_op jit(solution)/shard_map/ppermute | solution.py:501
  60.0 15.3 %collective-permute-start.6 = (bf16[256,1024]{1,0:T(8,128)(2,1)}, bf16[256,1024]{1,0:T(8,128)(2,1)}, u32[]{:S(2)}, u32[]{:S(2)}) collective-permute-start(bf16[256,1024]{1,0:T(8,128)(2,1)} %shard_map.301.first), channel_id=1, source_target_pairs={{0,4},{2,6},{4,0},{6,2},{8,12},{10,14},{12,8},{14,10},{16,20},{18,... | collective-permute-start | bytes 1572872 | tf_op jit(solution)/shard_map/ppermute | solution.py:501
  62.6 2.7 %copy-start.20 = (s32[256]{0:T(256)S(1)}, s32[256]{0:T(256)}, u32[]{:S(2)}) copy-start(s32[256]{0:T(256)} %param.19) | copy-start | bytes 3076
  62.6 5.5 %copy-start.18 = (f32[1024]{0:T(1024)S(1)}, f32[1024]{0:T(1024)}, u32[]{:S(2)}) copy-start(f32[1024]{0:T(1024)} %param.21) | copy-start | bytes 12292
  62.6 24.6 %collective-permute-start.13 = (bf16[512,1024]{1,0:T(8,128)(2,1)}, bf16[512,1024]{1,0:T(8,128)(2,1)}, u32[]{:S(2)}, u32[]{:S(2)}) collective-permute-start(bf16[512,1024]{1,0:T(8,128)(2,1)} %shard_map.310.outa), channel_id=1, source_target_pairs={{0,2},{2,0},{4,6},{6,4},{8,10},{10,8},{12,14},{14,12},{16,18},{18,... | collective-permute-start | bytes 3145736 | tf_op jit(solution)/shard_map/ppermute | solution.py:501
  68.1 1.6 copy-start.1
  69.7 1.0 copy-start.8
  70.7 1.0 copy-start.10
  72.6 9.2 %collective-permute-start.10 = (bf16[128,1024]{1,0:T(8,128)(2,1)S(1)}, bf16[128,1024]{1,0:T(8,128)(2,1)S(1)}, u32[]{:S(2)}, u32[]{:S(2)}) collective-permute-start(bf16[128,1024]{1,0:T(8,128)(2,1)S(1)} %get-tuple-element.94.own), channel_id=1, source_target_pairs={{0,1},{1,0},{2,3},{3,2},{4,5},{5,4},{6,7},{7,6},{8,9},{9,8},{10,11... | collective-permute-start | bytes 786440 | tf_op jit(solution)/shard_map/ppermute | solution.py:504
  74.1 12.8 %collective-permute-start = (bf16[128,1024]{1,0:T(8,128)(2,1)S(1)}, bf16[128,1024]{1,0:T(8,128)(2,1)S(1)}, u32[]{:S(2)}, u32[]{:S(2)}) collective-permute-start(bf16[128,1024]{1,0:T(8,128)(2,1)S(1)} %get-tuple-element.82.own), channel_id=1, source_target_pairs={{0,1},{1,0},{2,3},{3,2},{4,5},{5,4},{6,7},{7,6},{8,9},{9,8},{10,11... | collective-permute-start | bytes 786440 | tf_op jit(solution)/shard_map/ppermute | solution.py:504
  76.6 17.9 %collective-permute-start.7 = (bf16[512,1024]{1,0:T(8,128)(2,1)S(1)}, bf16[512,1024]{1,0:T(8,128)(2,1)S(1)}, u32[]{:S(2)}, u32[]{:S(2)}) collective-permute-start(bf16[512,1024]{1,0:T(8,128)(2,1)S(1)} %shard_map.302.wza), channel_id=1, source_target_pairs={{0,2},{2,0},{4,6},{6,4},{8,10},{10,8},{12,14},{14,12},{16,18},{18,... | collective-permute-start | bytes 3145736 | tf_op jit(solution)/shard_map/ppermute | solution.py:501
  87.2 2.3 %copy-start.14 = (f32[4,1024]{1,0:T(4,128)S(1)}, f32[4,1024]{1,0:T(4,128)}, u32[]{:S(2)}) copy-start(f32[4,1024]{1,0:T(4,128)} %a_11_.1) | copy-start | bytes 49156
  87.2 2.3 %copy-start.15 = (f32[1024]{0:T(1024)S(1)}, f32[1024]{0:T(1024)}, u32[]{:S(2)}) copy-start(f32[1024]{0:T(1024)} %param.27) | copy-start | bytes 12292
  87.2 2.3 %copy-start.17 = (f32[4,256]{1,0:T(4,128)S(1)}, f32[4,256]{1,0:T(4,128)}, u32[]{:S(2)}) copy-start(f32[4,256]{1,0:T(4,128)} %a_12_.1) | copy-start | bytes 12292
  87.2 2.3 %copy-start.19 = (f32[256]{0:T(256)S(1)}, f32[256]{0:T(256)}, u32[]{:S(2)}) copy-start(f32[256]{0:T(256)} %param.29) | copy-start | bytes 3076
  89.6 4.9 %copy-start.16 = (f32[1024]{0:T(1024)S(1)}, f32[1024]{0:T(1024)}, u32[]{:S(2)}) copy-start(f32[1024]{0:T(1024)} %param.33) | copy-start | bytes 12292
  94.5 2.6 %copy-start = (bf16[1024,1024]{1,0:T(8,128)(2,1)S(1)}, bf16[1024,1024]{1,0:T(8,128)(2,1)}, u32[]{:S(2)}) copy-start(bf16[1024,1024]{1,0:T(8,128)(2,1)} %get-tuple-element.127.picks) | copy-start | bytes 6291460
  95.6 3.8 %collective-permute-start.14 = (f32[16,256]{1,0:T(8,128)S(1)}, f32[16,256]{1,0:T(8,128)S(1)}, u32[]{:S(2)}, u32[]{:S(2)}) collective-permute-start(f32[16,256]{1,0:T(8,128)S(1)} %get-tuple-element.98.a_1_.a_8_), channel_id=1, source_target_pairs={{0,1},{1,0},{2,3},{3,2},{4,5},{5,4},{6,7},{7,6},{8,9},{9,8},{10,11... | collective-permute-start | bytes 49160 | tf_op jit(solution)/shard_map/ppermute | solution.py:504
  101.4 1.0 copy-start.2
  105.1 1.0 copy-start.4
  114.9 4.6 %copy-start.6 = (bf16[512,1024]{1,0:T(8,128)(2,1)}, bf16[512,1024]{1,0:T(8,128)(2,1)S(1)}, u32[]{:S(2)}) copy-start(bf16[512,1024]{1,0:T(8,128)(2,1)S(1)} %get-tuple-element.125) | copy-start | bytes 3145732
  115.0 5.2 %collective-permute-start.30 = (bf16[256,256]{1,0:T(8,128)(2,1)S(1)}, bf16[256,256]{1,0:T(8,128)(2,1)S(1)}, u32[]{:S(2)}, u32[]{:S(2)}) collective-permute-start(bf16[256,256]{1,0:T(8,128)(2,1)S(1)} %get-tuple-element.128), channel_id=1, source_target_pairs={{0,1},{1,0},{2,3},{3,2},{4,5},{5,4},{6,7},{7,6},{8,9},{9,8},{10,11... | collective-permute-start | bytes 393224 | tf_op jit(solution)/shard_map/ppermute | solution.py:504
  119.5 6.5 %copy-start.9 = (f32[128,1024]{1,0:T(8,128)S(1)}, f32[128,1024]{1,0:T(8,128)}, u32[]{:S(2)}) copy-start(f32[128,1024]{1,0:T(8,128)} %cot.3) | copy-start | bytes 1572868
  119.5 6.5 %copy-start.11 = (f32[128,1024]{1,0:T(8,128)S(1)}, f32[128,1024]{1,0:T(8,128)}, u32[]{:S(2)}) copy-start(f32[128,1024]{1,0:T(8,128)} %res.2) | copy-start | bytes 1572868
  119.5 6.5 %collective-permute-start.16 = (bf16[128,1024]{1,0:T(8,128)(2,1)S(1)}, bf16[128,1024]{1,0:T(8,128)(2,1)S(1)}, u32[]{:S(2)}, u32[]{:S(2)}) collective-permute-start(bf16[128,1024]{1,0:T(8,128)(2,1)S(1)} %get-tuple-element.117), channel_id=1, source_target_pairs={{0,1},{1,0},{2,3},{3,2},{4,5},{5,4},{6,7},{7,6},{8,9},{9,8},{10,11... | collective-permute-start | bytes 786440 | tf_op jit(solution)/shard_map/ppermute | solution.py:504
  120.7 7.2 %collective-permute-start.31 = (bf16[256,384]{1,0:T(8,128)(2,1)S(1)}, bf16[256,384]{1,0:T(8,128)(2,1)S(1)}, u32[]{:S(2)}, u32[]{:S(2)}) collective-permute-start(bf16[256,384]{1,0:T(8,128)(2,1)S(1)} %get-tuple-element.130), channel_id=1, source_target_pairs={{0,2},{2,0},{4,6},{6,4},{8,10},{10,8},{12,14},{14,12},{16,18},{18,... | collective-permute-start | bytes 589832 | tf_op jit(solution)/shard_map/ppermute | solution.py:501
  127.8 1.8 collective-permute-start.17
  127.9 8.0 %collective-permute-start.32 = (bf16[128,384]{1,0:T(8,128)(2,1)S(1)}, bf16[128,384]{1,0:T(8,128)(2,1)S(1)}, u32[]{:S(2)}, u32[]{:S(2)}) collective-permute-start(bf16[128,384]{1,0:T(8,128)(2,1)S(1)} %get-tuple-element.167), channel_id=1, source_target_pairs={{0,4},{2,6},{4,0},{6,2},{8,12},{10,14},{12,8},{14,10},{16,20},{18,... | collective-permute-start | bytes 294920 | tf_op jit(solution)/shard_map/ppermute | solution.py:501
  129.5 5.0 %collective-permute-start.18 = (f32[16,1024]{1,0:T(8,128)S(1)}, f32[16,1024]{1,0:T(8,128)S(1)}, u32[]{:S(2)}, u32[]{:S(2)}) collective-permute-start(f32[16,1024]{1,0:T(8,128)S(1)} %add.194), channel_id=1, source_target_pairs={{0,4},{2,6},{4,0},{6,2},{8,12},{10,14},{12,8},{14,10},{16,20},{18,... | collective-permute-start | bytes 196616 | tf_op jit(solution)/shard_map/ppermute | solution.py:501
  130.7 26.1 %collective-permute-start.26 = (bf16[512,1024]{1,0:T(8,128)(2,1)}, bf16[512,1024]{1,0:T(8,128)(2,1)S(1)}, u32[]{:S(2)}, u32[]{:S(2)}) collective-permute-start(bf16[512,1024]{1,0:T(8,128)(2,1)} %get-tuple-element.126), channel_id=1, source_target_pairs={{0,2},{2,0},{4,6},{6,4},{8,10},{10,8},{12,14},{14,12},{16,18},{18,... | collective-permute-start | bytes 3145736 | tf_op jit(solution)/shard_map/ppermute | solution.py:501
  134.6 6.4 %collective-permute-start.19 = (f32[16,1024]{1,0:T(8,128)S(1)}, f32[16,1024]{1,0:T(8,128)S(1)}, u32[]{:S(2)}, u32[]{:S(2)}) collective-permute-start(f32[16,1024]{1,0:T(8,128)S(1)} %add.195), channel_id=1, source_target_pairs={{0,8},{2,10},{4,12},{6,14},{8,0},{10,2},{12,4},{14,6},{16,24},{18,... | collective-permute-start | bytes 196616 | tf_op jit(solution)/shard_map/ppermute | solution.py:501
  136.0 5.5 %collective-permute-start.33 = (bf16[64,384]{1,0:T(8,128)(2,1)S(1)}, bf16[64,384]{1,0:T(8,128)(2,1)S(1)}, u32[]{:S(2)}, u32[]{:S(2)}) collective-permute-start(bf16[64,384]{1,0:T(8,128)(2,1)S(1)} %get-tuple-element.169), channel_id=1, source_target_pairs={{0,8},{2,10},{4,12},{6,14},{8,0},{10,2},{12,4},{14,6},{16,24},{18,... | collective-permute-start | bytes 147464 | tf_op jit(solution)/shard_map/ppermute | solution.py:501
  139.8 7.3 %collective-permute-start.15 = (bf16[128,1024]{1,0:T(8,128)(2,1)S(1)}, bf16[128,1024]{1,0:T(8,128)(2,1)S(1)}, u32[]{:S(2)}, u32[]{:S(2)}) collective-permute-start(bf16[128,1024]{1,0:T(8,128)(2,1)S(1)} %get-tuple-element.102), channel_id=1, source_target_pairs={{0,1},{1,0},{2,3},{3,2},{4,5},{5,4},{6,7},{7,6},{8,9},{9,8},{10,11... | collective-permute-start | bytes 786440 | tf_op jit(solution)/shard_map/ppermute | solution.py:504
  141.0 17.8 %collective-permute-start.22 = (bf16[512,1024]{1,0:T(8,128)(2,1)}, bf16[512,1024]{1,0:T(8,128)(2,1)}, u32[]{:S(2)}, u32[]{:S(2)}) collective-permute-start(bf16[512,1024]{1,0:T(8,128)(2,1)} %get-tuple-element.124), channel_id=1, source_target_pairs={{0,2},{2,0},{4,6},{6,4},{8,10},{10,8},{12,14},{14,12},{16,18},{18,... | collective-permute-start | bytes 3145736 | tf_op jit(solution)/shard_map/ppermute | solution.py:501
  141.0 20.8 %collective-permute-start.35 = (bf16[512,1024]{1,0:T(8,128)(2,1)}, bf16[512,1024]{1,0:T(8,128)(2,1)}, u32[]{:S(2)}, u32[]{:S(2)}) collective-permute-start(bf16[512,1024]{1,0:T(8,128)(2,1)} %get-tuple-element.105), channel_id=1, source_target_pairs={{0,2},{2,0},{4,6},{6,4},{8,10},{10,8},{12,14},{14,12},{16,18},{18,... | collective-permute-start | bytes 3145736 | tf_op jit(solution)/shard_map/ppermute | solution.py:501
  141.5 10.1 %collective-permute-start.20 = (f32[16,1024]{1,0:T(8,128)S(1)}, f32[16,1024]{1,0:T(8,128)S(1)}, u32[]{:S(2)}, u32[]{:S(2)}) collective-permute-start(f32[16,1024]{1,0:T(8,128)S(1)} %add.196), channel_id=1, source_target_pairs={{0,16},{2,18},{4,20},{6,22},{8,24},{10,26},{12,28},{14,30},{16,0},... | collective-permute-start | bytes 196616 | tf_op jit(solution)/shard_map/ppermute | solution.py:501
  147.2 5.7 %collective-permute-start.34 = (bf16[32,384]{1,0:T(8,128)(2,1)S(1)}, bf16[32,384]{1,0:T(8,128)(2,1)S(1)}, u32[]{:S(2)}, u32[]{:S(2)}) collective-permute-start(bf16[32,384]{1,0:T(8,128)(2,1)S(1)} %get-tuple-element.170), channel_id=1, source_target_pairs={{0,16},{2,18},{4,20},{6,22},{8,24},{10,26},{12,28},{14,30},{16,0},... | collective-permute-start | bytes 73736 | tf_op jit(solution)/shard_map/ppermute | solution.py:501
  151.6 5.2 %copy-start.7 = (bf16[512,1024]{1,0:T(8,128)(2,1)S(1)}, bf16[512,1024]{1,0:T(8,128)(2,1)}, u32[]{:S(2)}) copy-start(bf16[512,1024]{1,0:T(8,128)(2,1)} %copy-done.6) | copy-start | bytes 3145732
  151.7 4.0 %collective-permute-start.21 = (f32[8,1024]{1,0:T(8,128)S(1)}, f32[8,1024]{1,0:T(8,128)S(1)}, u32[]{:S(2)}, u32[]{:S(2)}) collective-permute-start(f32[8,1024]{1,0:T(8,128)S(1)} %slice.270), channel_id=1, source_target_pairs={{0,1},{1,0},{2,3},{3,2},{4,5},{5,4},{6,7},{7,6},{8,9},{9,8},{10,11... | collective-permute-start | bytes 98312 | tf_op jit(solution)/shard_map/ppermute | solution.py:504
  154.1 4.7 %copy-start.5 = (bf16[512,1024]{1,0:T(8,128)(2,1)S(1)}, bf16[512,1024]{1,0:T(8,128)(2,1)}, u32[]{:S(2)}) copy-start(bf16[512,1024]{1,0:T(8,128)(2,1)} %copy-done.4) | copy-start | bytes 3145732
  156.8 5.0 %copy-start.3 = (bf16[512,1024]{1,0:T(8,128)(2,1)S(1)}, bf16[512,1024]{1,0:T(8,128)(2,1)}, u32[]{:S(2)}) copy-start(bf16[512,1024]{1,0:T(8,128)(2,1)} %copy-done.2) | copy-start | bytes 3145732
  157.2 14.9 %collective-permute-start.27 = (bf16[256,1024]{1,0:T(8,128)(2,1)S(1)}, bf16[256,1024]{1,0:T(8,128)(2,1)S(1)}, u32[]{:S(2)}, u32[]{:S(2)}) collective-permute-start(bf16[256,1024]{1,0:T(8,128)(2,1)S(1)} %get-tuple-element.159), channel_id=1, source_target_pairs={{0,4},{2,6},{4,0},{6,2},{8,12},{10,14},{12,8},{14,10},{16,20},{18,... | collective-permute-start | bytes 1572872 | tf_op jit(solution)/shard_map/ppermute | solution.py:501
  160.0 16.0 %collective-permute-start.23 = (bf16[256,1024]{1,0:T(8,128)(2,1)S(1)}, bf16[256,1024]{1,0:T(8,128)(2,1)S(1)}, u32[]{:S(2)}, u32[]{:S(2)}) collective-permute-start(bf16[256,1024]{1,0:T(8,128)(2,1)S(1)} %bitcast.63), channel_id=1, source_target_pairs={{0,8},{2,10},{4,12},{6,14},{8,0},{10,2},{12,4},{14,6},{16,24},{18,... | collective-permute-start | bytes 1572872 | tf_op jit(solution)/shard_map/ppermute | solution.py:501
  163.3 15.7 %collective-permute-start.36 = (bf16[256,1024]{1,0:T(8,128)(2,1)S(1)}, bf16[256,1024]{1,0:T(8,128)(2,1)S(1)}, u32[]{:S(2)}, u32[]{:S(2)}) collective-permute-start(bf16[256,1024]{1,0:T(8,128)(2,1)S(1)} %get-tuple-element.157), channel_id=1, source_target_pairs={{0,4},{2,6},{4,0},{6,2},{8,12},{10,14},{12,8},{14,10},{16,20},{18,... | collective-permute-start | bytes 1572872 | tf_op jit(solution)/shard_map/ppermute | solution.py:501
  172.2 8.9 %collective-permute-start.28 = (bf16[128,1024]{1,0:T(8,128)(2,1)S(1)}, bf16[128,1024]{1,0:T(8,128)(2,1)S(1)}, u32[]{:S(2)}, u32[]{:S(2)}) collective-permute-start(bf16[128,1024]{1,0:T(8,128)(2,1)S(1)} %get-tuple-element.163), channel_id=1, source_target_pairs={{0,8},{2,10},{4,12},{6,14},{8,0},{10,2},{12,4},{14,6},{16,24},{18,... | collective-permute-start | bytes 786440 | tf_op jit(solution)/shard_map/ppermute | solution.py:501
  176.2 12.9 %collective-permute-start.24 = (bf16[128,1024]{1,0:T(8,128)(2,1)S(1)}, bf16[128,1024]{1,0:T(8,128)(2,1)S(1)}, u32[]{:S(2)}, u32[]{:S(2)}) collective-permute-start(bf16[128,1024]{1,0:T(8,128)(2,1)S(1)} %bitcast.64), channel_id=1, source_target_pairs={{0,16},{2,18},{4,20},{6,22},{8,24},{10,26},{12,28},{14,30},{16,0},... | collective-permute-start | bytes 786440 | tf_op jit(solution)/shard_map/ppermute | solution.py:501
  179.3 10.3 %collective-permute-start.37 = (bf16[128,1024]{1,0:T(8,128)(2,1)S(1)}, bf16[128,1024]{1,0:T(8,128)(2,1)S(1)}, u32[]{:S(2)}, u32[]{:S(2)}) collective-permute-start(bf16[128,1024]{1,0:T(8,128)(2,1)S(1)} %get-tuple-element.161), channel_id=1, source_target_pairs={{0,8},{2,10},{4,12},{6,14},{8,0},{10,2},{12,4},{14,6},{16,24},{18,... | collective-permute-start | bytes 786440 | tf_op jit(solution)/shard_map/ppermute | solution.py:501
  181.2 13.1 %collective-permute-start.29 = (bf16[64,1024]{1,0:T(8,128)(2,1)S(1)}, bf16[64,1024]{1,0:T(8,128)(2,1)S(1)}, u32[]{:S(2)}, u32[]{:S(2)}) collective-permute-start(bf16[64,1024]{1,0:T(8,128)(2,1)S(1)} %fusion.9), channel_id=1, source_target_pairs={{0,16},{2,18},{4,20},{6,22},{8,24},{10,26},{12,28},{14,30},{16,0},... | collective-permute-start | bytes 393224 | tf_op jit(solution)/shard_map/ppermute | solution.py:501
  189.1 5.9 %collective-permute-start.25 = (bf16[64,1024]{1,0:T(8,128)(2,1)S(1)}, bf16[64,1024]{1,0:T(8,128)(2,1)S(1)}, u32[]{:S(2)}, u32[]{:S(2)}) collective-permute-start(bf16[64,1024]{1,0:T(8,128)(2,1)S(1)} %fusion.5), channel_id=1, source_target_pairs={{0,4},{2,6},{4,0},{6,2},{8,12},{10,14},{12,8},{14,10},{16,20},{18,... | collective-permute-start | bytes 393224 | tf_op jit(solution)/shard_map/ppermute | solution.py:501
  189.6 7.4 %collective-permute-start.38 = (bf16[64,1024]{1,0:T(8,128)(2,1)S(1)}, bf16[64,1024]{1,0:T(8,128)(2,1)S(1)}, u32[]{:S(2)}, u32[]{:S(2)}) collective-permute-start(bf16[64,1024]{1,0:T(8,128)(2,1)S(1)} %fusion.7), channel_id=1, source_target_pairs={{0,16},{2,18},{4,20},{6,22},{8,24},{10,26},{12,28},{14,30},{16,0},... | collective-permute-start | bytes 393224 | tf_op jit(solution)/shard_map/ppermute | solution.py:501

commit v4 on v3

--- a/solution.py
+++ b/solution.py
@@ -94,10 +94,14 @@
     return dpre, dw, jnp.sum(dv, axis=0, keepdims=True)
 
 
-def prepare(dtpre, dtb, alog, segc, segr):
+def rates(dtpre, dtb, alog):
     v = dtpre + dtb
     step = jnp.maximum(v, 0.0) + jnp.log1p(jnp.exp(-jnp.abs(v)))
-    logd = -step * jnp.exp(alog)
+    return v, step, -step * jnp.exp(alog)
+
+
+def prepare(dtpre, dtb, alog, segc, segr):
+    v, step, logd = rates(dtpre, dtb, alog)
     row = iota((SPAN, SPAN), 0)
     col = iota((SPAN, SPAN), 1)
     lower = row >= col
@@ -129,7 +133,7 @@
 
 
 def fwd_body(width, nrm, w1a, w1b, cols, segr, cx, cxb, cbc, cbcb, dtb, alog,
-             xpre_o, xc_o, y_o, bcpre_o, bcc_o, dt_o, dec_o):
+             xpre_o, xc_o, y_o, bcpre_o, bcc_o, dt_o, dec_o, wt_o, edge_o):
     inner = xc_o.shape[1]
     state = bcc_o.shape[1] // 2
     x = nrm[...]
@@ -152,6 +156,8 @@
     scores = [
         dot_nt(cs[k * SPAN : (k + 1) * SPAN], bs[k * SPAN : (k + 1) * SPAN], HI) for k in range(2)
     ]
+    edge_o[:SPAN] = coef
+    edge_o[SPAN:] = grow
     b0 = bs[:SPAN].astype(bf16)
     c1 = cs[SPAN:].astype(bf16)
     c1 = jnp.concatenate([c1, c1], 1)
@@ -171,6 +177,7 @@
                 dec = decay(cum[k], cum_t[k], mask[k], h)
                 dec_o[2 * h + k] = dec
                 w = (dec * scores[k]).astype(bf16)
+                wt_o[2 * h + k] = w.T
                 part = dot_nn(w, ub[rows])
                 y = part if y is None else jnp.where(lane >= i * width, part, y)
             if k:
@@ -262,7 +269,7 @@
         keep_o[:, at] = dot_nn(nrm_t[:half], dz_o[:, at]).astype(bf16)
 
 
-def bwd_body(width, nrm_t, dy_r, xpre_r, xc_r, y_r, bcpre_r, bcc_r, dt_r, dec_r, cols, segr, cx,
+def bwd_body(width, nrm_t, dy_r, xpre_r, xc_r, y_r, bcpre_r, bcc_r, dt_r, dec_r, wt_r, edge_r, cols, segr, cx,
              cbc, dtb, alog, dsk, dx_o, dbc_o, sm_o, keep_o, send_o, dc_s):
     inner = xc_r.shape[1]
     state = bcc_r.shape[1] // 2
@@ -270,10 +277,9 @@
     segc = cols[:, SEG : SEG + 1]
     bs = silu(bcc_r[:, :state])
     cs = silu(bcc_r[:, state:])
-    v, step, logd, _, _, _, grow, coef = prepare(dt_r[...], dtb[...], alog[...], segc, segr[...])
-    scores = [
-        dot_nt(cs[k * SPAN : (k + 1) * SPAN], bs[k * SPAN : (k + 1) * SPAN], HI) for k in range(2)
-    ]
+    v, step, logd = rates(dt_r[...], dtb[...], alog[...])
+    coef = edge_r[:SPAN]
+    grow = edge_r[SPAN:]
     b0 = bs[:SPAN].astype(bf16)
     c1 = cs[SPAN:].astype(bf16)
     b00 = jnp.concatenate([b0, b0], 1)
@@ -316,8 +322,7 @@
             for i in range(per):
                 h = j * per + i
                 dec = dec_r[2 * h + k]
-                w = (dec * scores[k]).astype(bf16)
-                part = dot_tn(w, dyb[rows])
+                part = dot_nn(wt_r[2 * h + k], dyb[rows])
                 du = part if du is None else jnp.where(lane >= i * width, part, du)
                 inside = (lane >= i * width) & (lane < (i + 1) * width)
                 mine = jnp.where(inside, dy[rows], 0.0).astype(bf16)
@@ -517,6 +522,9 @@
                 (v,) = call(0.5, cat_body, [((2 * v.shape[0], v.shape[1]), bf16)], v, r)
         return v, r, marks
 
+    def finish(pair):
+        return plus(*pair)
+
     def plus(a, b):
         return a.astype(f32) + b.astype(f32)
 
@@ -606,10 +614,11 @@
             return fwd_body(head_width, *a)
 
         (dm,) = call(3.0, dmix_body, [big], cot, outa, outb, cols)
-        xpre, xc, y, bcpre, bcc, dtp, dec = call(
+        xpre, xc, y, bcpre, bcc, dtp, dec, wt, edge = call(
             7.0, fwd,
             [big, big, big, ((tokens, two_state), f32), ((tokens, two_state), f32),
-             ((tokens, LANES), f32), ((2 * heads, SPAN, SPAN), f32)],
+             ((tokens, LANES), f32), ((2 * heads, SPAN, SPAN), f32),
+             ((2 * heads, SPAN, SPAN), bf16), ((tokens, LANES), f32)],
             nrm, w1a, w1b, cols, segr, conv_x, cxb, conv_bc, cbcb, dtb, alog,
         )
         z, g, sums = call(
@@ -629,7 +638,7 @@
             g, sums, sums2, gg, cols, cot_t,
         )
         blk_own, blk_send = call(2.5, blk_body, apart, where, mixed, outa, outb, scalars=1)
-        out_sum = plus(*scatter(out_keep, out_send, near))
+        out_sum = finish(scatter(out_keep, out_send, near))
 
         blk_other = cross(blk_send)
         (block_out,) = call(
@@ -645,7 +654,7 @@
              ((cut, inner), bf16)],
             after(nrm_t, out_send), g, dm, z, y, xc, dsk, gg, sums, sums2,
         )
-        z_weight_grad = plus(*scatter(z_keep, z_send, far))
+        z_weight_grad = finish(scatter(z_keep, z_send, far))
 
         def back(*a):
             return bwd_body(head_width, *a)
@@ -655,7 +664,7 @@
             8.0, back,
             [((tokens, wide), bf16), ((tokens, two_state), bf16), ((16, inner), f32),
              ((cut, inner), bf16), ((cut, inner), bf16)],
-            nrm_t, dy, xpre, xc, y, bcpre, bcc, dtp, dec, cols, segr, conv_x, conv_bc, dtb, alog,
+            nrm_t, dy, xpre, xc, y, bcpre, bcc, dtp, dec, wt, edge, cols, segr, conv_x, conv_bc, dtb, alog,
             dsk,
             scratch=[pltpu.VMEM((tokens, two_state), f32)],
         )

time: 198 us -> 198 us (level)
  transfers between devices with their start and end apart: 39 -> 39, of which waited for: 19 -> 19; matrix products, arithmetic and copies ran while one was open for 7% -> 7% of each run, Pallas kernels for 12% -> 13%
where the time goes in v4:
time: 198 us
  waiting for transfers between devices  89 us (45%)
  starting transfers between devices  46 us (23%)
  Pallas kernels  39.4 us (20%)
  other arithmetic  11.2 us (6%)
  local copies, waits for them, and re-layouts  10.5 us (5%)
    ppermute x32, waiting for transfers between devices, swap(): return lax.ppermute(v, 'dp', [(i, i ^ bit) for i in range(n)])  68.1 us
    pallas_call x27, Pallas kernels, call(): pl.pallas_call(body, out_shape=[jax.ShapeDtypeStruct(s, d) for s, d in ou...  39.4 us
    ppermute x32, starting transfers between devices, swap(): return lax.ppermute(v, 'dp', [(i, i ^ bit) for i in range(n)])  37.9 us
    ppermute x7, waiting for transfers between devices, cross(): return lax.ppermute(v, 'tensor', [(0, 1), (1, 0)])  20.9 us
    ppermute x7, starting transfers between devices, cross(): return lax.ppermute(v, 'tensor', [(0, 1), (1, 0)])  8.09 us
    unnamed x44, local copies, waits for them, and re-layouts  7.19 us
  transfers between devices with their start and end apart: 39, of which 19 were waited for; matrix products, arithmetic and copies ran while one was open for 7% of the time, Pallas kernels for 13%

profile of v4, /device:TPU:0, one launch (start us, length us, event | category | flops | bytes accessed | tf_op | source)
XLA Modules:
  0.0 197.8 jit_solution(5281078915577099015)
XLA Ops:
  1.5 0.9 fusion.11.first
  2.4 4.1 %collective-permute-start.1 = (bf16[64,1408]{1,0:T(8,128)(2,1)S(1)}, bf16[64,1408]{1,0:T(8,128)(2,1)S(1)}, u32[]{:S(2)}, u32[]{:S(2)}) collective-permute-start(bf16[64,1408]{1,0:T(8,128)(2,1)S(1)} %fusion.11.first), channel_id=1, source_target_pairs={{0,16},{2,18},{4,20},{6,22},{8,24},{10,26},{12,28},{14,30},{16,0},... | collective-permute-start | bytes 540680 | tf_op jit(solution)/shard_map/ppermute | solution.py:506
  6.5 8.4 %collective-permute-done.1.second = bf16[64,1408]{1,0:T(8,128)(2,1)S(1)} collective-permute-done((bf16[64,1408]{1,0:T(8,128)(2,1)S(1)}, bf16[64,1408]{1,0:T(8,128)(2,1)S(1)}, u32[]{:S(2)}, u32[]{:S(2)}) %collective-permute-start.1) | collective-permute-done | bytes 180256 | tf_op jit(solution)/shard_map/ppermute | solution.py:506
  15.8 8.9 %collective-permute-done.2.second = bf16[128,1408]{1,0:T(8,128)(2,1)S(1)} collective-permute-done((bf16[128,1408]{1,0:T(8,128)(2,1)S(1)}, bf16[128,1408]{1,0:T(8,128)(2,1)S(1)}, u32[]{:S(2)}, u32[]{:S(2)}) %collective-permute-start.2) | collective-permute-done | bytes 360480 | tf_op jit(solution)/shard_map/ppermute | solution.py:506
  24.6 3.1 %collective-permute-start.3 = (bf16[64,1024]{1,0:T(8,128)(2,1)}, bf16[64,1024]{1,0:T(8,128)(2,1)S(1)}, u32[]{:S(2)}, u32[]{:S(2)}) collective-permute-start(bf16[64,1024]{1,0:T(8,128)(2,1)} %bitcast.53), channel_id=1, source_target_pairs={{0,16},{2,18},{4,20},{6,22},{8,24},{10,26},{12,28},{14,30},{16,0},... | collective-permute-start | bytes 393224 | tf_op jit(solution)/shard_map/ppermute | solution.py:506
  27.8 1.6 collective-permute-start.8
  29.4 4.5 %collective-permute-done.3.second = bf16[64,1024]{1,0:T(8,128)(2,1)S(1)} collective-permute-done((bf16[64,1024]{1,0:T(8,128)(2,1)}, bf16[64,1024]{1,0:T(8,128)(2,1)S(1)}, u32[]{:S(2)}, u32[]{:S(2)}) %collective-permute-start.3) | collective-permute-done | bytes 131104 | tf_op jit(solution)/shard_map/ppermute | solution.py:506
  33.9 0.9 collective-permute-start.11
  34.8 6.5 %collective-permute-done.11.second = bf16[128,1024]{1,0:T(8,128)(2,1)S(1)} collective-permute-done((bf16[128,1024]{1,0:T(8,128)(2,1)S(1)}, bf16[128,1024]{1,0:T(8,128)(2,1)S(1)}, u32[]{:S(2)}, u32[]{:S(2)}) %collective-permute-start.11) | collective-permute-done | bytes 262176 | tf_op jit(solution)/shard_map/ppermute | solution.py:506
  41.3 1.6 collective-permute-start.12
  42.9 3.2 %collective-permute-start.4 = (bf16[64,1024]{1,0:T(8,128)(2,1)S(1)}, bf16[64,1024]{1,0:T(8,128)(2,1)S(1)}, u32[]{:S(2)}, u32[]{:S(2)}) collective-permute-start(bf16[64,1024]{1,0:T(8,128)(2,1)S(1)} %copy-done.13), channel_id=1, source_target_pairs={{0,16},{2,18},{4,20},{6,22},{8,24},{10,26},{12,28},{14,30},{16,0},... | collective-permute-start | bytes 393224 | tf_op jit(solution)/shard_map/ppermute | solution.py:506
  46.1 5.6 %collective-permute-done.4.second = bf16[64,1024]{1,0:T(8,128)(2,1)S(1)} collective-permute-done((bf16[64,1024]{1,0:T(8,128)(2,1)S(1)}, bf16[64,1024]{1,0:T(8,128)(2,1)S(1)}, u32[]{:S(2)}, u32[]{:S(2)}) %collective-permute-start.4) | collective-permute-done | bytes 131104 | tf_op jit(solution)/shard_map/ppermute | solution.py:506
  52.8 6.4 %collective-permute-done.5.second = bf16[128,1024]{1,0:T(8,128)(2,1)S(1)} collective-permute-done((bf16[128,1024]{1,0:T(8,128)(2,1)S(1)}, bf16[128,1024]{1,0:T(8,128)(2,1)S(1)}, u32[]{:S(2)}, u32[]{:S(2)}) %collective-permute-start.5) | collective-permute-done | bytes 262176 | tf_op jit(solution)/shard_map/ppermute | solution.py:506
  59.2 0.8 shard_map.301.first
  60.5 2.1 %shard_map.310.outa = bf16[512,1024]{1,0:T(8,128)(2,1)} custom-call(bf16[256,1024]{1,0:T(8,128)(2,1)S(1)} %shard_map.309.first, bf16[256,1024]{1,0:T(8,128)(2,1)} %collective-permute-done.12.second), custom_call_target="tpu_custom_call" | custom-call | flops 450000000 | bytes 1500000 | tf_op jit(solution)/shard_map/pallas_call | solution.py:31
  62.6 2.7 %fusion.1 = (bf16[1024,1024]{1,0:T(8,128)(2,1)S(1)}, bf16[1024,1024]{1,0:T(8,128)(2,1)}, bf16[1024,1024]{1,0:T(8,128)(2,1)}) fusion(s32[1024]{0:T(1024)S(1)} %fusion.38, s32[1024]{0:T(1024)S(1)} %fusion.36), kind=kLoop, calls=%fused_computation.4 | loop fusion | flops 6291456 | bytes 6299648 | tf_op jit(solution)/shard_map/convert_element_type | solution.py:577
  65.3 1.3 broadcast_in_dim.36
  68.1 1.6 copy-done.1
  69.7 1.0 copy-done.8
  70.7 1.0 copy-done.10
  72.6 1.6 collective-permute-start.10
  75.3 1.3 shard_map.302.wza
  76.8 5.0 %collective-permute-done.10.other = bf16[128,1024]{1,0:T(8,128)(2,1)S(1)} collective-permute-done((bf16[128,1024]{1,0:T(8,128)(2,1)S(1)}, bf16[128,1024]{1,0:T(8,128)(2,1)S(1)}, u32[]{:S(2)}, u32[]{:S(2)}) %collective-permute-start.10) | collective-permute-done | bytes 262176 | tf_op jit(solution)/shard_map/ppermute | solution.py:509
  82.0 4.9 %collective-permute-done.other = bf16[128,1024]{1,0:T(8,128)(2,1)S(1)} collective-permute-done((bf16[128,1024]{1,0:T(8,128)(2,1)S(1)}, bf16[128,1024]{1,0:T(8,128)(2,1)S(1)}, u32[]{:S(2)}, u32[]{:S(2)}) %collective-permute-start) | collective-permute-done | bytes 262176 | tf_op jit(solution)/shard_map/ppermute | solution.py:509
  87.2 2.3 %shard_map.311.dm_r.a_2_ = f32[256,1024]{1,0:T(8,128)S(1)} custom-call(bf16[256,1024]{1,0:T(8,128)(2,1)S(1)} %get-tuple-element.97.cot, bf16[512,1024]{1,0:T(8,128)(2,1)} %shard_map.310.outa, bf16[512,1024]{1,0:T(8,128)(2,1)} %collective-permute-done.13.outb, f32[256,128]{1,0:T(8,128)S(1)} %shard_map.305.a_3_.cols.a_4_.a_11_), custom_call_target="tpu_custom_call" | custom-call | flops 2700000000 | bytes 9000000 | tf_op jit(solution)/shard_map/pallas_call | solution.py:31
  89.6 5.5 %shard_map.306 = (f32[256,1024]{1,0:T(8,128)S(1)}, f32[256,1024]{1,0:T(8,128)S(1)}, f32[256,1024]{1,0:T(8,128)S(1)}, f32[256,256]{1,0:T(8,128)S(1)}, f32[256,256...) custom-call(bf16[256,1024]{1,0:T(8,128)(2,1)S(1)} %get-tuple-element, ...), custom_call_target="tpu_custom_call" | custom-call | flops 6300000256 | bytes 21000000 | tf_op jit(solution)/shard_map/pallas_call | solution.py:31
  95.1 1.1 shard_map.312
  96.2 1.5 collective-permute-start.14
  98.4 1.5 collective-permute-done.14.a_2_.a_9_
  100.0 2.0 %shard_map.313 = (bf16[512,1024]{1,0:T(8,128)(2,1)S(1)}, bf16[512,1024]{1,0:T(8,128)(2,1)}, bf16[256,1024]{1,0:T(8,128)(2,1)S(1)}) custom-call(f32[256,1024]{1,0:T(8,128)S(1)} %get-tuple-element.99.a_0_.a_1_, f32[16,256]{1,0:T(8,128)S(1)} %get-tuple-element.100.a_1_.a_8_, f32[16,256]{1,0:T(8,128)S(1)} %collective-permute-done.14.a_2_.a_9_, ...), custom_call_target="tpu_custom_call" | custom-call | flops 3600000000 | bytes 12000000 | tf_op jit(solution)/shard_map/pallas_call | solution.py:31
  102.0 1.0 copy-done.2
  102.9 2.7 %shard_map.316 = (bf16[256,1024]{1,0:T(8,128)(2,1)S(1)}, f32[256,1024]{1,0:T(8,128)S(1)}, f32[1,1024]{1,0:T(1,128)S(1)}, bf16[512,1024]{1,0:T(8,128)(2,1)S(1)}, bf16[512,1024]{1,0:T(8,128)(2,1)}) custom-call(bf16[1024,256]{1,0:T(8,128)(2,1)S(1)} %get-tuple-element.108.a_0_.turned, f32[256,1024]{1,0:T(8,128)S(1)} %get-tuple-element.99.a_0_.a_1_, ...), custom_call_target="tpu_custom_call" | custom-call | flops 5400000000 | bytes 18000000 | tf_op jit(solution)/shard_map/pallas_call | solution.py:31
  105.6 1.0 copy-done.4
  106.6 8.3 %shard_map.317 = (bf16[256,1408]{1,0:T(8,128)(2,1)S(1)}, bf16[256,256]{1,0:T(8,128)(2,1)S(1)}, f32[16,1024]{1,0:T(8,128)S(1)}, bf16[512,1024]{1,0:T(8,128)(2,1)S(1)}, bf16[512,1024]{1,0:T(8,128)(2,1)}) custom-call(bf16[1024,256]{1,0:T(8,128)(2,1)S(1)} %get-tuple-element.108.a_0_.turned, f32[256,1024]{1,0:T(8,128)S(1)} %get-tuple-element.111.a_1_, ...), custom_call_target="tpu_custom_call" | custom-call | flops 7200000000 | bytes 24000000 | tf_op jit(solution)/shard_map/pallas_call | solution.py:31
  114.9 1.5 collective-permute-start.30
  116.5 3.0 %shard_map.318 = (f32[128,1024]{1,0:T(8,128)S(1)}, bf16[128,1024]{1,0:T(8,128)(2,1)S(1)}) custom-call(s32[1]{0:T(128)} %bitcast.7.side, bf16[256,1024]{1,0:T(8,128)(2,1)S(1)} %get-tuple-element.110.dz, bf16[512,1024]{1,0:T(8,128)(2,1)S(1)} %shard_map.302.wza, bf16[512,1024]{1,0:T(8,128)(2,1)S(1)} %collective-permute-done.7.wzb, ...), custom_call_target="tpu_custom_call" | custom-call | flops 4499999744 | bytes 15000000 | tf_op jit(solution)/shard_map/pallas_call | solution.py:31
  120.7 5.3 %collective-permute-done.16.other = bf16[128,1024]{1,0:T(8,128)(2,1)S(1)} collective-permute-done((bf16[128,1024]{1,0:T(8,128)(2,1)S(1)}, bf16[128,1024]{1,0:T(8,128)(2,1)S(1)}, u32[]{:S(2)}, u32[]{:S(2)}) %collective-permute-start.16) | collective-permute-done | bytes 262176 | tf_op jit(solution)/shard_map/ppermute | solution.py:509
  126.0 1.7 shard_map.319
  127.9 1.6 collective-permute-start.32
  129.5 1.2 collective-permute-start.18
  130.7 3.9 %collective-permute-done.18 = f32[16,1024]{1,0:T(8,128)S(1)} collective-permute-done((f32[16,1024]{1,0:T(8,128)S(1)}, f32[16,1024]{1,0:T(8,128)S(1)}, u32[]{:S(2)}, u32[]{:S(2)}) %collective-permute-start.18) | collective-permute-done | bytes 65568 | tf_op jit(solution)/shard_map/ppermute | solution.py:506
  134.6 1.4 collective-permute-start.19
  136.7 3.0 %shard_map.314 = (f32[128,1024]{1,0:T(8,128)S(1)}, bf16[128,1024]{1,0:T(8,128)(2,1)S(1)}) custom-call(s32[1]{0:T(128)} %bitcast.7.side, bf16[256,1024]{1,0:T(8,128)(2,1)S(1)} %get-tuple-element.102.mixed, bf16[512,1024]{1,0:T(8,128)(2,1)} %shard_map.310.outa, bf16[512,1024]{1,0:T(8,128)(2,1)} %collective-permute-done.13.outb), custom_call_target="tpu_custom_call" | custom-call | flops 2249999872 | bytes 7500000 | tf_op jit(solution)/shard_map/pallas_call | solution.py:31
  139.8 1.2 collective-permute-start.15
  141.5 3.0 %collective-permute-start.20 = (f32[16,1024]{1,0:T(8,128)S(1)}, f32[16,1024]{1,0:T(8,128)S(1)}, u32[]{:S(2)}, u32[]{:S(2)}) collective-permute-start(f32[16,1024]{1,0:T(8,128)S(1)} %add.196), channel_id=1, source_target_pairs={{0,16},{2,18},{4,20},{6,22},{8,24},{10,26},{12,28},{14,30},{16,0},... | collective-permute-start | bytes 196616 | tf_op jit(solution)/shard_map/ppermute | solution.py:506
  144.5 2.6 %collective-permute-done.15.other = bf16[128,1024]{1,0:T(8,128)(2,1)S(1)} collective-permute-done((bf16[128,1024]{1,0:T(8,128)(2,1)S(1)}, bf16[128,1024]{1,0:T(8,128)(2,1)S(1)}, u32[]{:S(2)}, u32[]{:S(2)}) %collective-permute-start.15) | collective-permute-done | bytes 262176 | tf_op jit(solution)/shard_map/ppermute | solution.py:509
  147.1 2.9 %collective-permute-start.34 = (bf16[32,384]{1,0:T(8,128)(2,1)S(1)}, bf16[32,384]{1,0:T(8,128)(2,1)S(1)}, u32[]{:S(2)}, u32[]{:S(2)}) collective-permute-start(bf16[32,384]{1,0:T(8,128)(2,1)S(1)} %get-tuple-element.174), channel_id=1, source_target_pairs={{0,16},{2,18},{4,20},{6,22},{8,24},{10,26},{12,28},{14,30},{16,0},... | collective-permute-start | bytes 73736 | tf_op jit(solution)/shard_map/ppermute | solution.py:506
  150.1 1.5 shard_map.315
  151.6 1.1 collective-permute-start.21
  154.1 1.5 collective-permute-done.21.other
  157.1 1.6 collective-permute-start.27
  158.7 1.2 add_convert_fusion.4
  160.0 1.7 collective-permute-start.23
  161.7 1.6 add_convert_fusion.1
  163.9 1.2 fusion.3
  165.2 6.8 %collective-permute-done.27 = bf16[256,1024]{1,0:T(8,128)(2,1)S(1)} collective-permute-done((bf16[256,1024]{1,0:T(8,128)(2,1)S(1)}, bf16[256,1024]{1,0:T(8,128)(2,1)S(1)}, u32[]{:S(2)}, u32[]{:S(2)}) %collective-permute-start.27) | collective-permute-done | bytes 524320 | tf_op jit(solution)/shard_map/ppermute | solution.py:506
  172.2 1.8 collective-permute-start.28
  174.0 2.0 %collective-permute-done.23 = bf16[256,1024]{1,0:T(8,128)(2,1)S(1)} collective-permute-done((bf16[256,1024]{1,0:T(8,128)(2,1)S(1)}, bf16[256,1024]{1,0:T(8,128)(2,1)S(1)}, u32[]{:S(2)}, u32[]{:S(2)}) %collective-permute-start.23) | collective-permute-done | bytes 524320 | tf_op jit(solution)/shard_map/ppermute | solution.py:506
  176.3 2.7 %collective-permute-done.36 = bf16[256,1024]{1,0:T(8,128)(2,1)S(1)} collective-permute-done((bf16[256,1024]{1,0:T(8,128)(2,1)S(1)}, bf16[256,1024]{1,0:T(8,128)(2,1)S(1)}, u32[]{:S(2)}, u32[]{:S(2)}) %collective-permute-start.36) | collective-permute-done | bytes 524320 | tf_op jit(solution)/shard_map/ppermute | solution.py:506
  179.3 1.9 collective-permute-start.37
  181.2 0.8 collective-permute-start.29
  182.0 7.1 %collective-permute-done.24 = bf16[128,1024]{1,0:T(8,128)(2,1)S(1)} collective-permute-done((bf16[128,1024]{1,0:T(8,128)(2,1)S(1)}, bf16[128,1024]{1,0:T(8,128)(2,1)S(1)}, u32[]{:S(2)}, u32[]{:S(2)}) %collective-permute-start.24) | collective-permute-done | bytes 262176 | tf_op jit(solution)/shard_map/ppermute | solution.py:506
  190.2 4.0 %collective-permute-done.29 = bf16[64,1024]{1,0:T(8,128)(2,1)S(1)} collective-permute-done((bf16[64,1024]{1,0:T(8,128)(2,1)S(1)}, bf16[64,1024]{1,0:T(8,128)(2,1)S(1)}, u32[]{:S(2)}, u32[]{:S(2)}) %collective-permute-start.29) | collective-permute-done | bytes 131104 | tf_op jit(solution)/shard_map/ppermute | solution.py:506
  195.7 1.3 collective-permute-done.38
  (119 shorter events, 17.8 us)
Async XLA Ops:
  0.6 33.2 %copy-start.12 = (bf16[1024,64]{0,1:T(8,128)(2,1)S(1)}, bf16[1024,64]{0,1:T(8,128)(2,1)}, u32[]{:S(2)}) copy-start(bf16[1024,64]{0,1:T(8,128)(2,1)} %param.34) | copy-start | bytes 393220
  2.4 12.5 %collective-permute-start.1 = (bf16[64,1408]{1,0:T(8,128)(2,1)S(1)}, bf16[64,1408]{1,0:T(8,128)(2,1)S(1)}, u32[]{:S(2)}, u32[]{:S(2)}) collective-permute-start(bf16[64,1408]{1,0:T(8,128)(2,1)S(1)} %fusion.11.first), channel_id=1, source_target_pairs={{0,16},{2,18},{4,20},{6,22},{8,24},{10,26},{12,28},{14,30},{16,0},... | collective-permute-start | bytes 540680 | tf_op jit(solution)/shard_map/ppermute | solution.py:506
  15.0 9.6 %collective-permute-start.2 = (bf16[128,1408]{1,0:T(8,128)(2,1)S(1)}, bf16[128,1408]{1,0:T(8,128)(2,1)S(1)}, u32[]{:S(2)}, u32[]{:S(2)}) collective-permute-start(bf16[128,1408]{1,0:T(8,128)(2,1)S(1)} %shard_map.299.first), channel_id=1, source_target_pairs={{0,8},{2,10},{4,12},{6,14},{8,0},{10,2},{12,4},{14,6},{16,24},{18,... | collective-permute-start | bytes 1081352 | tf_op jit(solution)/shard_map/ppermute | solution.py:506
  24.6 18.3 %copy-start.13 = (bf16[64,1024]{1,0:T(8,128)(2,1)S(1)}, bf16[64,1024]{1,0:T(8,128)(2,1)}, u32[]{:S(2)}) copy-start(bf16[64,1024]{1,0:T(8,128)(2,1)} %first) | copy-start | bytes 393220
  24.6 9.2 %collective-permute-start.3 = (bf16[64,1024]{1,0:T(8,128)(2,1)}, bf16[64,1024]{1,0:T(8,128)(2,1)S(1)}, u32[]{:S(2)}, u32[]{:S(2)}) collective-permute-start(bf16[64,1024]{1,0:T(8,128)(2,1)} %bitcast.53), channel_id=1, source_target_pairs={{0,16},{2,18},{4,20},{6,22},{8,24},{10,26},{12,28},{14,30},{16,0},... | collective-permute-start | bytes 393224 | tf_op jit(solution)/shard_map/ppermute | solution.py:506
  27.8 24.8 %collective-permute-start.8 = (bf16[256,1408]{1,0:T(8,128)(2,1)S(1)}, bf16[256,1408]{1,0:T(8,128)(2,1)S(1)}, u32[]{:S(2)}, u32[]{:S(2)}) collective-permute-start(bf16[256,1408]{1,0:T(8,128)(2,1)S(1)} %shard_map.303.first), channel_id=1, source_target_pairs={{0,4},{2,6},{4,0},{6,2},{8,12},{10,14},{12,8},{14,10},{16,20},{18,... | collective-permute-start | bytes 2162696 | tf_op jit(solution)/shard_map/ppermute | solution.py:506
  33.9 7.4 %collective-permute-start.11 = (bf16[128,1024]{1,0:T(8,128)(2,1)S(1)}, bf16[128,1024]{1,0:T(8,128)(2,1)S(1)}, u32[]{:S(2)}, u32[]{:S(2)}) collective-permute-start(bf16[128,1024]{1,0:T(8,128)(2,1)S(1)} %shard_map.308.first), channel_id=1, source_target_pairs={{0,8},{2,10},{4,12},{6,14},{8,0},{10,2},{12,4},{14,6},{16,24},{18,... | collective-permute-start | bytes 786440 | tf_op jit(solution)/shard_map/ppermute | solution.py:506
  41.3 19.2 %collective-permute-start.12 = (bf16[256,1024]{1,0:T(8,128)(2,1)S(1)}, bf16[256,1024]{1,0:T(8,128)(2,1)}, u32[]{:S(2)}, u32[]{:S(2)}) collective-permute-start(bf16[256,1024]{1,0:T(8,128)(2,1)S(1)} %shard_map.309.first), channel_id=1, source_target_pairs={{0,4},{2,6},{4,0},{6,2},{8,12},{10,14},{12,8},{14,10},{16,20},{18,... | collective-permute-start | bytes 1572872 | tf_op jit(solution)/shard_map/ppermute | solution.py:506
  42.9 8.8 %collective-permute-start.4 = (bf16[64,1024]{1,0:T(8,128)(2,1)S(1)}, bf16[64,1024]{1,0:T(8,128)(2,1)S(1)}, u32[]{:S(2)}, u32[]{:S(2)}) collective-permute-start(bf16[64,1024]{1,0:T(8,128)(2,1)S(1)} %copy-done.13), channel_id=1, source_target_pairs={{0,16},{2,18},{4,20},{6,22},{8,24},{10,26},{12,28},{14,30},{16,0},... | collective-permute-start | bytes 393224 | tf_op jit(solution)/shard_map/ppermute | solution.py:506
  51.8 7.4 %collective-permute-start.5 = (bf16[128,1024]{1,0:T(8,128)(2,1)S(1)}, bf16[128,1024]{1,0:T(8,128)(2,1)S(1)}, u32[]{:S(2)}, u32[]{:S(2)}) collective-permute-start(bf16[128,1024]{1,0:T(8,128)(2,1)S(1)} %shard_map.300.first), channel_id=1, source_target_pairs={{0,8},{2,10},{4,12},{6,14},{8,0},{10,2},{12,4},{14,6},{16,24},{18,... | collective-permute-start | bytes 786440 | tf_op jit(solution)/shard_map/ppermute | solution.py:506
  52.7 36.8 %collective-permute-start.9 = (bf16[512,1408]{1,0:T(8,128)(2,1)S(1)}, bf16[512,1408]{1,0:T(8,128)(2,1)}, u32[]{:S(2)}, u32[]{:S(2)}) collective-permute-start(bf16[512,1408]{1,0:T(8,128)(2,1)S(1)} %shard_map.304.a_1_.w1a), channel_id=1, source_target_pairs={{0,2},{2,0},{4,6},{6,4},{8,10},{10,8},{12,14},{14,12},{16,18},{18,... | collective-permute-start | bytes 4325384 | tf_op jit(solution)/shard_map/ppermute | solution.py:506
  60.0 15.3 %collective-permute-start.6 = (bf16[256,1024]{1,0:T(8,128)(2,1)}, bf16[256,1024]{1,0:T(8,128)(2,1)}, u32[]{:S(2)}, u32[]{:S(2)}) collective-permute-start(bf16[256,1024]{1,0:T(8,128)(2,1)} %shard_map.301.first), channel_id=1, source_target_pairs={{0,4},{2,6},{4,0},{6,2},{8,12},{10,14},{12,8},{14,10},{16,20},{18,... | collective-permute-start | bytes 1572872 | tf_op jit(solution)/shard_map/ppermute | solution.py:506
  62.6 2.7 %copy-start.20 = (s32[256]{0:T(256)S(1)}, s32[256]{0:T(256)}, u32[]{:S(2)}) copy-start(s32[256]{0:T(256)} %param.19) | copy-start | bytes 3076
  62.6 5.5 %copy-start.18 = (f32[1024]{0:T(1024)S(1)}, f32[1024]{0:T(1024)}, u32[]{:S(2)}) copy-start(f32[1024]{0:T(1024)} %param.21) | copy-start | bytes 12292
  62.6 24.6 %collective-permute-start.13 = (bf16[512,1024]{1,0:T(8,128)(2,1)}, bf16[512,1024]{1,0:T(8,128)(2,1)}, u32[]{:S(2)}, u32[]{:S(2)}) collective-permute-start(bf16[512,1024]{1,0:T(8,128)(2,1)} %shard_map.310.outa), channel_id=1, source_target_pairs={{0,2},{2,0},{4,6},{6,4},{8,10},{10,8},{12,14},{14,12},{16,18},{18,... | collective-permute-start | bytes 3145736 | tf_op jit(solution)/shard_map/ppermute | solution.py:506
  68.1 1.6 copy-start.1
  69.7 1.0 copy-start.8
  70.7 1.0 copy-start.10
  72.6 9.2 %collective-permute-start.10 = (bf16[128,1024]{1,0:T(8,128)(2,1)S(1)}, bf16[128,1024]{1,0:T(8,128)(2,1)S(1)}, u32[]{:S(2)}, u32[]{:S(2)}) collective-permute-start(bf16[128,1024]{1,0:T(8,128)(2,1)S(1)} %get-tuple-element.96.own), channel_id=1, source_target_pairs={{0,1},{1,0},{2,3},{3,2},{4,5},{5,4},{6,7},{7,6},{8,9},{9,8},{10,11... | collective-permute-start | bytes 786440 | tf_op jit(solution)/shard_map/ppermute | solution.py:509
  74.1 12.8 %collective-permute-start = (bf16[128,1024]{1,0:T(8,128)(2,1)S(1)}, bf16[128,1024]{1,0:T(8,128)(2,1)S(1)}, u32[]{:S(2)}, u32[]{:S(2)}) collective-permute-start(bf16[128,1024]{1,0:T(8,128)(2,1)S(1)} %get-tuple-element.84.own), channel_id=1, source_target_pairs={{0,1},{1,0},{2,3},{3,2},{4,5},{5,4},{6,7},{7,6},{8,9},{9,8},{10,11... | collective-permute-start | bytes 786440 | tf_op jit(solution)/shard_map/ppermute | solution.py:509
  76.6 18.5 %collective-permute-start.7 = (bf16[512,1024]{1,0:T(8,128)(2,1)S(1)}, bf16[512,1024]{1,0:T(8,128)(2,1)S(1)}, u32[]{:S(2)}, u32[]{:S(2)}) collective-permute-start(bf16[512,1024]{1,0:T(8,128)(2,1)S(1)} %shard_map.302.wza), channel_id=1, source_target_pairs={{0,2},{2,0},{4,6},{6,4},{8,10},{10,8},{12,14},{14,12},{16,18},{18,... | collective-permute-start | bytes 3145736 | tf_op jit(solution)/shard_map/ppermute | solution.py:506
  87.2 2.3 %copy-start.14 = (f32[4,1024]{1,0:T(4,128)S(1)}, f32[4,1024]{1,0:T(4,128)}, u32[]{:S(2)}) copy-start(f32[4,1024]{1,0:T(4,128)} %a_13_.1) | copy-start | bytes 49156
  87.2 2.3 %copy-start.15 = (f32[1024]{0:T(1024)S(1)}, f32[1024]{0:T(1024)}, u32[]{:S(2)}) copy-start(f32[1024]{0:T(1024)} %param.27) | copy-start | bytes 12292
  87.2 2.3 %copy-start.17 = (f32[4,256]{1,0:T(4,128)S(1)}, f32[4,256]{1,0:T(4,128)}, u32[]{:S(2)}) copy-start(f32[4,256]{1,0:T(4,128)} %a_14_.1) | copy-start | bytes 12292
  87.2 2.3 %copy-start.19 = (f32[256]{0:T(256)S(1)}, f32[256]{0:T(256)}, u32[]{:S(2)}) copy-start(f32[256]{0:T(256)} %param.29) | copy-start | bytes 3076
  89.6 5.5 %copy-start.16 = (f32[1024]{0:T(1024)S(1)}, f32[1024]{0:T(1024)}, u32[]{:S(2)}) copy-start(f32[1024]{0:T(1024)} %param.33) | copy-start | bytes 12292
  95.1 2.6 %copy-start = (bf16[1024,1024]{1,0:T(8,128)(2,1)S(1)}, bf16[1024,1024]{1,0:T(8,128)(2,1)}, u32[]{:S(2)}) copy-start(bf16[1024,1024]{1,0:T(8,128)(2,1)} %get-tuple-element.131.picks) | copy-start | bytes 6291460
  96.2 3.8 %collective-permute-start.14 = (f32[16,256]{1,0:T(8,128)S(1)}, f32[16,256]{1,0:T(8,128)S(1)}, u32[]{:S(2)}, u32[]{:S(2)}) collective-permute-start(f32[16,256]{1,0:T(8,128)S(1)} %get-tuple-element.100.a_1_.a_8_), channel_id=1, source_target_pairs={{0,1},{1,0},{2,3},{3,2},{4,5},{5,4},{6,7},{7,6},{8,9},{9,8},{10,11... | collective-permute-start | bytes 49160 | tf_op jit(solution)/shard_map/ppermute | solution.py:509
  102.0 1.0 copy-start.2
  105.6 1.0 copy-start.4
  114.9 4.6 %copy-start.6 = (bf16[512,1024]{1,0:T(8,128)(2,1)}, bf16[512,1024]{1,0:T(8,128)(2,1)S(1)}, u32[]{:S(2)}) copy-start(bf16[512,1024]{1,0:T(8,128)(2,1)S(1)} %get-tuple-element.129) | copy-start | bytes 3145732
  114.9 5.2 %collective-permute-start.30 = (bf16[256,256]{1,0:T(8,128)(2,1)S(1)}, bf16[256,256]{1,0:T(8,128)(2,1)S(1)}, u32[]{:S(2)}, u32[]{:S(2)}) collective-permute-start(bf16[256,256]{1,0:T(8,128)(2,1)S(1)} %get-tuple-element.132), channel_id=1, source_target_pairs={{0,1},{1,0},{2,3},{3,2},{4,5},{5,4},{6,7},{7,6},{8,9},{9,8},{10,11... | collective-permute-start | bytes 393224 | tf_op jit(solution)/shard_map/ppermute | solution.py:509
  119.5 6.5 %copy-start.9 = (f32[128,1024]{1,0:T(8,128)S(1)}, f32[128,1024]{1,0:T(8,128)}, u32[]{:S(2)}) copy-start(f32[128,1024]{1,0:T(8,128)} %cot.3) | copy-start | bytes 1572868
  119.5 6.5 %copy-start.11 = (f32[128,1024]{1,0:T(8,128)S(1)}, f32[128,1024]{1,0:T(8,128)}, u32[]{:S(2)}) copy-start(f32[128,1024]{1,0:T(8,128)} %res.2) | copy-start | bytes 1572868
  119.5 6.5 %collective-permute-start.16 = (bf16[128,1024]{1,0:T(8,128)(2,1)S(1)}, bf16[128,1024]{1,0:T(8,128)(2,1)S(1)}, u32[]{:S(2)}, u32[]{:S(2)}) collective-permute-start(bf16[128,1024]{1,0:T(8,128)(2,1)S(1)} %get-tuple-element.121), channel_id=1, source_target_pairs={{0,1},{1,0},{2,3},{3,2},{4,5},{5,4},{6,7},{7,6},{8,9},{9,8},{10,11... | collective-permute-start | bytes 786440 | tf_op jit(solution)/shard_map/ppermute | solution.py:509
  120.6 7.2 %collective-permute-start.31 = (bf16[256,384]{1,0:T(8,128)(2,1)S(1)}, bf16[256,384]{1,0:T(8,128)(2,1)S(1)}, u32[]{:S(2)}, u32[]{:S(2)}) collective-permute-start(bf16[256,384]{1,0:T(8,128)(2,1)S(1)} %get-tuple-element.134), channel_id=1, source_target_pairs={{0,2},{2,0},{4,6},{6,4},{8,10},{10,8},{12,14},{14,12},{16,18},{18,... | collective-permute-start | bytes 589832 | tf_op jit(solution)/shard_map/ppermute | solution.py:506
  127.7 1.8 collective-permute-start.17
  127.9 8.0 %collective-permute-start.32 = (bf16[128,384]{1,0:T(8,128)(2,1)S(1)}, bf16[128,384]{1,0:T(8,128)(2,1)S(1)}, u32[]{:S(2)}, u32[]{:S(2)}) collective-permute-start(bf16[128,384]{1,0:T(8,128)(2,1)S(1)} %get-tuple-element.171), channel_id=1, source_target_pairs={{0,4},{2,6},{4,0},{6,2},{8,12},{10,14},{12,8},{14,10},{16,20},{18,... | collective-permute-start | bytes 294920 | tf_op jit(solution)/shard_map/ppermute | solution.py:506
  129.5 5.0 %collective-permute-start.18 = (f32[16,1024]{1,0:T(8,128)S(1)}, f32[16,1024]{1,0:T(8,128)S(1)}, u32[]{:S(2)}, u32[]{:S(2)}) collective-permute-start(f32[16,1024]{1,0:T(8,128)S(1)} %add.194), channel_id=1, source_target_pairs={{0,4},{2,6},{4,0},{6,2},{8,12},{10,14},{12,8},{14,10},{16,20},{18,... | collective-permute-start | bytes 196616 | tf_op jit(solution)/shard_map/ppermute | solution.py:506
  130.7 26.1 %collective-permute-start.26 = (bf16[512,1024]{1,0:T(8,128)(2,1)}, bf16[512,1024]{1,0:T(8,128)(2,1)S(1)}, u32[]{:S(2)}, u32[]{:S(2)}) collective-permute-start(bf16[512,1024]{1,0:T(8,128)(2,1)} %get-tuple-element.130), channel_id=1, source_target_pairs={{0,2},{2,0},{4,6},{6,4},{8,10},{10,8},{12,14},{14,12},{16,18},{18,... | collective-permute-start | bytes 3145736 | tf_op jit(solution)/shard_map/ppermute | solution.py:506
  134.6 6.4 %collective-permute-start.19 = (f32[16,1024]{1,0:T(8,128)S(1)}, f32[16,1024]{1,0:T(8,128)S(1)}, u32[]{:S(2)}, u32[]{:S(2)}) collective-permute-start(f32[16,1024]{1,0:T(8,128)S(1)} %add.195), channel_id=1, source_target_pairs={{0,8},{2,10},{4,12},{6,14},{8,0},{10,2},{12,4},{14,6},{16,24},{18,... | collective-permute-start | bytes 196616 | tf_op jit(solution)/shard_map/ppermute | solution.py:506
  136.0 5.5 %collective-permute-start.33 = (bf16[64,384]{1,0:T(8,128)(2,1)S(1)}, bf16[64,384]{1,0:T(8,128)(2,1)S(1)}, u32[]{:S(2)}, u32[]{:S(2)}) collective-permute-start(bf16[64,384]{1,0:T(8,128)(2,1)S(1)} %get-tuple-element.173), channel_id=1, source_target_pairs={{0,8},{2,10},{4,12},{6,14},{8,0},{10,2},{12,4},{14,6},{16,24},{18,... | collective-permute-start | bytes 147464 | tf_op jit(solution)/shard_map/ppermute | solution.py:506
  139.8 7.3 %collective-permute-start.15 = (bf16[128,1024]{1,0:T(8,128)(2,1)S(1)}, bf16[128,1024]{1,0:T(8,128)(2,1)S(1)}, u32[]{:S(2)}, u32[]{:S(2)}) collective-permute-start(bf16[128,1024]{1,0:T(8,128)(2,1)S(1)} %get-tuple-element.104), channel_id=1, source_target_pairs={{0,1},{1,0},{2,3},{3,2},{4,5},{5,4},{6,7},{7,6},{8,9},{9,8},{10,11... | collective-permute-start | bytes 786440 | tf_op jit(solution)/shard_map/ppermute | solution.py:509
  141.0 17.8 %collective-permute-start.22 = (bf16[512,1024]{1,0:T(8,128)(2,1)}, bf16[512,1024]{1,0:T(8,128)(2,1)}, u32[]{:S(2)}, u32[]{:S(2)}) collective-permute-start(bf16[512,1024]{1,0:T(8,128)(2,1)} %get-tuple-element.128), channel_id=1, source_target_pairs={{0,2},{2,0},{4,6},{6,4},{8,10},{10,8},{12,14},{14,12},{16,18},{18,... | collective-permute-start | bytes 3145736 | tf_op jit(solution)/shard_map/ppermute | solution.py:506
  141.0 20.8 %collective-permute-start.35 = (bf16[512,1024]{1,0:T(8,128)(2,1)}, bf16[512,1024]{1,0:T(8,128)(2,1)}, u32[]{:S(2)}, u32[]{:S(2)}) collective-permute-start(bf16[512,1024]{1,0:T(8,128)(2,1)} %get-tuple-element.107), channel_id=1, source_target_pairs={{0,2},{2,0},{4,6},{6,4},{8,10},{10,8},{12,14},{14,12},{16,18},{18,... | collective-permute-start | bytes 3145736 | tf_op jit(solution)/shard_map/ppermute | solution.py:506
  141.5 10.1 %collective-permute-start.20 = (f32[16,1024]{1,0:T(8,128)S(1)}, f32[16,1024]{1,0:T(8,128)S(1)}, u32[]{:S(2)}, u32[]{:S(2)}) collective-permute-start(f32[16,1024]{1,0:T(8,128)S(1)} %add.196), channel_id=1, source_target_pairs={{0,16},{2,18},{4,20},{6,22},{8,24},{10,26},{12,28},{14,30},{16,0},... | collective-permute-start | bytes 196616 | tf_op jit(solution)/shard_map/ppermute | solution.py:506
  147.1 5.6 %collective-permute-start.34 = (bf16[32,384]{1,0:T(8,128)(2,1)S(1)}, bf16[32,384]{1,0:T(8,128)(2,1)S(1)}, u32[]{:S(2)}, u32[]{:S(2)}) collective-permute-start(bf16[32,384]{1,0:T(8,128)(2,1)S(1)} %get-tuple-element.174), channel_id=1, source_target_pairs={{0,16},{2,18},{4,20},{6,22},{8,24},{10,26},{12,28},{14,30},{16,0},... | collective-permute-start | bytes 73736 | tf_op jit(solution)/shard_map/ppermute | solution.py:506
  151.6 5.2 %copy-start.7 = (bf16[512,1024]{1,0:T(8,128)(2,1)S(1)}, bf16[512,1024]{1,0:T(8,128)(2,1)}, u32[]{:S(2)}) copy-start(bf16[512,1024]{1,0:T(8,128)(2,1)} %copy-done.6) | copy-start | bytes 3145732
  151.6 4.0 %collective-permute-start.21 = (f32[8,1024]{1,0:T(8,128)S(1)}, f32[8,1024]{1,0:T(8,128)S(1)}, u32[]{:S(2)}, u32[]{:S(2)}) collective-permute-start(f32[8,1024]{1,0:T(8,128)S(1)} %slice.270), channel_id=1, source_target_pairs={{0,1},{1,0},{2,3},{3,2},{4,5},{5,4},{6,7},{7,6},{8,9},{9,8},{10,11... | collective-permute-start | bytes 98312 | tf_op jit(solution)/shard_map/ppermute | solution.py:509
  154.1 4.7 %copy-start.5 = (bf16[512,1024]{1,0:T(8,128)(2,1)S(1)}, bf16[512,1024]{1,0:T(8,128)(2,1)}, u32[]{:S(2)}) copy-start(bf16[512,1024]{1,0:T(8,128)(2,1)} %copy-done.4) | copy-start | bytes 3145732
  156.8 5.0 %copy-start.3 = (bf16[512,1024]{1,0:T(8,128)(2,1)S(1)}, bf16[512,1024]{1,0:T(8,128)(2,1)}, u32[]{:S(2)}) copy-start(bf16[512,1024]{1,0:T(8,128)(2,1)} %copy-done.2) | copy-start | bytes 3145732
  157.1 14.9 %collective-permute-start.27 = (bf16[256,1024]{1,0:T(8,128)(2,1)S(1)}, bf16[256,1024]{1,0:T(8,128)(2,1)S(1)}, u32[]{:S(2)}, u32[]{:S(2)}) collective-permute-start(bf16[256,1024]{1,0:T(8,128)(2,1)S(1)} %get-tuple-element.163), channel_id=1, source_target_pairs={{0,4},{2,6},{4,0},{6,2},{8,12},{10,14},{12,8},{14,10},{16,20},{18,... | collective-permute-start | bytes 1572872 | tf_op jit(solution)/shard_map/ppermute | solution.py:506
  160.0 16.0 %collective-permute-start.23 = (bf16[256,1024]{1,0:T(8,128)(2,1)S(1)}, bf16[256,1024]{1,0:T(8,128)(2,1)S(1)}, u32[]{:S(2)}, u32[]{:S(2)}) collective-permute-start(bf16[256,1024]{1,0:T(8,128)(2,1)S(1)} %bitcast.63), channel_id=1, source_target_pairs={{0,8},{2,10},{4,12},{6,14},{8,0},{10,2},{12,4},{14,6},{16,24},{18,... | collective-permute-start | bytes 1572872 | tf_op jit(solution)/shard_map/ppermute | solution.py:506
  163.3 15.7 %collective-permute-start.36 = (bf16[256,1024]{1,0:T(8,128)(2,1)S(1)}, bf16[256,1024]{1,0:T(8,128)(2,1)S(1)}, u32[]{:S(2)}, u32[]{:S(2)}) collective-permute-start(bf16[256,1024]{1,0:T(8,128)(2,1)S(1)} %get-tuple-element.161), channel_id=1, source_target_pairs={{0,4},{2,6},{4,0},{6,2},{8,12},{10,14},{12,8},{14,10},{16,20},{18,... | collective-permute-start | bytes 1572872 | tf_op jit(solution)/shard_map/ppermute | solution.py:506
  172.2 8.9 %collective-permute-start.28 = (bf16[128,1024]{1,0:T(8,128)(2,1)S(1)}, bf16[128,1024]{1,0:T(8,128)(2,1)S(1)}, u32[]{:S(2)}, u32[]{:S(2)}) collective-permute-start(bf16[128,1024]{1,0:T(8,128)(2,1)S(1)} %get-tuple-element.167), channel_id=1, source_target_pairs={{0,8},{2,10},{4,12},{6,14},{8,0},{10,2},{12,4},{14,6},{16,24},{18,... | collective-permute-start | bytes 786440 | tf_op jit(solution)/shard_map/ppermute | solution.py:506
  176.2 12.9 %collective-permute-start.24 = (bf16[128,1024]{1,0:T(8,128)(2,1)S(1)}, bf16[128,1024]{1,0:T(8,128)(2,1)S(1)}, u32[]{:S(2)}, u32[]{:S(2)}) collective-permute-start(bf16[128,1024]{1,0:T(8,128)(2,1)S(1)} %bitcast.64), channel_id=1, source_target_pairs={{0,16},{2,18},{4,20},{6,22},{8,24},{10,26},{12,28},{14,30},{16,0},... | collective-permute-start | bytes 786440 | tf_op jit(solution)/shard_map/ppermute | solution.py:506
  179.3 10.3 %collective-permute-start.37 = (bf16[128,1024]{1,0:T(8,128)(2,1)S(1)}, bf16[128,1024]{1,0:T(8,128)(2,1)S(1)}, u32[]{:S(2)}, u32[]{:S(2)}) collective-permute-start(bf16[128,1024]{1,0:T(8,128)(2,1)S(1)} %get-tuple-element.165), channel_id=1, source_target_pairs={{0,8},{2,10},{4,12},{6,14},{8,0},{10,2},{12,4},{14,6},{16,24},{18,... | collective-permute-start | bytes 786440 | tf_op jit(solution)/shard_map/ppermute | solution.py:506
  181.2 13.1 %collective-permute-start.29 = (bf16[64,1024]{1,0:T(8,128)(2,1)S(1)}, bf16[64,1024]{1,0:T(8,128)(2,1)S(1)}, u32[]{:S(2)}, u32[]{:S(2)}) collective-permute-start(bf16[64,1024]{1,0:T(8,128)(2,1)S(1)} %fusion.9), channel_id=1, source_target_pairs={{0,16},{2,18},{4,20},{6,22},{8,24},{10,26},{12,28},{14,30},{16,0},... | collective-permute-start | bytes 393224 | tf_op jit(solution)/shard_map/ppermute | solution.py:506
  189.1 5.9 %collective-permute-start.25 = (bf16[64,1024]{1,0:T(8,128)(2,1)S(1)}, bf16[64,1024]{1,0:T(8,128)(2,1)S(1)}, u32[]{:S(2)}, u32[]{:S(2)}) collective-permute-start(bf16[64,1024]{1,0:T(8,128)(2,1)S(1)} %fusion.5), channel_id=1, source_target_pairs={{0,4},{2,6},{4,0},{6,2},{8,12},{10,14},{12,8},{14,10},{16,20},{18,... | collective-permute-start | bytes 393224 | tf_op jit(solution)/shard_map/ppermute | solution.py:506
  189.6 7.4 %collective-permute-start.38 = (bf16[64,1024]{1,0:T(8,128)(2,1)S(1)}, bf16[64,1024]{1,0:T(8,128)(2,1)S(1)}, u32[]{:S(2)}, u32[]{:S(2)}) collective-permute-start(bf16[64,1024]{1,0:T(8,128)(2,1)S(1)} %fusion.7), channel_id=1, source_target_pairs={{0,16},{2,18},{4,20},{6,22},{8,24},{10,26},{12,28},{14,30},{16,0},... | collective-permute-start | bytes 393224 | tf_op jit(solution)/shard_map/ppermute | solution.py:506
